TPU v7x, 256 devices: a whole 4x4x8 slice. The times are simulated.
256 devices in a mesh: rows: 8 (over x, z_hi), specs: 32 (over y, z_lo, core).
Axes of the slice: x: 4, y: 4, z: 8 (z_hi: 2, z_lo: 4; z = z_hi * 4 + z_lo), core: 2. Of those that a mesh axis runs over, the one named last changes fastest.
Arguments:
- center: float32 [64, 512, 64], P('rows'), may hold values from -6 to 6
- radius: float32 [64, 512, 64], P('rows'), may hold values from 0.01 to 0.2
- conv_weight: float32 [3, 3, 64, 64], replicated, may hold values from -0.25 to 0.25
- conv_bias: float32 [64], replicated, may hold values from -3 to 3
- split_status: int32 [64, 512, 64], P('rows'), may hold values from 0 to 2
- out_coeffs: bfloat16 [256, 64, 512, 64], P('specs', 'rows'), may hold values from -6 to 6
- spec_ids: int32 [256], P('specs'), may hold values from 0 to 4095
- spec_offsets: float32 [4096], replicated, may hold values from -5 to 5
Outputs:
- input_coeffs: bfloat16 [256, 64, 512, 64], P('specs', 'rows')
- bounds: float32 [256], P('specs')
All inputs are finite; a program needn't handle non-finite values.
Results may differ from a plain program's by a relative error of at most 0.0052.
Values may be sent and summed in bfloat16 or wider, within the bound.
No kernel may reach another device: no remote copies, remote signals or barrier semaphores. Data moves between devices by JAX's collectives and lax.ppermute only.
A program may use at most 128 MiB of HBM per device.

v0:
```python
import jax
import jax.numpy as jnp
from jax import lax
from jax.sharding import PartitionSpec as P


def padded_2(value, sides, width):
    for axis, dim in sides:
        count, length = (lax.axis_size(axis), value.shape[dim])
        up = [(i, (i + 1) % count) for i in range(count - 1)]
        down = [(j, i) for i, j in up]
        last = lax.slice_in_dim(value, length - width, length, axis=dim)
        initial = lax.slice_in_dim(value, 0, width, axis=dim)
        before = lax.ppermute(last, axis, up)
        after = lax.ppermute(initial, axis, down)
        value = jnp.concatenate([before, value, after], axis=dim)
    return value


def convolve(field, kernel, precision_mode, column_pad):
    return lax.conv_general_dilated(
        field,
        kernel,
        (1, 1),
        ((0, 0), (column_pad, column_pad)),
        dimension_numbers=("NHWC", "HWIO", "NHWC"),
        precision=precision_mode,
        preferred_element_type=jnp.float32,
    )


def relaxation(extended, status, conv_weight, conv_bias):
    center_out = convolve(extended[0:1], conv_weight, lax.Precision.HIGHEST, 0)[0] + conv_bias
    radius_out = convolve(extended[1:2], jnp.abs(conv_weight), lax.Precision.HIGHEST, 0)[0]
    upper_end = center_out + radius_out
    lower_end = center_out - radius_out
    spread = 2.0 * radius_out
    relaxed = jnp.minimum(jnp.maximum(upper_end, 0.0), spread) / spread
    slopes = jnp.where(status == 2, relaxed, jnp.where(status == 1, 1.0, 0.0)).astype(jnp.bfloat16)
    intercepts = jnp.where(status == 2, -relaxed * jnp.minimum(lower_end, 0.0), 0.0).astype(
        jnp.bfloat16
    )
    return (slopes, intercepts)


def per_device(
    center, radius, conv_weight, conv_bias, split_status, out_coeffs, spec_ids, spec_offsets
):
    rows_local, columns, channels = center.shape
    stacked = jnp.pad(jnp.stack([center, radius]), ((0, 0), (0, 0), (1, 1), (0, 0)))
    tile_cols = columns // lax.axis_size("specs")
    first_col = lax.axis_index("specs") * tile_cols
    column_tile = lax.dynamic_slice_in_dim(stacked, first_col, tile_cols + 2, 2)
    extended = padded_2(column_tile, (("rows", 1),), 1)
    status = lax.dynamic_slice_in_dim(split_status, first_col, tile_cols, 1)
    slopes, intercepts = relaxation(extended, status, conv_weight, conv_bias)
    slopes, intercepts = (
        lax.all_gather(slopes, "specs", axis=1, tiled=True),
        lax.all_gather(intercepts, "specs", axis=1, tiled=True),
    )
    coeff_full = out_coeffs.astype(jnp.float32)
    pre_coeffs = (coeff_full * slopes.astype(jnp.float32)).astype(jnp.bfloat16)
    offset_sum = jnp.sum(
        jnp.minimum(coeff_full, 0.0) * intercepts.astype(jnp.float32)
        + pre_coeffs.astype(jnp.float32) * conv_bias,
        axis=(1, 2, 3),
    )
    padded = padded_2(pre_coeffs, (("rows", 1),), 1)
    flipped = jnp.transpose(conv_weight[::-1, ::-1], (0, 1, 3, 2)).astype(jnp.bfloat16)
    input_coeffs = convolve(padded, flipped, None, 1)
    partial_value = (
        jnp.sum(input_coeffs * center - jnp.abs(input_coeffs) * radius, axis=(1, 2, 3)) + offset_sum
    )
    summed = lax.psum(partial_value, "rows")
    pixels = rows_local * lax.axis_size("rows") * columns
    entries = spec_offsets.shape[0]
    onehot = spec_ids[:, None] == jnp.arange(entries, dtype=jnp.int32)[None, :]
    table_terms = jnp.sum(jnp.where(onehot, spec_offsets[None, :], 0.0), axis=1)
    bounds = summed / pixels + table_terms
    return (input_coeffs.astype(jnp.bfloat16), bounds)


def solution(mesh):
    in_specs = (
        P("rows", None, None),
        P("rows", None, None),
        P(),
        P(),
        P("rows", None, None),
        P("specs", "rows", None, None),
        P("specs"),
        P(),
    )
    out_specs = (P("specs", "rows", None, None), P("specs"))
    return jax.shard_map(
        per_device, mesh=mesh, in_specs=in_specs, out_specs=out_specs, check_vma=False
    )
```

profile of v0, /device:TPU:56, one launch (start us, length us, event | category | flops | bytes accessed | tf_op | source)
XLA Modules:
  0.0 268.8 jit_solution(2656032865432795436)
XLA Ops:
  0.6 1.9 copy.71
  2.6 3.2 %copy.72 = f32[8,512,64]{2,1,0:T(8,128)} copy(f32[8,512,64]{1,2,0:T(8,128)} %param.9) | data formatting | bytes 2097152 | tf_op args[1]
  5.7 1.1 fusion.20
  6.8 0.6 copy-done.3
  7.5 0.6 fusion.35
  8.1 8.2 %collective-permute-start = (f32[2,1,18,64]{3,0,2,1:T(2,128)}, f32[2,1,18,64]{3,0,2,1:T(2,128)S(1)}, u32[]{:S(2)}, u32[]{:S(2)}) collective-permute-start(f32[2,1,18,64]{3,0,2,1:T(2,128)} %get-tuple-element.22), channel_id=1, source_target_pairs={{0,32},{32,64},{64,96},{96,128},{128,160},{160,192},{192,224},{1,3... | collective-permute-start | bytes 27656 | tf_op jit(solution)/shard_map/ppermute | solution.py:14
  16.3 1.3 collective-permute-start.1
  17.6 0.9 constant_dynamic-slice_fusion
  18.5 1.1 copy.90
  19.5 10.1 %copy.69 = bf16[8,8,512,64]{3,0,2,1:T(8,128)(2,1)} copy(bf16[8,8,512,64]{2,3,1,0:T(8,128)(2,1)} %param.13) | data formatting | bytes 8388608 | tf_op args[5]
  29.6 1.0 pad_maximum_fusion
  32.4 40.3 %all_gather.6 = bf16[8,512,64]{2,0,1:T(8,128)(2,1)} all-gather(bf16[8,16,64]{2,0,1:T(8,128)(2,1)S(1)} %get-tuple-element.19), channel_id=1, replica_groups=mesh['rows'=8,'specs'=32] {'specs'}, dimensions={1}, use_global_device_ids=true | all-gather | bytes 540672 | tf_op jit(solution)/shard_map/all_gather | solution.py:58
  72.6 2.7 copy.79
  75.3 2.7 %copy.80 = f32[8,512,64]{2,1,0:T(8,128)} copy(bf16[8,512,64]{1,2,0:T(8,128)(2,1)} %copy.79) | data formatting | bytes 1572864 | tf_op jit(solution)/shard_map/convert_element_type | solution.py:62
  78.1 46.9 %all_gather.7 = bf16[8,512,64]{2,0,1:T(8,128)(2,1)} all-gather(bf16[8,16,64]{2,0,1:T(8,128)(2,1)S(1)} %get-tuple-element.18), channel_id=1, replica_groups=mesh['rows'=8,'specs'=32] {'specs'}, dimensions={1}, use_global_device_ids=true | all-gather | bytes 540672 | tf_op jit(solution)/shard_map/all_gather | solution.py:59
  125.0 2.7 copy.87
  127.7 2.7 %copy.88 = f32[8,512,64]{2,1,0:T(8,128)} copy(bf16[8,512,64]{1,2,0:T(8,128)(2,1)} %copy.87) | data formatting | bytes 1572864 | tf_op jit(solution)/shard_map/convert_element_type | solution.py:64
  130.4 7.6 %fusion.3 = (f32[8]{0:T(128)S(1)}, bf16[8,8,512,64]{3,0,2,1:T(8,128)(2,1)S(1)}) fusion(bf16[8,8,512,64]{3,0,2,1:T(8,128)(2,1)} %copy.69, f32[64]{0:T(128)S(1)} %copy-done.5, f32[8,512,64]{2,1,0:T(8,128)} %copy.88, f32[8,512,64]{2,1,0:T(8,128)} %copy.80), kind=kLoop, calls=%fused_computation.5 | loop fusion | flops 18874360 | bytes 10486048 | tf_op jit(solution)/shard_map/reduce_sum | solution.py:63
  138.0 3.2 %copy-done.1 = bf16[8,8,512,64]{3,0,2,1:T(8,128)(2,1)} copy-done((bf16[8,8,512,64]{3,0,2,1:T(8,128)(2,1)}, bf16[8,8,512,64]{3,0,2,1:T(8,128)(2,1)S(1)}, u32[]{:S(2)}) %copy-start.1) | copy-done | bytes 4194328
  141.2 1.5 fusion.34
  142.7 2.7 copy.81
  145.4 9.2 %collective-permute-start.2 = (bf16[8,1,512,64]{2,3,1,0:T(8,128)(2,1)}, bf16[8,1,512,64]{2,3,1,0:T(8,128)(2,1)}, u32[]{:S(2)}, u32[]{:S(2)}) collective-permute-start(bf16[8,1,512,64]{2,3,1,0:T(8,128)(2,1)} %copy.81), channel_id=1, source_target_pairs={{0,32},{32,64},{64,96},{96,128},{128,160},{160,192},{192,224},{1,3... | collective-permute-start | bytes 1572872 | tf_op jit(solution)/shard_map/ppermute | solution.py:14
  154.6 2.7 copy.82
  157.3 1.5 collective-permute-start.3
  158.8 0.7 rev.5
  159.4 6.5 %collective-permute-done.2 = bf16[8,1,512,64]{2,3,1,0:T(8,128)(2,1)} collective-permute-done((bf16[8,1,512,64]{2,3,1,0:T(8,128)(2,1)}, bf16[8,1,512,64]{2,3,1,0:T(8,128)(2,1)}, u32[]{:S(2)}, u32[]{:S(2)}) %collective-permute-start.2) | collective-permute-done | bytes 524320 | tf_op jit(solution)/shard_map/ppermute | solution.py:14
  166.0 2.7 %copy.83 = bf16[8,1,512,64]{3,0,2,1:T(8,128)(2,1)} copy(bf16[8,1,512,64]{2,3,1,0:T(8,128)(2,1)} %collective-permute-done.2) | data formatting | bytes 1048576 | tf_op jit(solution)/shard_map/ppermute | solution.py:14
  168.7 34.8 %collective-permute-done.3 = bf16[8,1,512,64]{2,3,1,0:T(8,128)(2,1)} collective-permute-done((bf16[8,1,512,64]{2,3,1,0:T(8,128)(2,1)}, bf16[8,1,512,64]{2,3,1,0:T(8,128)(2,1)}, u32[]{:S(2)}, u32[]{:S(2)}) %collective-permute-start.3) | collective-permute-done | bytes 524320 | tf_op jit(solution)/shard_map/ppermute | solution.py:15
  203.5 2.8 %copy.84 = bf16[8,1,512,64]{3,0,2,1:T(8,128)(2,1)} copy(bf16[8,1,512,64]{2,3,1,0:T(8,128)(2,1)} %collective-permute-done.3) | data formatting | bytes 1048576 | tf_op jit(solution)/shard_map/ppermute | solution.py:15
  206.3 24.7 %subtract_reduce_fusion = (f32[8]{0:T(128)S(1)}, bf16[8,8,512,64]{3,0,2,1:T(8,128)(2,1)}) fusion(f32[8,512,64]{2,1,0:T(8,128)} %copy.72, f32[8,512,64]{2,1,0:T(8,128)S(1)} %copy.71, bf16[3,3,64,64]{3,2,1,0:T(8,128)(2,1)} %rev.5, bf16[8,1,512,64]{3,0,2,1:T(8,128)(2,1)} %copy.84, bf16[8,8,512,64]{3,0,2,1:T(8,128)(2,1)} %copy-done.1, ...), kind=kOutput, calls=%fused_computation.6 | convolution fusion | flops 2441084928 | bytes 11608096 | tf_op jit(solution)/shard_map/conv_general_dilated | solution.py:21
  231.3 27.2 %psum.7 = f32[8]{0:T(128)S(1)} all-reduce(f32[8]{0:T(128)S(1)} %add.36), channel_id=1, replica_groups=mesh['rows'=8,'specs'=32] {'rows'}, use_global_device_ids=true, to_apply=%region_2.3 | all-reduce | flops 8 | bytes 64 | tf_op jit(solution)/shard_map/psum | solution.py:74
  258.5 9.7 %copy.89 = bf16[8,8,512,64]{2,3,1,0:T(8,128)(2,1)} copy(bf16[8,8,512,64]{3,0,2,1:T(8,128)(2,1)} %get-tuple-element.13) | data formatting | bytes 8388608
  (31 shorter events, 2.4 us)
Async XLA Ops:
  0.6 16.9 %copy-start = (s32[8,512,64]{1,2,0:T(8,128)S(1)}, s32[8,512,64]{1,2,0:T(8,128)}, u32[]{:S(2)}) copy-start(s32[8,512,64]{1,2,0:T(8,128)} %param.12) | copy-start | bytes 3145732
  6.8 0.7 copy-start.3
  7.5 23.4 %copy-start.2 = (f32[3,3,64,64]{3,2,1,0:T(8,128)S(1)}, f32[3,3,64,64]{3,2,1,0:T(8,128)}, u32[]{:S(2)}) copy-start(f32[3,3,64,64]{3,2,1,0:T(8,128)} %param.10) | copy-start | bytes 442372
  7.5 23.4 %copy-start.7 = (pred[8,3]{0,1:T(4,128)(4,1)S(1)}, pred[8,3]{0,1:T(4,128)(4,1)}, u32[]{:S(2)}) copy-start(pred[8,3]{0,1:T(4,128)(4,1)} %constant.40) | copy-start | bytes 76
  8.1 21.5 %collective-permute-start = (f32[2,1,18,64]{3,0,2,1:T(2,128)}, f32[2,1,18,64]{3,0,2,1:T(2,128)S(1)}, u32[]{:S(2)}, u32[]{:S(2)}) collective-permute-start(f32[2,1,18,64]{3,0,2,1:T(2,128)} %get-tuple-element.22), channel_id=1, source_target_pairs={{0,32},{32,64},{64,96},{96,128},{128,160},{160,192},{192,224},{1,3... | collective-permute-start | bytes 27656 | tf_op jit(solution)/shard_map/ppermute | solution.py:14
  16.3 13.3 %collective-permute-start.1 = (f32[2,1,18,64]{3,0,2,1:T(2,128)}, f32[2,1,18,64]{3,0,2,1:T(2,128)S(1)}, u32[]{:S(2)}, u32[]{:S(2)}) collective-permute-start(f32[2,1,18,64]{3,0,2,1:T(2,128)} %get-tuple-element.23), channel_id=1, source_target_pairs={{32,0},{64,32},{96,64},{128,96},{160,128},{192,160},{224,192},{33,... | collective-permute-start | bytes 27656 | tf_op jit(solution)/shard_map/ppermute | solution.py:15
  17.6 14.7 %copy-start.5 = (f32[64]{0:T(128)S(1)}, f32[64]{0:T(128)}, u32[]{:S(2)}) copy-start(f32[64]{0:T(128)} %param.11) | copy-start | bytes 772
  138.0 3.2 %copy-start.1 = (bf16[8,8,512,64]{3,0,2,1:T(8,128)(2,1)}, bf16[8,8,512,64]{3,0,2,1:T(8,128)(2,1)S(1)}, u32[]{:S(2)}) copy-start(bf16[8,8,512,64]{3,0,2,1:T(8,128)(2,1)S(1)} %get-tuple-element.15) | copy-start | bytes 12582916
  145.4 20.5 %collective-permute-start.2 = (bf16[8,1,512,64]{2,3,1,0:T(8,128)(2,1)}, bf16[8,1,512,64]{2,3,1,0:T(8,128)(2,1)}, u32[]{:S(2)}, u32[]{:S(2)}) collective-permute-start(bf16[8,1,512,64]{2,3,1,0:T(8,128)(2,1)} %copy.81), channel_id=1, source_target_pairs={{0,32},{32,64},{64,96},{96,128},{128,160},{160,192},{192,224},{1,3... | collective-permute-start | bytes 1572872 | tf_op jit(solution)/shard_map/ppermute | solution.py:14
  157.3 46.2 %collective-permute-start.3 = (bf16[8,1,512,64]{2,3,1,0:T(8,128)(2,1)}, bf16[8,1,512,64]{2,3,1,0:T(8,128)(2,1)}, u32[]{:S(2)}, u32[]{:S(2)}) collective-permute-start(bf16[8,1,512,64]{2,3,1,0:T(8,128)(2,1)} %copy.82), channel_id=1, source_target_pairs={{32,0},{64,32},{96,64},{128,96},{160,128},{192,160},{224,192},{33,... | collective-permute-start | bytes 1572872 | tf_op jit(solution)/shard_map/ppermute | solution.py:15
  206.3 24.7 %copy-start.4 = (f32[4096]{0:T(1024)S(1)}, f32[4096]{0:T(1024)}, u32[]{:S(2)}) copy-start(f32[4096]{0:T(1024)} %param.15) | copy-start | bytes 49156
  206.3 24.7 %copy-start.6 = (s32[8]{0:T(128)S(1)}, s32[8]{0:T(128)}, u32[]{:S(2)}) copy-start(s32[8]{0:T(128)} %param.14) | copy-start | bytes 100
where the time goes:
time: 274 us; the launch traced here: 269 us
  blocking collectives  114 us (42%)
  local copies, waits for them, and re-layouts  55.5 us (20%)
  waiting for transfers between devices  41.4 us (15%)
  matrix products  25.9 us (9%)
  starting transfers between devices  20.1 us (7%)
  other arithmetic  10.5 us (4%)
    all_gather x1, blocking collectives, per_device(): lax.all_gather(intercepts, 'specs', axis=1, tiled=True)  46.9 us
    all_gather x1, blocking collectives, per_device(): lax.all_gather(slopes, 'specs', axis=1, tiled=True)  40.3 us
    ppermute x2, waiting for transfers between devices, padded_2(): after = lax.ppermute(initial, axis, down)  34.8 us
    unnamed x21, local copies, waits for them, and re-layouts  29.8 us
    psum x1, blocking collectives, per_device(): summed = lax.psum(partial_value, 'rows')  27.2 us
    conv_general_dilated x3, matrix products, convolve(): lax.conv_general_dilated(field, kernel, (1, 1), ((0, 0), (column_pad, col...  25.9 us
    ppermute x2, starting transfers between devices, padded_2(): before = lax.ppermute(last, axis, up)  17.4 us
    reduce_sum x1, other arithmetic, per_device(): jnp.sum(jnp.minimum(coeff_full, 0.0) * intercepts.astype(jnp.float32) + p...  7.64 us
  transfers between devices with their start and end apart: 4, of which 2 were waited for; matrix products, arithmetic and copies ran while one was open for 7% of the time, Pallas kernels for 0%

commit v1 on v0

v1 whole, which is shorter than its diff:
```python
import functools

import jax
import jax.numpy as jnp
from jax import lax
from jax.experimental import pallas as pl
from jax.experimental.pallas import tpu as pltpu
from jax.sharding import PartitionSpec as P

F32, BF16 = (jnp.float32, jnp.bfloat16)
SHARE = 8
UNITS = 7


def spread_columns(stack, columns):
    size = stack.shape[0] // 3
    where = lax.broadcasted_iota(jnp.int32, (size, columns), 1)
    right = pltpu.roll(stack[:size], 1, 1)
    left = pltpu.roll(stack[2 * size :], columns - 1, 1)
    right = jnp.where(where == 0, 0.0, right)
    left = jnp.where(where == columns - 1, 0.0, left)
    return right + stack[size : 2 * size] + left


def mul(a, b):
    return jnp.dot(a, b, preferred_element_type=F32)


def high_low(value):
    high = value.astype(BF16)
    return high, (value - high.astype(F32)).astype(BF16)


def send_kernel(
    where_ref,
    center_ref,
    radius_ref,
    status_ref,
    coeff_ref,
    out_ref,
    last_ref,
    first_ref,
    sems,
):
    rows = coeff_ref.shape[1]
    copies = [
        pltpu.make_async_copy(coeff_ref.at[:, rows - 1], last_ref, sems.at[0]),
        pltpu.make_async_copy(coeff_ref.at[:, 0], first_ref, sems.at[1]),
    ]
    for copy in copies:
        copy.start()
    high, low = high_low(center_ref[...])
    out_ref[0:2] = high
    out_ref[2:4] = low
    out_ref[4:6] = radius_ref[...].astype(BF16)
    out_ref[6:7] = status_ref[...].astype(F32).astype(BF16)
    for copy in copies:
        copy.wait()


def send_pass(where, center, radius, status, coeffs):
    specs, rows, channels, columns = coeffs.shape
    part = channels * 2 // SHARE
    box = pl.BlockSpec((2, part, columns), lambda g, w: (w[0], w[1], 0))
    edge = jax.ShapeDtypeStruct((specs, channels, columns), BF16)
    return pl.pallas_call(
        send_kernel,
        out_shape=(jax.ShapeDtypeStruct((UNITS, part, columns), BF16), edge, edge),
        grid_spec=pltpu.PrefetchScalarGridSpec(
            num_scalar_prefetch=1,
            grid=(1,),
            in_specs=[
                box,
                box,
                pl.BlockSpec((1, part, columns), lambda g, w: (w[2], w[1], 0)),
                pl.BlockSpec(memory_space=pl.ANY),
            ],
            out_specs=(
                pl.BlockSpec((UNITS, part, columns), lambda g, w: (0, 0, 0)),
                pl.BlockSpec(memory_space=pl.ANY),
                pl.BlockSpec(memory_space=pl.ANY),
            ),
            scratch_shapes=[pltpu.SemaphoreType.DMA((2,))],
        ),
    )(where, center, radius, status, coeffs)


def main_kernel(
    halo_ref,
    center_ref,
    radius_ref,
    status_ref,
    forward_ref,
    absolute_ref,
    backward_ref,
    bias_ref,
    coeff_ref,
    out_ref,
    edge_ref,
    slope_edge_ref,
    total_ref,
    ch_ref,
    cl_ref,
    rh_ref,
    rl_ref,
    status_ext_ref,
    slope_ref,
    intercept_ref,
    linear_ref,
    pre_ref,
):
    rows, channels, columns = center_ref.shape
    c = channels
    part = halo_ref.shape[2]

    @pl.when(pl.program_id(0) == 0)
    def _():
        for side, base in ((0, 0), (1, rows + 2)):
            for y in range(c // part):
                piece = halo_ref.at[2 * y + side]
                for k in range(2):
                    at = pl.ds((base + k) * c + y * part, part)
                    ch_ref[at, :] = piece[k]
                    cl_ref[at, :] = piece[2 + k]
                    rh_ref[at, :] = piece[4 + k]
                    rl_ref[at, :] = jnp.zeros((part, columns), BF16)
                row = 0 if side == 0 else rows + 1
                status_ext_ref[pl.ds(row * c + y * part, part), :] = piece[6]
        for h in range(rows):
            at = pl.ds((h + 2) * c, c)
            ch_ref[at, :], cl_ref[at, :] = high_low(center_ref[h])
            rh_ref[at, :], rl_ref[at, :] = high_low(radius_ref[h])
            status_ext_ref[pl.ds((h + 1) * c, c), :] = status_ref[h].astype(F32).astype(BF16)
        pre_ref[pl.ds(0, c), :] = jnp.zeros((c, columns), BF16)
        pre_ref[pl.ds((rows + 1) * c, c), :] = jnp.zeros((c, columns), BF16)

        @pl.loop(0, (rows + 2) // 2)
        def _(b):
            at = pl.ds(pl.multiple_of(b * 2 * c, 2 * c), 4 * c)
            here = pl.ds(pl.multiple_of(b * 2 * c, 2 * c), 2 * c)
            six = 6 * c
            fh, fl = (forward_ref[:six, :], forward_ref[six:, :])
            ah, al = (absolute_ref[:six, :], absolute_ref[six:, :])
            low = spread_columns(mul(fh, ch_ref[at, :]) + mul(fh, cl_ref[at, :]), columns)
            linear = low + bias_ref[...]
            center_out = linear + spread_columns(mul(fl, ch_ref[at, :]), columns)
            radius_out = spread_columns(
                mul(ah, rh_ref[at, :]) + mul(ah, rl_ref[at, :]) + mul(al, rh_ref[at, :]), columns
            )
            upper = center_out + radius_out
            lower = center_out - radius_out
            width = 2.0 * radius_out
            relaxed = jnp.minimum(jnp.maximum(upper, 0.0), width) / width
            status = status_ext_ref[here, :].astype(F32)
            open_ = status == 2.0
            slope = jnp.where(open_, relaxed, jnp.where(status == 1.0, 1.0, 0.0))
            slope_ref[here, :] = slope.astype(BF16)
            intercept = jnp.where(open_, -relaxed * jnp.minimum(lower, 0.0), 0.0)
            intercept_ref[here, :] = intercept.astype(BF16)
            linear_ref[here, :] = linear

        slope_edge_ref[0] = slope_ref[pl.ds(0, c), :]
        slope_edge_ref[1] = slope_ref[pl.ds((rows + 1) * c, c), :]

    total = jnp.zeros((8, columns), F32)
    for h in range(rows):
        at = pl.ds((h + 1) * c, c)
        coeff = coeff_ref[0, h]
        wide = coeff.astype(F32)
        pre = (wide * slope_ref[at, :].astype(F32)).astype(BF16)
        pre_ref[at, :] = pre
        terms = (
            jnp.minimum(wide, 0.0) * intercept_ref[at, :].astype(F32)
            + pre.astype(F32) * linear_ref[at, :]
        )
        total = total + jnp.sum(terms.reshape(c // 8, 8, columns), axis=0)

    for b in range(rows // 2):
        at = pl.ds(b * 2 * c, 4 * c)
        value = spread_columns(mul(backward_ref[...], pre_ref[at, :]), columns)
        for r in range(2):
            h = 2 * b + r
            row = value[r * c : (r + 1) * c]
            if h == 0 or h == rows - 1:
                edge_ref[0, 0 if h == 0 else 1] = row
            else:
                terms = jnp.abs(row) * radius_ref[h]
                total = total - jnp.sum(terms.reshape(c // 8, 8, columns), axis=0)
            out_ref[0, h] = row.astype(BF16)
    folded = total[:, :128]
    for k in range(1, columns // 128):
        folded = folded + total[:, k * 128 : (k + 1) * 128]
    total_ref[0] = folded


def main_pass(halo, center, radius, status, forward, absolute, backward, bias, coeffs):
    specs, rows, channels, columns = coeffs.shape
    whole = lambda a: pl.BlockSpec(a.shape, lambda s, n=a.ndim: (0,) * n)
    ext = (rows + 4) * channels
    mid = (rows + 2) * channels
    return pl.pallas_call(
        main_kernel,
        grid=(specs,),
        out_shape=(
            jax.ShapeDtypeStruct(coeffs.shape, BF16),
            jax.ShapeDtypeStruct((specs, 2, channels, columns), F32),
            jax.ShapeDtypeStruct((2, channels, columns), BF16),
            jax.ShapeDtypeStruct((specs, 8, 128), F32),
        ),
        in_specs=[
            whole(a) for a in (halo, center, radius, status, forward, absolute, backward, bias)
        ]
        + [pl.BlockSpec((1, rows, channels, columns), lambda s: (s, 0, 0, 0))],
        out_specs=(
            pl.BlockSpec((1, rows, channels, columns), lambda s: (s, 0, 0, 0)),
            pl.BlockSpec((1, 2, channels, columns), lambda s: (s, 0, 0, 0)),
            pl.BlockSpec((2, channels, columns), lambda s: (0, 0, 0)),
            pl.BlockSpec((1, 8, 128), lambda s: (s, 0, 0)),
        ),
        scratch_shapes=[pltpu.VMEM((ext, columns), BF16)] * 4
        + [
            pltpu.VMEM((mid, columns), BF16),
            pltpu.VMEM((mid, columns), BF16),
            pltpu.VMEM((mid, columns), BF16),
            pltpu.VMEM((mid, columns), F32),
            pltpu.VMEM((mid, columns), BF16),
        ],
        compiler_params=pltpu.CompilerParams(vmem_limit_bytes=48 << 20),
        cost_estimate=pl.CostEstimate(
            flops=20_000_000_000, bytes_accessed=16 << 20, transcendentals=0
        ),
    )(halo, center, radius, status, forward, absolute, backward, bias, coeffs)


def edge_kernel(
    before_ref,
    after_ref,
    slope_ref,
    edge_ref,
    first_ref,
    last_ref,
    weight_ref,
    total_ref,
    _,
    out_ref,
    sum_ref,
    done_ref,
    sems,
):
    specs, channels, columns = before_ref.shape
    rows = out_ref.shape[1]
    for s in range(specs):
        total = jnp.sum(total_ref[s], axis=0, keepdims=True)
        for k, (halo_ref, radius_ref) in enumerate(((before_ref, first_ref), (after_ref, last_ref))):
            pre = (halo_ref[s].astype(F32) * slope_ref[k].astype(F32)).astype(BF16)
            value = edge_ref[s, k] + spread_columns(mul(weight_ref[k], pre), columns)
            done_ref[s, k] = value.astype(BF16)
            pltpu.make_async_copy(
                done_ref.at[s, k], out_ref.at[s, 0 if k == 0 else rows - 1], sems.at[s, k]
            ).start()
            terms = jnp.abs(value) * radius_ref[0]
            terms = jnp.sum(terms.reshape(channels // 8, 8, columns), axis=0)
            folded = terms[:, :128]
            for m in range(1, columns // 128):
                folded = folded + terms[:, m * 128 : (m + 1) * 128]
            total = total - jnp.sum(folded, axis=0, keepdims=True)
        sum_ref[s : s + 1, :] = total
    for s in range(specs):
        for k in range(2):
            pltpu.make_async_copy(
                done_ref.at[s, k], out_ref.at[s, 0 if k == 0 else rows - 1], sems.at[s, k]
            ).wait()


def edge_pass(before, after, slope, edge, radius, weight, total, out):
    specs, rows, channels, columns = out.shape
    whole = lambda a: pl.BlockSpec(a.shape, lambda g, n=a.ndim: (0,) * n)
    return pl.pallas_call(
        edge_kernel,
        grid=(1,),
        out_shape=(
            jax.ShapeDtypeStruct(out.shape, BF16),
            jax.ShapeDtypeStruct((specs, 128), F32),
        ),
        in_specs=[
            whole(before),
            whole(after),
            whole(slope),
            whole(edge),
            pl.BlockSpec((1, channels, columns), lambda g: (0, 0, 0)),
            pl.BlockSpec((1, channels, columns), lambda g: (rows - 1, 0, 0)),
            whole(weight),
            whole(total),
            pl.BlockSpec(memory_space=pl.ANY),
        ],
        out_specs=(
            pl.BlockSpec(memory_space=pl.ANY),
            pl.BlockSpec((specs, 128), lambda g: (0, 0)),
        ),
        scratch_shapes=[
            pltpu.VMEM((specs, 2, channels, columns), BF16),
            pltpu.SemaphoreType.DMA((specs, 2)),
        ],
        input_output_aliases={8: 0},
        compiler_params=pltpu.CompilerParams(vmem_limit_bytes=32 << 20),
        cost_estimate=pl.CostEstimate(
            flops=400_000_000, bytes_accessed=4 << 20, transcendentals=0
        ),
    )(before, after, slope, edge, radius, radius, weight, total, out)


def bands(kernel):
    flat = jnp.transpose(kernel, (1, 2, 0, 3))
    columns, m, rows, k = flat.shape
    flat = flat.reshape(columns, m, rows * k)
    pair = jnp.stack(
        [jnp.pad(flat, ((0, 0), (0, 0), (0, k))), jnp.pad(flat, ((0, 0), (0, 0), (k, 0)))], axis=1
    )
    return pair.reshape(columns * 2 * m, 4 * k)


def split_weight(kernel):
    high = lax.reduce_precision(kernel, 8, 7)
    both = jnp.stack([high, kernel - high]).astype(BF16)
    return jnp.concatenate([bands(both[0]), bands(both[1])], axis=0)


def per_device(
    center, radius, conv_weight, conv_bias, split_status, out_coeffs, spec_ids, spec_offsets
):
    count, groups = (lax.axis_size("rows"), lax.axis_size("specs"))
    rows, columns, channels = center.shape
    center, radius, status = (jnp.swapaxes(a, 1, 2) for a in (center, radius, split_status))
    coeffs = jnp.swapaxes(out_coeffs, 2, 3)

    lanes = groups // SHARE
    me = lax.axis_index("specs")
    core, y = (lax.rem(me, 2), me // (2 * lanes))
    up = core == 0
    where = jnp.stack(
        [jnp.where(up, rows // 2 - 1, 0), y, jnp.where(up, rows - 1, 0)]
    ).astype(jnp.int32)
    box, last, first = send_pass(where, center, radius, status, coeffs)
    moves = []
    for r in range(count):
        for s in range(groups):
            other = r + (1 if s % 2 == 0 else -1)
            if 0 <= other < count:
                moves.append((r * groups + s, other * groups + s))
    box = lax.ppermute(box, ("rows", "specs"), moves)
    before = lax.ppermute(last, "rows", [(i, i + 1) for i in range(count - 1)])
    after = lax.ppermute(first, "rows", [(i + 1, i) for i in range(count - 1)])
    halo = lax.all_gather(
        box,
        "specs",
        axis_index_groups=[
            [(k * lanes + z) * 2 + e for k in range(SHARE // 2) for e in range(2)]
            for z in range(lanes)
        ],
    )

    turned = jnp.swapaxes(conv_weight, 2, 3)
    forward = split_weight(turned)
    absolute = split_weight(jnp.abs(turned))
    low = conv_weight.astype(BF16)
    backward = bands(low[::-1, ::-1])
    ends = jnp.stack(
        [
            low[2, ::-1].reshape(3 * channels, channels),
            low[0, ::-1].reshape(3 * channels, channels),
        ]
    )
    bias = jnp.tile(conv_bias, 2)[:, None]

    out, edge, slope, total = main_pass(
        halo, center, radius, status, forward, absolute, backward, bias, coeffs
    )
    out, partial = edge_pass(before, after, slope, edge, radius, ends, total, out)

    step = 1
    while step < count:
        partial = partial + lax.ppermute(partial, "rows", [(i, i ^ step) for i in range(count)])
        step *= 2
    summed = jnp.sum(partial, axis=1)
    pixels = rows * count * columns
    entries = spec_offsets.shape[0]
    onehot = spec_ids[:, None] == jnp.arange(entries, dtype=jnp.int32)[None, :]
    table_terms = jnp.sum(jnp.where(onehot, spec_offsets[None, :], 0.0), axis=1)
    bounds = summed / pixels + table_terms
    return (jnp.swapaxes(out, 2, 3), bounds)


def solution(mesh):
    in_specs = (
        P("rows", None, None),
        P("rows", None, None),
        P(),
        P(),
        P("rows", None, None),
        P("specs", "rows", None, None),
        P("specs"),
        P(),
    )
    out_specs = (P("specs", "rows", None, None), P("specs"))
    return jax.shard_map(
        per_device, mesh=mesh, in_specs=in_specs, out_specs=out_specs, check_vma=False
    )
```

time: 274 us -> 129 us (0.47)
  the two profiles are of different devices: /device:TPU:56 before, /device:TPU:4 now
where the time goes in v1:
time: 129 us; the launch traced here: 128 us
  Pallas kernels  55.3 us (43%)
  starting transfers between devices  21 us (16%)
  local copies, waits for them, and re-layouts  15.9 us (12%)
  waiting for transfers between devices  14.8 us (11%)
  blocking collectives  14.3 us (11%)
  other arithmetic  5.58 us (4%)
    pallas_call x1, Pallas kernels, send_pass(): pl.pallas_call(send_kernel, out_shape=(jax.ShapeDtypeStruct((UNITS, part,...  35.1 us
    pallas_call x1, Pallas kernels, main_pass(): pl.pallas_call(main_kernel, grid=(specs,), out_shape=(jax.ShapeDtypeStruc...  16.7 us
    ppermute x3, waiting for transfers between devices, per_device(): lax.ppermute(partial, 'rows', [(i, i ^ step) for i in range(count)])  14.8 us
    all_gather x1, blocking collectives, per_device(): lax.all_gather(box, 'specs', axis_index_groups=[[(k * lanes + z) * 2 + e...  14.3 us
    ppermute x1, starting transfers between devices, per_device(): box = lax.ppermute(box, ('rows', 'specs'), moves)  9.1 us
    ppermute x1, starting transfers between devices, per_device(): after = lax.ppermute(first, 'rows', [(i + 1, i) for i in range(count - 1)])  8.73 us
    another operation x10, local copies, waits for them, and re-layouts, bands(): jnp.stack([jnp.pad(flat, ((0, 0), (0, 0), (0, k))), jnp.pad(flat, ((0, 0)...  4.47 us
    unnamed x22, local copies, waits for them, and re-layouts  4.38 us
  transfers between devices with their start and end apart: 6, of which 3 were waited for; matrix products, arithmetic and copies ran while one was open for 12% of the time, Pallas kernels for 13%

profile of v1, /device:TPU:4, one launch (start us, length us, event | category | flops | bytes accessed | tf_op | source)
XLA Modules:
  0.0 127.7 jit_solution(16933482727415290498)
XLA Ops:
  0.7 0.6 pad_add_fusion.where_ref
  1.3 35.1 %shard_map.95 = (bf16[7,16,512]{2,1,0:T(8,128)(2,1)}, bf16[8,64,512]{2,1,0:T(8,128)(2,1)}, bf16[8,64,512]{2,1,0:T(8,128)(2,1)}) custom-call(s32[3]{0:T(128)} %pad_add_fusion.where_ref, f32[8,64,512]{2,1,0:T(8,128)} %bitcast.71, f32[8,64,512]{2,1,0:T(8,128)} %bitcast.67, s32[8,64,512]{2,1,0:T(8,128)} %bitcast.73, bf16[8,8,64,512]{3,2,1,0:T(8,128)(2,1)} %bitcast.78), custom_call_target="tpu_custom_call" | custom-call | tf_op jit(solution)/shard_map/pallas_call | solution.py:66
  36.4 9.1 %collective-permute-start.2 = (bf16[7,16,512]{2,1,0:T(8,128)(2,1)}, bf16[7,16,512]{2,1,0:T(8,128)(2,1)}, u32[]{:S(2)}, u32[]{:S(2)}) collective-permute-start(bf16[7,16,512]{2,1,0:T(8,128)(2,1)} %get-tuple-element.13), channel_id=1, source_target_pairs={{0,32},{2,34},{4,36},{6,38},{8,40},{10,42},{12,44},{14,46},{16,48}... | collective-permute-start | bytes 344072 | tf_op jit(solution)/shard_map/ppermute | solution.py:350
  45.5 1.9 %collective-permute-start = (bf16[8,64,512]{2,1,0:T(8,128)(2,1)}, bf16[8,64,512]{2,1,0:T(8,128)(2,1)}, u32[]{:S(2)}, u32[]{:S(2)}) collective-permute-start(bf16[8,64,512]{2,1,0:T(8,128)(2,1)} %get-tuple-element.11), channel_id=1, source_target_pairs={{0,32},{32,64},{64,96},{96,128},{128,160},{160,192},{192,224},{1,3... | collective-permute-start | bytes 1572872 | tf_op jit(solution)/shard_map/ppermute | solution.py:351
  47.4 8.7 %collective-permute-start.1 = (bf16[8,64,512]{2,1,0:T(8,128)(2,1)}, bf16[8,64,512]{2,1,0:T(8,128)(2,1)}, u32[]{:S(2)}, u32[]{:S(2)}) collective-permute-start(bf16[8,64,512]{2,1,0:T(8,128)(2,1)} %get-tuple-element.12), channel_id=1, source_target_pairs={{32,0},{64,32},{96,64},{128,96},{160,128},{192,160},{224,192},{33,... | collective-permute-start | bytes 1572872 | tf_op jit(solution)/shard_map/ppermute | solution.py:352
  56.1 0.8 fusion.5
  57.0 0.7 reverse_bitcast_fusion
  57.6 0.6 fusion.6
  58.4 0.8 copy.40
  59.5 0.8 copy.42
  60.5 0.8 copy.44
  61.4 1.1 copy.45
  62.6 0.8 copy.46
  63.4 1.0 copy.47
  64.6 0.8 copy.48
  65.5 0.8 broadcast_in_dim_tile.4.bias_ref
  66.2 1.4 %rev.10 = bf16[1,3,64,64]{3,2,1,0:T(8,128)(2,1)} reverse(bf16[1,3,64,64]{3,2,1,0:T(8,128)(2,1)} %get-tuple-element.24), dimensions={1} | reverse | bytes 49152 | tf_op jit(solution)/shard_map/rev | solution.py:369
  67.7 2.0 %pad_maximum_fusion.2 = (bf16[768,256]{1,0:T(8,128)(2,1)S(1)}, bf16[768,256]{1,0:T(8,128)(2,1)}) fusion(bf16[384,256]{1,0:T(8,128)(2,1)} %bitcast.81, bf16[384,256]{1,0:T(8,128)(2,1)} %bitcast.80, bf16[384,256]{1,0:T(8,128)(2,1)} %bitcast.83, bf16[384,256]{1,0:T(8,128)(2,1)} %bitcast.82), kind=kLoop, calls=%fused_computation.6 | loop fusion | flops 1572864 | bytes 1572864 | tf_op jit(solution)/shard_map/concatenate | solution.py:325
  69.7 1.4 %rev.11 = bf16[1,3,64,64]{3,2,1,0:T(8,128)(2,1)} reverse(bf16[1,3,64,64]{3,2,1,0:T(8,128)(2,1)} %get-tuple-element.25), dimensions={1} | reverse | bytes 49152 | tf_op jit(solution)/shard_map/rev | solution.py:370
  71.1 0.8 pad_maximum_fusion.7.weight_ref
  71.9 14.3 %all-gather = bf16[56,16,512]{2,1,0:T(8,128)(2,1)S(1)} all-gather(bf16[7,16,512]{2,1,0:T(8,128)(2,1)} %collective-permute-done.2), channel_id=2, replica_groups={{0,1,8,9,16,17,24,25},{2,3,10,11,18,19,26,27},{4,5,12,13,20,21,28,29},{..., dimensions={0}, use_global_device_ids=true | all-gather | bytes 1032192 | tf_op jit(solution)/shard_map/all_gather | solution.py:353
  86.2 1.0 copy-done.4
  87.2 0.9 copy-done.5
  88.1 0.8 copy-done.6
  89.0 16.7 %shard_map.96 = (bf16[8,8,64,512]{3,2,1,0:T(8,128)(2,1)}, f32[8,2,64,512]{3,2,1,0:T(8,128)}, bf16[2,64,512]{2,1,0:T(8,128)(2,1)S(1)}, f32[8,8,128]{2,1,0:T(8,128)S(1)}) custom-call(bf16[8,7,16,512]{3,2,1,0:T(8,128)(2,1)S(1)} %bitcast.75, f32[8,64,512]{2,1,0:T(8,128)S(1)} %bitcast.72, f32[8,64,512]{2,1,0:T(8,128)S(1)} %bitcast.68, ...), custom_call_target="tpu_custom_call" | custom-call | flops 20000000000 | bytes 16777216 | tf_op jit(solution)/shard_map/pallas_call | solution.py:201
  105.7 1.6 %copy-done.1 = f32[8,2,64,512]{3,2,1,0:T(8,128)S(1)} copy-done((f32[8,2,64,512]{3,2,1,0:T(8,128)S(1)}, f32[8,2,64,512]{3,2,1,0:T(8,128)}, u32[]{:S(2)}) %copy-start.1) | copy-done | bytes 2097176
  107.3 3.5 %shard_map.97 = (bf16[8,8,64,512]{3,2,1,0:T(8,128)(2,1)}, f32[8,128]{1,0:T(8,128)S(1)}) custom-call(bf16[8,64,512]{2,1,0:T(8,128)(2,1)} %collective-permute-done.before_ref, bf16[8,64,512]{2,1,0:T(8,128)(2,1)} %collective-permute-done.1.after_ref, bf16[2,64,512]{2,1,0:T(8,128)(2,1)S(1)} %get-tuple-element.14.slope_ref, ...), custom_call_target="tpu_custom_call", output_to_operand_aliasing={{0}: (8, {})} | custom-call | flops 400000000 | bytes 4194304 | tf_op jit(solution)/shard_map/pallas_call | solution.py:278
  110.9 7.5 %collective-permute-done.3 = f32[8,128]{1,0:T(8,128)S(1)} collective-permute-done((f32[8,128]{1,0:T(8,128)S(1)}, f32[8,128]{1,0:T(8,128)S(1)}, u32[]{:S(2)}, u32[]{:S(2)}) %collective-permute-start.3) | collective-permute-done | bytes 4128 | tf_op jit(solution)/shard_map/ppermute | solution.py:382
  118.4 1.2 collective-permute-start.4
  119.6 2.4 %collective-permute-done.4 = f32[8,128]{1,0:T(8,128)S(1)} collective-permute-done((f32[8,128]{1,0:T(8,128)S(1)}, f32[8,128]{1,0:T(8,128)S(1)}, u32[]{:S(2)}, u32[]{:S(2)}) %collective-permute-start.4) | collective-permute-done | bytes 4128 | tf_op jit(solution)/shard_map/ppermute | solution.py:382
  122.2 4.9 %collective-permute-done.5 = f32[8,128]{1,0:T(8,128)S(1)} collective-permute-done((f32[8,128]{1,0:T(8,128)S(1)}, f32[8,128]{1,0:T(8,128)S(1)}, u32[]{:S(2)}, u32[]{:S(2)}) %collective-permute-start.5) | collective-permute-done | bytes 4128 | tf_op jit(solution)/shard_map/ppermute | solution.py:382
  127.2 0.5 multiply_add_fusion
  (42 shorter events, 1.2 us)
Async XLA Ops:
  0.6 55.5 %copy-start.7 = (f32[3,3,64,64]{3,2,1,0:T(8,128)S(1)}, f32[3,3,64,64]{3,2,1,0:T(8,128)}, u32[]{:S(2)}) copy-start(f32[3,3,64,64]{3,2,1,0:T(8,128)} %param.10) | copy-start | bytes 442372
  36.4 35.6 %collective-permute-start.2 = (bf16[7,16,512]{2,1,0:T(8,128)(2,1)}, bf16[7,16,512]{2,1,0:T(8,128)(2,1)}, u32[]{:S(2)}, u32[]{:S(2)}) collective-permute-start(bf16[7,16,512]{2,1,0:T(8,128)(2,1)} %get-tuple-element.13), channel_id=1, source_target_pairs={{0,32},{2,34},{4,36},{6,38},{8,40},{10,42},{12,44},{14,46},{16,48}... | collective-permute-start | bytes 344072 | tf_op jit(solution)/shard_map/ppermute | solution.py:350
  45.5 60.2 %collective-permute-start = (bf16[8,64,512]{2,1,0:T(8,128)(2,1)}, bf16[8,64,512]{2,1,0:T(8,128)(2,1)}, u32[]{:S(2)}, u32[]{:S(2)}) collective-permute-start(bf16[8,64,512]{2,1,0:T(8,128)(2,1)} %get-tuple-element.11), channel_id=1, source_target_pairs={{0,32},{32,64},{64,96},{96,128},{128,160},{160,192},{192,224},{1,3... | collective-permute-start | bytes 1572872 | tf_op jit(solution)/shard_map/ppermute | solution.py:351
  47.4 58.3 %collective-permute-start.1 = (bf16[8,64,512]{2,1,0:T(8,128)(2,1)}, bf16[8,64,512]{2,1,0:T(8,128)(2,1)}, u32[]{:S(2)}, u32[]{:S(2)}) collective-permute-start(bf16[8,64,512]{2,1,0:T(8,128)(2,1)} %get-tuple-element.12), channel_id=1, source_target_pairs={{32,0},{64,32},{96,64},{128,96},{160,128},{192,160},{224,192},{33,... | collective-permute-start | bytes 1572872 | tf_op jit(solution)/shard_map/ppermute | solution.py:352
  59.3 6.2 %copy-start.10 = (f32[64]{0:T(128)S(1)}, f32[64]{0:T(128)}, u32[]{:S(2)}) copy-start(f32[64]{0:T(128)} %param.11) | copy-start | bytes 772
  60.5 25.7 %copy-start = (f32[8,512,64]{1,2,0:T(8,128)S(1)}, f32[8,512,64]{1,2,0:T(8,128)}, u32[]{:S(2)}) copy-start(f32[8,512,64]{1,2,0:T(8,128)} %param.9) | copy-start | bytes 3145732
  60.5 25.7 %copy-start.2 = (f32[8,512,64]{1,2,0:T(8,128)S(1)}, f32[8,512,64]{1,2,0:T(8,128)}, u32[]{:S(2)}) copy-start(f32[8,512,64]{1,2,0:T(8,128)} %param.8) | copy-start | bytes 3145732
  60.5 25.7 %copy-start.3 = (s32[8,512,64]{1,2,0:T(8,128)S(1)}, s32[8,512,64]{1,2,0:T(8,128)}, u32[]{:S(2)}) copy-start(s32[8,512,64]{1,2,0:T(8,128)} %param.12) | copy-start | bytes 3145732
  86.2 1.0 copy-start.4
  87.2 0.9 copy-start.5
  88.1 0.8 copy-start.6
  105.7 1.6 %copy-start.1 = (f32[8,2,64,512]{3,2,1,0:T(8,128)S(1)}, f32[8,2,64,512]{3,2,1,0:T(8,128)}, u32[]{:S(2)}) copy-start(f32[8,2,64,512]{3,2,1,0:T(8,128)} %get-tuple-element.15.edge_ref) | copy-start | bytes 6291460
  107.2 14.7 %copy-start.8 = (f32[4096]{0:T(1024)S(1)}, f32[4096]{0:T(1024)}, u32[]{:S(2)}) copy-start(f32[4096]{0:T(1024)} %param.15) | copy-start | bytes 49156
  107.3 14.7 %copy-start.9 = (s32[8]{0:T(128)S(1)}, s32[8]{0:T(128)}, u32[]{:S(2)}) copy-start(s32[8]{0:T(128)} %param.14) | copy-start | bytes 100
  110.8 7.6 %collective-permute-start.3 = (f32[8,128]{1,0:T(8,128)S(1)}, f32[8,128]{1,0:T(8,128)S(1)}, u32[]{:S(2)}, u32[]{:S(2)}) collective-permute-start(f32[8,128]{1,0:T(8,128)S(1)} %get-tuple-element.19), channel_id=1, source_target_pairs={{0,32},{32,0},{64,96},{96,64},{128,160},{160,128},{192,224},{224,1... | collective-permute-start | bytes 12296 | tf_op jit(solution)/shard_map/ppermute | solution.py:382
  118.4 3.6 %collective-permute-start.4 = (f32[8,128]{1,0:T(8,128)S(1)}, f32[8,128]{1,0:T(8,128)S(1)}, u32[]{:S(2)}, u32[]{:S(2)}) collective-permute-start(f32[8,128]{1,0:T(8,128)S(1)} %add.33), channel_id=1, source_target_pairs={{0,64},{32,96},{64,0},{96,32},{128,192},{160,224},{192,128},{224,1... | collective-permute-start | bytes 12296 | tf_op jit(solution)/shard_map/ppermute | solution.py:382
  122.0 5.1 %collective-permute-start.5 = (f32[8,128]{1,0:T(8,128)S(1)}, f32[8,128]{1,0:T(8,128)S(1)}, u32[]{:S(2)}, u32[]{:S(2)}) collective-permute-start(f32[8,128]{1,0:T(8,128)S(1)} %add.34), channel_id=1, source_target_pairs={{0,128},{32,160},{64,192},{96,224},{128,0},{160,32},{192,64},{224,... | collective-permute-start | bytes 12296 | tf_op jit(solution)/shard_map/ppermute | solution.py:382

commit v2 on v1

--- a/solution.py
+++ b/solution.py
@@ -40,22 +40,26 @@
     out_ref,
     last_ref,
     first_ref,
+    held_ref,
     sems,
 ):
     rows = coeff_ref.shape[1]
-    copies = [
-        pltpu.make_async_copy(coeff_ref.at[:, rows - 1], last_ref, sems.at[0]),
-        pltpu.make_async_copy(coeff_ref.at[:, 0], first_ref, sems.at[1]),
-    ]
-    for copy in copies:
-        copy.start()
+    reads = []
+    for k, h in enumerate((rows - 1, 0)):
+        reads.append(pltpu.make_async_copy(coeff_ref.at[:, h], held_ref.at[k], sems.at[k]))
+        reads[k].start()
     high, low = high_low(center_ref[...])
     out_ref[0:2] = high
     out_ref[2:4] = low
     out_ref[4:6] = radius_ref[...].astype(BF16)
     out_ref[6:7] = status_ref[...].astype(F32).astype(BF16)
-    for copy in copies:
-        copy.wait()
+    writes = []
+    for k, ref in enumerate((last_ref, first_ref)):
+        reads[k].wait()
+        writes.append(pltpu.make_async_copy(held_ref.at[k], ref, sems.at[2 + k]))
+        writes[k].start()
+    for k in range(2):
+        writes[k].wait()
 
 
 def send_pass(where, center, radius, status, coeffs):
@@ -80,7 +84,10 @@
                 pl.BlockSpec(memory_space=pl.ANY),
                 pl.BlockSpec(memory_space=pl.ANY),
             ),
-            scratch_shapes=[pltpu.SemaphoreType.DMA((2,))],
+            scratch_shapes=[
+                pltpu.VMEM((2, specs, channels, columns), BF16),
+                pltpu.SemaphoreType.DMA((4,)),
+            ],
         ),
     )(where, center, radius, status, coeffs)
 
@@ -309,20 +316,47 @@
     )(before, after, slope, edge, radius, radius, weight, total, out)
 
 
-def bands(kernel):
-    flat = jnp.transpose(kernel, (1, 2, 0, 3))
-    columns, m, rows, k = flat.shape
-    flat = flat.reshape(columns, m, rows * k)
-    pair = jnp.stack(
-        [jnp.pad(flat, ((0, 0), (0, 0), (0, k))), jnp.pad(flat, ((0, 0), (0, 0), (k, 0)))], axis=1
+def weight_kernel(weight_ref, bias_ref, forward_ref, absolute_ref, backward_ref, ends_ref, tall_ref):
+    c = weight_ref.shape[2]
+    zero = jnp.zeros((c, c), F32)
+
+    def place(ref, base, blocks):
+        three = jnp.concatenate(blocks, axis=1)
+        ref[pl.ds(base, c), :] = jnp.concatenate([three, zero], axis=1).astype(BF16)
+        ref[pl.ds(base + c, c), :] = jnp.concatenate([zero, three], axis=1).astype(BF16)
+
+    for j in range(3):
+        turned = [weight_ref[i, j].T for i in range(3)]
+        for ref, blocks in ((forward_ref, turned), (absolute_ref, [jnp.abs(w) for w in turned])):
+            high = [w.astype(BF16).astype(F32) for w in blocks]
+            place(ref, j * 2 * c, high)
+            place(ref, (3 + j) * 2 * c, [w - h for w, h in zip(blocks, high)])
+        place(backward_ref, j * 2 * c, [weight_ref[i, 2 - j] for i in (2, 1, 0)])
+        for k, i in enumerate((2, 0)):
+            ends_ref[k, pl.ds(j * c, c), :] = weight_ref[i, 2 - j].astype(BF16)
+    tall = jnp.broadcast_to(bias_ref[...], (8, c)).T[:, :1]
+    tall_ref[pl.ds(0, c), :] = tall
+    tall_ref[pl.ds(c, c), :] = tall
+
+
+def weight_pass(weight, bias):
+    c = weight.shape[2]
+    whole = lambda a: pl.BlockSpec(a.shape, lambda g, n=len(a.shape): (0,) * n)
+    out = (
+        jax.ShapeDtypeStruct((12 * c, 4 * c), BF16),
+        jax.ShapeDtypeStruct((12 * c, 4 * c), BF16),
+        jax.ShapeDtypeStruct((6 * c, 4 * c), BF16),
+        jax.ShapeDtypeStruct((2, 3 * c, c), BF16),
+        jax.ShapeDtypeStruct((2 * c, 1), F32),
     )
-    return pair.reshape(columns * 2 * m, 4 * k)
-
-
-def split_weight(kernel):
-    high = lax.reduce_precision(kernel, 8, 7)
-    both = jnp.stack([high, kernel - high]).astype(BF16)
-    return jnp.concatenate([bands(both[0]), bands(both[1])], axis=0)
+    bias = bias[None, :]
+    return pl.pallas_call(
+        weight_kernel,
+        grid=(1,),
+        out_shape=out,
+        in_specs=[whole(weight), whole(bias)],
+        out_specs=tuple(whole(a) for a in out),
+    )(weight, bias)
 
 
 def per_device(
@@ -359,19 +393,7 @@
         ],
     )
 
-    turned = jnp.swapaxes(conv_weight, 2, 3)
-    forward = split_weight(turned)
-    absolute = split_weight(jnp.abs(turned))
-    low = conv_weight.astype(BF16)
-    backward = bands(low[::-1, ::-1])
-    ends = jnp.stack(
-        [
-            low[2, ::-1].reshape(3 * channels, channels),
-            low[0, ::-1].reshape(3 * channels, channels),
-        ]
-    )
-    bias = jnp.tile(conv_bias, 2)[:, None]
-
+    forward, absolute, backward, ends, bias = weight_pass(conv_weight, conv_bias)
     out, edge, slope, total = main_pass(
         halo, center, radius, status, forward, absolute, backward, bias, coeffs
     )

time: 129 us -> 93 us (0.72)
  the two profiles are of different devices: /device:TPU:4 before, /device:TPU:12 now
where the time goes in v2:
time: 93 us; the launch traced here: 92.4 us
  Pallas kernels  27.6 us (30%)
  waiting for transfers between devices  23.6 us (25%)
  starting transfers between devices  19.8 us (21%)
  blocking collectives  13.8 us (15%)
  local copies, waits for them, and re-layouts  5.37 us (6%)
  other arithmetic  1.5 us (2%)
    pallas_call x1, Pallas kernels, main_pass(): pl.pallas_call(main_kernel, grid=(specs,), out_shape=(jax.ShapeDtypeStruc...  16.7 us
    ppermute x3, waiting for transfers between devices, per_device(): lax.ppermute(partial, 'rows', [(i, i ^ step) for i in range(count)])  16 us
    all_gather x1, blocking collectives, per_device(): lax.all_gather(box, 'specs', axis_index_groups=[[(k * lanes + z) * 2 + e...  13.8 us
    ppermute x1, starting transfers between devices, per_device(): box = lax.ppermute(box, ('rows', 'specs'), moves)  9.1 us
    ppermute x1, starting transfers between devices, per_device(): after = lax.ppermute(first, 'rows', [(i + 1, i) for i in range(count - 1)])  8.73 us
    ppermute x1, waiting for transfers between devices, per_device(): after = lax.ppermute(first, 'rows', [(i + 1, i) for i in range(count - 1)])  7.61 us
    unnamed x22, local copies, waits for them, and re-layouts  5.37 us
    pallas_call x1, Pallas kernels, send_pass(): pl.pallas_call(send_kernel, out_shape=(jax.ShapeDtypeStruct((UNITS, part,...  4.52 us
  transfers between devices with their start and end apart: 6, of which 4 were waited for; matrix products, arithmetic and copies ran while one was open for 0% of the time, Pallas kernels for 21%

profile of v2, /device:TPU:12, one launch (start us, length us, event | category | flops | bytes accessed | tf_op | source)
XLA Modules:
  0.0 92.4 jit_solution(15509249228230320958)
XLA Ops:
  0.6 0.6 pad_add_fusion.where_ref
  1.3 4.5 %shard_map.95 = (bf16[7,16,512]{2,1,0:T(8,128)(2,1)}, bf16[8,64,512]{2,1,0:T(8,128)(2,1)}, bf16[8,64,512]{2,1,0:T(8,128)(2,1)}) custom-call(s32[3]{0:T(128)} %pad_add_fusion.where_ref, f32[8,64,512]{2,1,0:T(8,128)} %bitcast.14, f32[8,64,512]{2,1,0:T(8,128)} %bitcast.10, s32[8,64,512]{2,1,0:T(8,128)} %bitcast.16, bf16[8,8,64,512]{3,2,1,0:T(8,128)(2,1)} %bitcast.20), custom_call_target="tpu_custom_call" | custom-call | tf_op jit(solution)/shard_map/pallas_call | solution.py:70
  5.8 9.1 %collective-permute-start.2 = (bf16[7,16,512]{2,1,0:T(8,128)(2,1)}, bf16[7,16,512]{2,1,0:T(8,128)(2,1)S(1)}, u32[]{:S(2)}, u32[]{:S(2)}) collective-permute-start(bf16[7,16,512]{2,1,0:T(8,128)(2,1)} %get-tuple-element.18), channel_id=1, source_target_pairs={{0,32},{2,34},{4,36},{6,38},{8,40},{10,42},{12,44},{14,46},{16,48}... | collective-permute-start | bytes 344072 | tf_op jit(solution)/shard_map/ppermute | solution.py:384
  14.9 1.9 %collective-permute-start = (bf16[8,64,512]{2,1,0:T(8,128)(2,1)}, bf16[8,64,512]{2,1,0:T(8,128)(2,1)}, u32[]{:S(2)}, u32[]{:S(2)}) collective-permute-start(bf16[8,64,512]{2,1,0:T(8,128)(2,1)} %get-tuple-element.16), channel_id=1, source_target_pairs={{0,32},{32,64},{64,96},{96,128},{128,160},{160,192},{192,224},{1,3... | collective-permute-start | bytes 1572872 | tf_op jit(solution)/shard_map/ppermute | solution.py:385
  16.9 8.7 %collective-permute-start.1 = (bf16[8,64,512]{2,1,0:T(8,128)(2,1)}, bf16[8,64,512]{2,1,0:T(8,128)(2,1)}, u32[]{:S(2)}, u32[]{:S(2)}) collective-permute-start(bf16[8,64,512]{2,1,0:T(8,128)(2,1)} %get-tuple-element.17), channel_id=1, source_target_pairs={{32,0},{64,32},{96,64},{128,96},{160,128},{192,160},{224,192},{33,... | collective-permute-start | bytes 1572872 | tf_op jit(solution)/shard_map/ppermute | solution.py:386
  25.6 2.8 %shard_map.96 = (bf16[768,256]{1,0:T(8,128)(2,1)}, bf16[768,256]{1,0:T(8,128)(2,1)}, bf16[384,256]{1,0:T(8,128)(2,1)}, bf16[2,192,64]{2,1,0:T(8,128)(2,1)}, f32[128,1]{1,0:T(8,128)}) custom-call(f32[3,3,64,64]{3,2,1,0:T(8,128)} %weight_ref.1, f32[1,64]{1,0:T(1,128)} %bitcast.22), custom_call_target="tpu_custom_call" | custom-call | tf_op jit(solution)/shard_map/pallas_call | solution.py:353
  28.4 0.0 collective-permute-done.2
  28.5 13.8 %all-gather = bf16[56,16,512]{2,1,0:T(8,128)(2,1)S(1)} all-gather(bf16[7,16,512]{2,1,0:T(8,128)(2,1)S(1)} %collective-permute-done.2), channel_id=2, replica_groups={{0,1,8,9,16,17,24,25},{2,3,10,11,18,19,26,27},{4,5,12,13,20,21,28,29},{..., dimensions={0}, use_global_device_ids=true | all-gather | bytes 1032192 | tf_op jit(solution)/shard_map/all_gather | solution.py:387
  42.2 0.0 copy-done
  42.2 0.0 copy-done.2
  42.2 0.0 copy-done.3
  42.2 1.0 %copy-done.5 = bf16[768,256]{1,0:T(8,128)(2,1)S(1)} copy-done((bf16[768,256]{1,0:T(8,128)(2,1)S(1)}, bf16[768,256]{1,0:T(8,128)(2,1)}, u32[]{:S(2)}) %copy-start.5) | copy-done | bytes 393240
  43.2 1.0 %copy-done.6 = bf16[768,256]{1,0:T(8,128)(2,1)S(1)} copy-done((bf16[768,256]{1,0:T(8,128)(2,1)S(1)}, bf16[768,256]{1,0:T(8,128)(2,1)}, u32[]{:S(2)}) %copy-start.6) | copy-done | bytes 393240
  44.2 0.9 %copy-done.7 = bf16[384,256]{1,0:T(8,128)(2,1)S(1)} copy-done((bf16[384,256]{1,0:T(8,128)(2,1)S(1)}, bf16[384,256]{1,0:T(8,128)(2,1)}, u32[]{:S(2)}) %copy-start.7) | copy-done | bytes 196632
  45.1 0.8 copy-done.8
  46.0 16.7 %shard_map.97 = (bf16[8,8,64,512]{3,2,1,0:T(8,128)(2,1)}, f32[8,2,64,512]{3,2,1,0:T(8,128)}, bf16[2,64,512]{2,1,0:T(8,128)(2,1)S(1)}, f32[8,8,128]{2,1,0:T(8,128)S(1)}) custom-call(bf16[8,7,16,512]{3,2,1,0:T(8,128)(2,1)S(1)} %bitcast.18, f32[8,64,512]{2,1,0:T(8,128)S(1)} %bitcast.15, f32[8,64,512]{2,1,0:T(8,128)S(1)} %bitcast.11, ...), custom_call_target="tpu_custom_call" | custom-call | flops 20000000000 | bytes 16777216 | tf_op jit(solution)/shard_map/pallas_call | solution.py:208
  62.7 0.0 collective-permute-done.before_ref
  62.7 7.6 %collective-permute-done.1.after_ref = bf16[8,64,512]{2,1,0:T(8,128)(2,1)} collective-permute-done((bf16[8,64,512]{2,1,0:T(8,128)(2,1)}, bf16[8,64,512]{2,1,0:T(8,128)(2,1)}, u32[]{:S(2)}, u32[]{:S(2)}) %collective-permute-start.1) | collective-permute-done | bytes 524320 | tf_op jit(solution)/shard_map/ppermute | solution.py:386
  70.3 0.0 copy-done.4
  70.3 1.6 %copy-done.1 = f32[8,2,64,512]{3,2,1,0:T(8,128)S(1)} copy-done((f32[8,2,64,512]{3,2,1,0:T(8,128)S(1)}, f32[8,2,64,512]{3,2,1,0:T(8,128)}, u32[]{:S(2)}) %copy-start.1) | copy-done | bytes 2097176
  71.9 3.5 %shard_map.98 = (bf16[8,8,64,512]{3,2,1,0:T(8,128)(2,1)}, f32[8,128]{1,0:T(8,128)S(1)}) custom-call(bf16[8,64,512]{2,1,0:T(8,128)(2,1)} %collective-permute-done.before_ref, bf16[8,64,512]{2,1,0:T(8,128)(2,1)} %collective-permute-done.1.after_ref, bf16[2,64,512]{2,1,0:T(8,128)(2,1)S(1)} %get-tuple-element.23.slope_ref, ...), custom_call_target="tpu_custom_call", output_to_operand_aliasing={{0}: (8, {})} | custom-call | flops 400000000 | bytes 4194304 | tf_op jit(solution)/shard_map/pallas_call | solution.py:285
  75.4 0.1 collective-permute-start.3
  75.5 7.5 %collective-permute-done.3 = f32[8,128]{1,0:T(8,128)S(1)} collective-permute-done((f32[8,128]{1,0:T(8,128)S(1)}, f32[8,128]{1,0:T(8,128)S(1)}, u32[]{:S(2)}, u32[]{:S(2)}) %collective-permute-start.3) | collective-permute-done | bytes 4128 | tf_op jit(solution)/shard_map/ppermute | solution.py:404
  83.0 0.0 collective-permute-start.4
  83.0 3.6 %collective-permute-done.4 = f32[8,128]{1,0:T(8,128)S(1)} collective-permute-done((f32[8,128]{1,0:T(8,128)S(1)}, f32[8,128]{1,0:T(8,128)S(1)}, u32[]{:S(2)}, u32[]{:S(2)}) %collective-permute-start.4) | collective-permute-done | bytes 4128 | tf_op jit(solution)/shard_map/ppermute | solution.py:404
  86.6 0.0 collective-permute-start.5
  86.6 0.0 copy-done.9
  86.6 0.0 copy-done.10
  86.7 0.2 select_reduce_fusion
  86.9 4.9 %collective-permute-done.5 = f32[8,128]{1,0:T(8,128)S(1)} collective-permute-done((f32[8,128]{1,0:T(8,128)S(1)}, f32[8,128]{1,0:T(8,128)S(1)}, u32[]{:S(2)}, u32[]{:S(2)}) %collective-permute-start.5) | collective-permute-done | bytes 4128 | tf_op jit(solution)/shard_map/ppermute | solution.py:404
  91.7 0.1 add_reduce_fusion
  91.9 0.5 multiply_add_fusion
  (13 shorter events, 0.0 us)
Async XLA Ops:
  1.3 40.9 %copy-start = (f32[8,512,64]{1,2,0:T(8,128)S(1)}, f32[8,512,64]{1,2,0:T(8,128)}, u32[]{:S(2)}) copy-start(f32[8,512,64]{1,2,0:T(8,128)} %param.9) | copy-start | bytes 3145732
  1.3 40.9 %copy-start.2 = (f32[8,512,64]{1,2,0:T(8,128)S(1)}, f32[8,512,64]{1,2,0:T(8,128)}, u32[]{:S(2)}) copy-start(f32[8,512,64]{1,2,0:T(8,128)} %param.8) | copy-start | bytes 3145732
  1.3 40.9 %copy-start.3 = (s32[8,512,64]{1,2,0:T(8,128)S(1)}, s32[8,512,64]{1,2,0:T(8,128)}, u32[]{:S(2)}) copy-start(s32[8,512,64]{1,2,0:T(8,128)} %param.12) | copy-start | bytes 3145732
  5.8 22.6 %collective-permute-start.2 = (bf16[7,16,512]{2,1,0:T(8,128)(2,1)}, bf16[7,16,512]{2,1,0:T(8,128)(2,1)S(1)}, u32[]{:S(2)}, u32[]{:S(2)}) collective-permute-start(bf16[7,16,512]{2,1,0:T(8,128)(2,1)} %get-tuple-element.18), channel_id=1, source_target_pairs={{0,32},{2,34},{4,36},{6,38},{8,40},{10,42},{12,44},{14,46},{16,48}... | collective-permute-start | bytes 344072 | tf_op jit(solution)/shard_map/ppermute | solution.py:384
  14.9 47.7 %collective-permute-start = (bf16[8,64,512]{2,1,0:T(8,128)(2,1)}, bf16[8,64,512]{2,1,0:T(8,128)(2,1)}, u32[]{:S(2)}, u32[]{:S(2)}) collective-permute-start(bf16[8,64,512]{2,1,0:T(8,128)(2,1)} %get-tuple-element.16), channel_id=1, source_target_pairs={{0,32},{32,64},{64,96},{96,128},{128,160},{160,192},{192,224},{1,3... | collective-permute-start | bytes 1572872 | tf_op jit(solution)/shard_map/ppermute | solution.py:385
  16.9 53.4 %collective-permute-start.1 = (bf16[8,64,512]{2,1,0:T(8,128)(2,1)}, bf16[8,64,512]{2,1,0:T(8,128)(2,1)}, u32[]{:S(2)}, u32[]{:S(2)}) collective-permute-start(bf16[8,64,512]{2,1,0:T(8,128)(2,1)} %get-tuple-element.17), channel_id=1, source_target_pairs={{32,0},{64,32},{96,64},{128,96},{160,128},{192,160},{224,192},{33,... | collective-permute-start | bytes 1572872 | tf_op jit(solution)/shard_map/ppermute | solution.py:386
  42.2 1.0 %copy-start.5 = (bf16[768,256]{1,0:T(8,128)(2,1)S(1)}, bf16[768,256]{1,0:T(8,128)(2,1)}, u32[]{:S(2)}) copy-start(bf16[768,256]{1,0:T(8,128)(2,1)} %get-tuple-element.19.forward_ref) | copy-start | bytes 1179652
  43.2 1.0 %copy-start.6 = (bf16[768,256]{1,0:T(8,128)(2,1)S(1)}, bf16[768,256]{1,0:T(8,128)(2,1)}, u32[]{:S(2)}) copy-start(bf16[768,256]{1,0:T(8,128)(2,1)} %get-tuple-element.20.absolute_ref) | copy-start | bytes 1179652
  44.2 0.9 %copy-start.7 = (bf16[384,256]{1,0:T(8,128)(2,1)S(1)}, bf16[384,256]{1,0:T(8,128)(2,1)}, u32[]{:S(2)}) copy-start(bf16[384,256]{1,0:T(8,128)(2,1)} %get-tuple-element.21.backward_ref) | copy-start | bytes 589828
  45.1 0.8 copy-start.8
  46.0 24.3 %copy-start.4 = (bf16[2,192,64]{2,1,0:T(8,128)(2,1)S(1)}, bf16[2,192,64]{2,1,0:T(8,128)(2,1)}, u32[]{:S(2)}) copy-start(bf16[2,192,64]{2,1,0:T(8,128)(2,1)} %get-tuple-element.25.weight_ref) | copy-start | bytes 147460
  70.3 1.6 %copy-start.1 = (f32[8,2,64,512]{3,2,1,0:T(8,128)S(1)}, f32[8,2,64,512]{3,2,1,0:T(8,128)}, u32[]{:S(2)}) copy-start(f32[8,2,64,512]{3,2,1,0:T(8,128)} %get-tuple-element.24.edge_ref) | copy-start | bytes 6291460
  71.9 14.8 %copy-start.9 = (f32[4096]{0:T(1024)S(1)}, f32[4096]{0:T(1024)}, u32[]{:S(2)}) copy-start(f32[4096]{0:T(1024)} %param.15) | copy-start | bytes 49156
  71.9 14.8 %copy-start.10 = (s32[8]{0:T(128)S(1)}, s32[8]{0:T(128)}, u32[]{:S(2)}) copy-start(s32[8]{0:T(128)} %param.14) | copy-start | bytes 100
  75.4 7.6 %collective-permute-start.3 = (f32[8,128]{1,0:T(8,128)S(1)}, f32[8,128]{1,0:T(8,128)S(1)}, u32[]{:S(2)}, u32[]{:S(2)}) collective-permute-start(f32[8,128]{1,0:T(8,128)S(1)} %get-tuple-element.29), channel_id=1, source_target_pairs={{0,32},{32,0},{64,96},{96,64},{128,160},{160,128},{192,224},{224,1... | collective-permute-start | bytes 12296 | tf_op jit(solution)/shard_map/ppermute | solution.py:404
  83.0 3.6 %collective-permute-start.4 = (f32[8,128]{1,0:T(8,128)S(1)}, f32[8,128]{1,0:T(8,128)S(1)}, u32[]{:S(2)}, u32[]{:S(2)}) collective-permute-start(f32[8,128]{1,0:T(8,128)S(1)} %add.13), channel_id=1, source_target_pairs={{0,64},{32,96},{64,0},{96,32},{128,192},{160,224},{192,128},{224,1... | collective-permute-start | bytes 12296 | tf_op jit(solution)/shard_map/ppermute | solution.py:404
  86.6 5.1 %collective-permute-start.5 = (f32[8,128]{1,0:T(8,128)S(1)}, f32[8,128]{1,0:T(8,128)S(1)}, u32[]{:S(2)}, u32[]{:S(2)}) collective-permute-start(f32[8,128]{1,0:T(8,128)S(1)} %add.14), channel_id=1, source_target_pairs={{0,128},{32,160},{64,192},{96,224},{128,0},{160,32},{192,64},{224,... | collective-permute-start | bytes 12296 | tf_op jit(solution)/shard_map/ppermute | solution.py:404

commit v3 on v2

v3 whole, which is shorter than its diff:
```python
import functools

import jax
import jax.numpy as jnp
from jax import lax
from jax.experimental import pallas as pl
from jax.experimental.pallas import tpu as pltpu
from jax.sharding import PartitionSpec as P

F32, BF16 = (jnp.float32, jnp.bfloat16)
SHARE = 8
MAIN_FLOPS = 0
EDGE_FLOPS = 5_000_000_000
MAIN_VMEM = 44 << 20
EDGE_VMEM = 8 << 20
UNITS = 7


def spread_columns(stack, columns):
    size = stack.shape[0] // 3
    where = lax.broadcasted_iota(jnp.int32, (size, columns), 1)
    right = pltpu.roll(stack[:size], 1, 1)
    left = pltpu.roll(stack[2 * size :], columns - 1, 1)
    right = jnp.where(where == 0, 0.0, right)
    left = jnp.where(where == columns - 1, 0.0, left)
    return right + stack[size : 2 * size] + left


def mul(a, b):
    return jnp.dot(a, b, preferred_element_type=F32)


def high_low(value):
    high = value.astype(BF16)
    return high, (value - high.astype(F32)).astype(BF16)


def edges_kernel(coeff_ref, last_ref, first_ref, held_ref, sems):
    specs, rows = coeff_ref.shape[:2]
    rows_of = ((rows - 1, last_ref), (0, first_ref))
    todo = [(k, s, h, ref) for k, (h, ref) in enumerate(rows_of) for s in range(specs)]
    reads = [
        pltpu.make_async_copy(coeff_ref.at[s, h], held_ref.at[k, s], sems.at[0, k, s])
        for k, s, h, _ in todo
    ]
    writes = [
        pltpu.make_async_copy(held_ref.at[k, s], ref.at[s], sems.at[1, k, s])
        for k, s, _, ref in todo
    ]
    for read in reads:
        read.start()
    for read, write in zip(reads, writes):
        read.wait()
        write.start()
    for write in writes:
        write.wait()


def edges_pass(coeffs):
    specs, rows, channels, columns = coeffs.shape
    edge = jax.ShapeDtypeStruct((specs, channels, columns), BF16)
    anywhere = pl.BlockSpec(memory_space=pl.ANY)
    return pl.pallas_call(
        edges_kernel,
        out_shape=(edge, edge),
        in_specs=[anywhere],
        out_specs=(anywhere, anywhere),
        scratch_shapes=[
            pltpu.VMEM((2, specs, channels, columns), BF16),
            pltpu.SemaphoreType.DMA((2, 2, specs)),
        ],
        cost_estimate=pl.CostEstimate(flops=0, bytes_accessed=4 << 20, transcendentals=0),
    )(coeffs)


def payload_kernel(where_ref, center_ref, radius_ref, status_ref, _, out_ref):
    high, low = high_low(center_ref[...])
    out_ref[0:2] = high
    out_ref[2:4] = low
    out_ref[4:6] = radius_ref[...].astype(BF16)
    out_ref[6:7] = status_ref[...].astype(F32).astype(BF16)


def payload_pass(where, center, radius, status, after):
    rows, channels, columns = center.shape
    part = channels * 2 // SHARE
    box = pl.BlockSpec((2, part, columns), lambda g, w: (w[0], w[1], 0))
    return pl.pallas_call(
        payload_kernel,
        out_shape=jax.ShapeDtypeStruct((UNITS, part, columns), BF16),
        grid_spec=pltpu.PrefetchScalarGridSpec(
            num_scalar_prefetch=1,
            grid=(1,),
            in_specs=[
                box,
                box,
                pl.BlockSpec((1, part, columns), lambda g, w: (w[2], w[1], 0)),
                pl.BlockSpec(memory_space=pl.ANY),
            ],
            out_specs=pl.BlockSpec((UNITS, part, columns), lambda g, w: (0, 0, 0)),
        ),
        cost_estimate=pl.CostEstimate(flops=0, bytes_accessed=1 << 20, transcendentals=0),
    )(where, center, radius, status, after)


def main_kernel(
    halo_ref,
    center_ref,
    radius_ref,
    status_ref,
    bands_ref,
    bias_ref,
    coeff_ref,
    out_ref,
    edge_ref,
    slope_edge_ref,
    total_ref,
    ch_ref,
    cl_ref,
    rh_ref,
    rl_ref,
    status_ext_ref,
    slope_ref,
    intercept_ref,
    linear_ref,
    pre_ref,
):
    rows, channels, columns = center_ref.shape
    c = channels
    part = halo_ref.shape[2]

    @pl.when(pl.program_id(0) == 0)
    def _():
        for side, base in ((0, 0), (1, rows + 2)):
            for y in range(c // part):
                piece = halo_ref.at[2 * y + side]
                for k in range(2):
                    at = pl.ds((base + k) * c + y * part, part)
                    ch_ref[at, :] = piece[k]
                    cl_ref[at, :] = piece[2 + k]
                    rh_ref[at, :] = piece[4 + k]
                    rl_ref[at, :] = jnp.zeros((part, columns), BF16)
                row = 0 if side == 0 else rows + 1
                status_ext_ref[pl.ds(row * c + y * part, part), :] = piece[6]
        for h in range(rows):
            at = pl.ds((h + 2) * c, c)
            ch_ref[at, :], cl_ref[at, :] = high_low(center_ref[h])
            rh_ref[at, :], rl_ref[at, :] = high_low(radius_ref[h])
            status_ext_ref[pl.ds((h + 1) * c, c), :] = status_ref[h].astype(F32).astype(BF16)
        pre_ref[pl.ds(0, c), :] = jnp.zeros((c, columns), BF16)
        pre_ref[pl.ds((rows + 1) * c, c), :] = jnp.zeros((c, columns), BF16)

        tall = jnp.broadcast_to(bias_ref[...], (8, c)).T[:, :1]
        tall = jnp.concatenate([tall, tall], axis=0)
        six = 6 * c

        @pl.loop(0, (rows + 2) // 2)
        def _(b):
            at = pl.ds(pl.multiple_of(b * 2 * c, 2 * c), 4 * c)
            here = pl.ds(pl.multiple_of(b * 2 * c, 2 * c), 2 * c)
            fh, fl, ah, al = (bands_ref[k * six : (k + 1) * six, :] for k in range(4))
            low = spread_columns(mul(fh, ch_ref[at, :]) + mul(fh, cl_ref[at, :]), columns)
            linear = low + tall
            center_out = linear + spread_columns(mul(fl, ch_ref[at, :]), columns)
            radius_out = spread_columns(
                mul(ah, rh_ref[at, :]) + mul(ah, rl_ref[at, :]) + mul(al, rh_ref[at, :]), columns
            )
            upper = center_out + radius_out
            lower = center_out - radius_out
            width = 2.0 * radius_out
            relaxed = jnp.minimum(jnp.maximum(upper, 0.0), width) / width
            status = status_ext_ref[here, :].astype(F32)
            open_ = status == 2.0
            slope = jnp.where(open_, relaxed, jnp.where(status == 1.0, 1.0, 0.0))
            slope_ref[here, :] = slope.astype(BF16)
            intercept = jnp.where(open_, -relaxed * jnp.minimum(lower, 0.0), 0.0)
            intercept_ref[here, :] = intercept.astype(BF16)
            linear_ref[here, :] = linear

        slope_edge_ref[0] = slope_ref[pl.ds(0, c), :]
        slope_edge_ref[1] = slope_ref[pl.ds((rows + 1) * c, c), :]

    total = jnp.zeros((8, columns), F32)
    for h in range(rows):
        at = pl.ds((h + 1) * c, c)
        coeff = coeff_ref[0, h]
        wide = coeff.astype(F32)
        pre = (wide * slope_ref[at, :].astype(F32)).astype(BF16)
        pre_ref[at, :] = pre
        terms = (
            jnp.minimum(wide, 0.0) * intercept_ref[at, :].astype(F32)
            + pre.astype(F32) * linear_ref[at, :]
        )
        total = total + jnp.sum(terms.reshape(c // 8, 8, columns), axis=0)

    for b in range(rows // 2):
        at = pl.ds(b * 2 * c, 4 * c)
        value = spread_columns(mul(bands_ref[24 * c :, :], pre_ref[at, :]), columns)
        for r in range(2):
            h = 2 * b + r
            row = value[r * c : (r + 1) * c]
            if h == 0 or h == rows - 1:
                edge_ref[0, 0 if h == 0 else 1] = row
            else:
                terms = jnp.abs(row) * radius_ref[h]
                total = total - jnp.sum(terms.reshape(c // 8, 8, columns), axis=0)
            out_ref[0, h] = row.astype(BF16)
    folded = total[:, :128]
    for k in range(1, columns // 128):
        folded = folded + total[:, k * 128 : (k + 1) * 128]
    total_ref[0] = folded


def main_pass(halo, center, radius, status, bands, bias, coeffs):
    specs, rows, channels, columns = coeffs.shape
    whole = lambda a: pl.BlockSpec(a.shape, lambda s, n=a.ndim: (0,) * n)
    ext = (rows + 4) * channels
    mid = (rows + 2) * channels
    return pl.pallas_call(
        main_kernel,
        grid=(specs,),
        out_shape=(
            jax.ShapeDtypeStruct(coeffs.shape, BF16),
            jax.ShapeDtypeStruct((specs, 2, channels, columns), F32),
            jax.ShapeDtypeStruct((2, channels, columns), BF16),
            jax.ShapeDtypeStruct((specs, 8, 128), F32),
        ),
        in_specs=[
            whole(a) for a in (halo, center, radius, status, bands, bias)
        ]
        + [pl.BlockSpec((1, rows, channels, columns), lambda s: (s, 0, 0, 0))],
        out_specs=(
            pl.BlockSpec((1, rows, channels, columns), lambda s: (s, 0, 0, 0)),
            pl.BlockSpec((1, 2, channels, columns), lambda s: (s, 0, 0, 0)),
            pl.BlockSpec((2, channels, columns), lambda s: (0, 0, 0)),
            pl.BlockSpec((1, 8, 128), lambda s: (s, 0, 0)),
        ),
        scratch_shapes=[pltpu.VMEM((ext, columns), BF16)] * 4
        + [
            pltpu.VMEM((mid, columns), BF16),
            pltpu.VMEM((mid, columns), BF16),
            pltpu.VMEM((mid, columns), BF16),
            pltpu.VMEM((mid, columns), F32),
            pltpu.VMEM((mid, columns), BF16),
        ],
        compiler_params=pltpu.CompilerParams(vmem_limit_bytes=MAIN_VMEM),
        cost_estimate=pl.CostEstimate(
            flops=MAIN_FLOPS, bytes_accessed=1024, transcendentals=0
        ),
    )(halo, center, radius, status, bands, bias, coeffs)


def edge_kernel(
    row,
    halo_ref,
    slope_ref,
    edge_ref,
    radius_ref,
    weight_ref,
    total_ref,
    _,
    out_ref,
    sum_ref,
    done_ref,
    sems,
):
    size, channels, columns = halo_ref.shape
    specs = out_ref.shape[0]
    step = pl.program_id(0)

    def store(s):
        return pltpu.make_async_copy(done_ref.at[s], out_ref.at[s, row], sems.at[s])

    for i in range(size):
        s = step * size + i
        pre = (halo_ref[i].astype(F32) * slope_ref[0].astype(F32)).astype(BF16)
        value = edge_ref[i, 0] + spread_columns(mul(weight_ref[0], pre), columns)
        done_ref[s] = value.astype(BF16)
        store(s).start()
        terms = jnp.abs(value) * radius_ref[0]
        terms = jnp.sum(terms.reshape(channels // 8, 8, columns), axis=0)
        folded = terms[:, :128]
        for m in range(1, columns // 128):
            folded = folded + terms[:, m * 128 : (m + 1) * 128]
        folded = total_ref[i] - folded
        if len(sum_ref.shape) == 3:
            sum_ref[i] = folded
        else:
            sum_ref[pl.ds(s, 1), :] = jnp.sum(folded, axis=0, keepdims=True)

    @pl.when(step == pl.num_programs(0) - 1)
    def _():
        for s in range(specs):
            store(s).wait()


def edge_pass(k, halo, slope, edge, radius, weight, total, out):
    specs, rows, channels, columns = out.shape
    size = 2
    row = 0 if k == 0 else rows - 1
    if k == 0:
        sums = jax.ShapeDtypeStruct(total.shape, F32)
        sums_spec = pl.BlockSpec((size, *total.shape[1:]), lambda g: (g, 0, 0))
    else:
        sums = jax.ShapeDtypeStruct((specs, 128), F32)
        sums_spec = pl.BlockSpec((specs, 128), lambda g: (0, 0))
    return pl.pallas_call(
        lambda *refs: edge_kernel(row, *refs),
        grid=(specs // size,),
        out_shape=(
            jax.ShapeDtypeStruct(out.shape, BF16),
            sums,
        ),
        in_specs=[
            pl.BlockSpec((size, channels, columns), lambda g: (g, 0, 0)),
            pl.BlockSpec((1, channels, columns), lambda g: (k, 0, 0)),
            pl.BlockSpec((size, 1, channels, columns), lambda g: (g, k, 0, 0)),
            pl.BlockSpec((1, channels, columns), lambda g: (row, 0, 0)),
            pl.BlockSpec((1, 3 * channels, channels), lambda g: (k, 0, 0)),
            pl.BlockSpec((size, *total.shape[1:]), lambda g: (g, 0, 0)),
            pl.BlockSpec(memory_space=pl.ANY),
        ],
        out_specs=(
            pl.BlockSpec(memory_space=pl.ANY),
            sums_spec,
        ),
        scratch_shapes=[
            pltpu.VMEM((specs, channels, columns), BF16),
            pltpu.SemaphoreType.DMA((specs,)),
        ],
        input_output_aliases={6: 0},
        compiler_params=pltpu.CompilerParams(vmem_limit_bytes=EDGE_VMEM),
        cost_estimate=pl.CostEstimate(
            flops=EDGE_FLOPS, bytes_accessed=1024, transcendentals=0
        ),
    )(halo, slope, edge, radius, weight, total, out)


def weight_kernel(weight_ref, bands_ref, ends_ref):
    c = weight_ref.shape[2]
    zero = jnp.zeros((c, c), F32)

    def place(base, blocks):
        three = jnp.concatenate(blocks, axis=1)
        bands_ref[pl.ds(base, c), :] = jnp.concatenate([three, zero], axis=1).astype(BF16)
        bands_ref[pl.ds(base + c, c), :] = jnp.concatenate([zero, three], axis=1).astype(BF16)

    for j in range(3):
        turned = [weight_ref[i, j].T for i in range(3)]
        for base, blocks in ((0, turned), (12 * c, [jnp.abs(w) for w in turned])):
            high = [w.astype(BF16).astype(F32) for w in blocks]
            place(base + j * 2 * c, high)
            place(base + (3 + j) * 2 * c, [w - h for w, h in zip(blocks, high)])
        place((12 + j) * 2 * c, [weight_ref[i, 2 - j] for i in (2, 1, 0)])
        for k, i in enumerate((2, 0)):
            ends_ref[k, pl.ds(j * c, c), :] = weight_ref[i, 2 - j].astype(BF16)


def weight_pass(weight):
    c = weight.shape[2]
    whole = lambda a: pl.BlockSpec(a.shape, lambda g, n=len(a.shape): (0,) * n)
    out = (
        jax.ShapeDtypeStruct((30 * c, 4 * c), BF16),
        jax.ShapeDtypeStruct((2, 3 * c, c), BF16),
    )
    return pl.pallas_call(
        weight_kernel,
        grid=(1,),
        out_shape=out,
        in_specs=[whole(weight)],
        out_specs=tuple(whole(a) for a in out),
    )(weight)


def per_device(
    center, radius, conv_weight, conv_bias, split_status, out_coeffs, spec_ids, spec_offsets
):
    count, groups = (lax.axis_size("rows"), lax.axis_size("specs"))
    rows, columns, channels = center.shape
    center, radius, status = (jnp.swapaxes(a, 1, 2) for a in (center, radius, split_status))
    coeffs = jnp.swapaxes(out_coeffs, 2, 3)

    lanes = groups // SHARE
    me = lax.axis_index("specs")
    core, y = (lax.rem(me, 2), me // (2 * lanes))
    up = core == 0
    where = jnp.stack(
        [jnp.where(up, rows // 2 - 1, 0), y, jnp.where(up, rows - 1, 0)]
    ).astype(jnp.int32)
    last, first = edges_pass(coeffs)
    before = lax.ppermute(last, "rows", [(i, i + 1) for i in range(count - 1)])
    box = payload_pass(where, center, radius, status, last)
    moves = []
    for r in range(count):
        for s in range(groups):
            other = r + (1 if s % 2 == 0 else -1)
            if 0 <= other < count:
                moves.append((r * groups + s, other * groups + s))
    box = lax.ppermute(box, ("rows", "specs"), moves)
    after = lax.ppermute(first, "rows", [(i + 1, i) for i in range(count - 1)])
    halo = lax.all_gather(
        box,
        "specs",
        axis_index_groups=[
            [(k * lanes + z) * 2 + e for k in range(SHARE // 2) for e in range(2)]
            for z in range(lanes)
        ],
    )

    bands, ends = weight_pass(conv_weight)
    out, edge, slope, total = main_pass(
        halo, center, radius, status, bands, conv_bias[None, :], coeffs
    )
    out, total = edge_pass(0, before, slope, edge, radius, ends, total, out)
    out, partial = edge_pass(1, after, slope, edge, radius, ends, total, out)

    others = [
        lax.ppermute(partial, "rows", [(i, i ^ step) for i in range(count)])
        for step in range(1, count)
    ]
    pairs = [partial, *others]
    while len(pairs) > 1:
        pairs = [a + b for a, b in zip(pairs[::2], pairs[1::2])]
    summed = jnp.sum(pairs[0], axis=1)
    pixels = rows * count * columns
    entries = spec_offsets.shape[0]
    onehot = spec_ids[:, None] == jnp.arange(entries, dtype=jnp.int32)[None, :]
    table_terms = jnp.sum(jnp.where(onehot, spec_offsets[None, :], 0.0), axis=1)
    bounds = summed / pixels + table_terms
    return (jnp.swapaxes(out, 2, 3), bounds)


def solution(mesh):
    in_specs = (
        P("rows", None, None),
        P("rows", None, None),
        P(),
        P(),
        P("rows", None, None),
        P("specs", "rows", None, None),
        P("specs"),
        P(),
    )
    out_specs = (P("specs", "rows", None, None), P("specs"))
    return jax.shard_map(
        per_device, mesh=mesh, in_specs=in_specs, out_specs=out_specs, check_vma=False
    )
```

time: 93 us -> 118 us (1.27)
  the two profiles are of different devices: /device:TPU:12 before, /device:TPU:56 now
where the time goes in v3:
time: 118 us; the launch traced here: 117 us
  starting transfers between devices  48.9 us (41%)
  Pallas kernels  31.1 us (26%)
  waiting for transfers between devices  19.3 us (16%)
  blocking collectives  14 us (12%)
  other arithmetic  1.51 us (1%)
  local copies, waits for them, and re-layouts  1.24 us (1%)
    ppermute x7, starting transfers between devices, per_device(): lax.ppermute(partial, 'rows', [(i, i ^ step) for i in range(count)])  36.9 us
    pallas_call x1, Pallas kernels, main_pass(): pl.pallas_call(main_kernel, grid=(specs,), out_shape=(jax.ShapeDtypeStruc...  16.3 us
    all_gather x1, blocking collectives, per_device(): lax.all_gather(box, 'specs', axis_index_groups=[[(k * lanes + z) * 2 + e...  14 us
    ppermute x1, waiting for transfers between devices, per_device(): box = lax.ppermute(box, ('rows', 'specs'), moves)  12.5 us
    ppermute x1, starting transfers between devices, per_device(): before = lax.ppermute(last, 'rows', [(i, i + 1) for i in range(count - 1)])  9.02 us
    pallas_call x2, Pallas kernels, edge_pass(): pl.pallas_call(lambda *refs: edge_kernel(row, *refs), grid=(specs // size...  7.38 us
    ppermute x7, waiting for transfers between devices, per_device(): lax.ppermute(partial, 'rows', [(i, i ^ step) for i in range(count)])  6.82 us
    pallas_call x1, Pallas kernels, weight_pass(): pl.pallas_call(weight_kernel, grid=(1,), out_shape=out, in_specs=[whole(w...  2.89 us
  transfers between devices with their start and end apart: 10, of which 3 were waited for; matrix products, arithmetic and copies ran while one was open for 1% of the time, Pallas kernels for 21%

profile of v3, /device:TPU:56, one launch (start us, length us, event | category | flops | bytes accessed | tf_op | source)
XLA Modules:
  0.0 116.9 jit_solution(6775196692777589705)
XLA Ops:
  0.6 0.0 copy-start
  0.6 0.0 copy-start.1
  0.7 0.0 copy-start.2
  0.7 2.3 %shard_map.95 = (bf16[8,64,512]{2,1,0:T(8,128)(2,1)}, bf16[8,64,512]{2,1,0:T(8,128)(2,1)}) custom-call(bf16[8,8,64,512]{3,2,1,0:T(8,128)(2,1)} %bitcast.20), custom_call_target="tpu_custom_call" | custom-call | bytes 4194304 | tf_op jit(solution)/shard_map/pallas_call | solution.py:63
  3.0 9.0 %collective-permute-start.2 = (bf16[8,64,512]{2,1,0:T(8,128)(2,1)}, bf16[8,64,512]{2,1,0:T(8,128)(2,1)}, u32[]{:S(2)}, u32[]{:S(2)}) collective-permute-start(bf16[8,64,512]{2,1,0:T(8,128)(2,1)} %get-tuple-element.15._), channel_id=1, source_target_pairs={{0,32},{32,64},{64,96},{96,128},{128,160},{160,192},{192,224},{1,3... | collective-permute-start | bytes 1572872 | tf_op jit(solution)/shard_map/ppermute | solution.py:391
  12.0 0.7 pad_add_fusion.where_ref
  12.7 2.2 %shard_map.96 = bf16[7,16,512]{2,1,0:T(8,128)(2,1)} custom-call(s32[3]{0:T(128)} %pad_add_fusion.where_ref, f32[8,64,512]{2,1,0:T(8,128)} %bitcast.10, f32[8,64,512]{2,1,0:T(8,128)} %bitcast.14, s32[8,64,512]{2,1,0:T(8,128)} %bitcast.12, bf16[8,64,512]{2,1,0:T(8,128)(2,1)} %get-tuple-element.15._), custom_call_target="tpu_custom_call" | custom-call | bytes 1048576 | tf_op jit(solution)/shard_map/pallas_call | solution.py:88
  14.9 1.7 %collective-permute-start.1 = (bf16[7,16,512]{2,1,0:T(8,128)(2,1)}, bf16[7,16,512]{2,1,0:T(8,128)(2,1)S(1)}, u32[]{:S(2)}, u32[]{:S(2)}) collective-permute-start(bf16[7,16,512]{2,1,0:T(8,128)(2,1)} %shard_map.96), channel_id=1, source_target_pairs={{0,32},{2,34},{4,36},{6,38},{8,40},{10,42},{12,44},{14,46},{16,48}... | collective-permute-start | bytes 344072 | tf_op jit(solution)/shard_map/ppermute | solution.py:399
  16.6 1.3 %collective-permute-start = (bf16[8,64,512]{2,1,0:T(8,128)(2,1)}, bf16[8,64,512]{2,1,0:T(8,128)(2,1)}, u32[]{:S(2)}, u32[]{:S(2)}) collective-permute-start(bf16[8,64,512]{2,1,0:T(8,128)(2,1)} %get-tuple-element.14), channel_id=1, source_target_pairs={{32,0},{64,32},{96,64},{128,96},{160,128},{192,160},{224,192},{33,... | collective-permute-start | bytes 1572872 | tf_op jit(solution)/shard_map/ppermute | solution.py:400
  17.9 2.9 %shard_map.97 = (bf16[1920,256]{1,0:T(8,128)(2,1)}, bf16[2,192,64]{2,1,0:T(8,128)(2,1)}) custom-call(f32[3,3,64,64]{3,2,1,0:T(8,128)} %weight_ref.1), custom_call_target="tpu_custom_call" | custom-call | tf_op jit(solution)/shard_map/pallas_call | solution.py:366
  20.8 12.5 %collective-permute-done.1 = bf16[7,16,512]{2,1,0:T(8,128)(2,1)S(1)} collective-permute-done((bf16[7,16,512]{2,1,0:T(8,128)(2,1)}, bf16[7,16,512]{2,1,0:T(8,128)(2,1)S(1)}, u32[]{:S(2)}, u32[]{:S(2)}) %collective-permute-start.1) | collective-permute-done | bytes 114720 | tf_op jit(solution)/shard_map/ppermute | solution.py:399
  33.3 14.0 %all-gather = bf16[56,16,512]{2,1,0:T(8,128)(2,1)S(1)} all-gather(bf16[7,16,512]{2,1,0:T(8,128)(2,1)S(1)} %collective-permute-done.1), channel_id=2, replica_groups={{0,1,8,9,16,17,24,25},{2,3,10,11,18,19,26,27},{4,5,12,13,20,21,28,29},{..., dimensions={0}, use_global_device_ids=true | all-gather | bytes 1032192 | tf_op jit(solution)/shard_map/all_gather | solution.py:401
  47.3 0.0 copy-start.3
  47.3 1.2 %copy-done.3 = bf16[1920,256]{1,0:T(8,128)(2,1)S(1)} copy-done((bf16[1920,256]{1,0:T(8,128)(2,1)S(1)}, bf16[1920,256]{1,0:T(8,128)(2,1)}, u32[]{:S(2)}) %copy-start.3) | copy-done | bytes 983064
  48.5 16.3 %shard_map.98 = (bf16[8,8,64,512]{3,2,1,0:T(8,128)(2,1)}, f32[8,2,64,512]{3,2,1,0:T(8,128)S(1)}, bf16[2,64,512]{2,1,0:T(8,128)(2,1)S(1)}, f32[8,8,128]{2,1,0:T(8,128)S(1)}) custom-call(bf16[8,7,16,512]{3,2,1,0:T(8,128)(2,1)S(1)} %bitcast.18, f32[8,64,512]{2,1,0:T(8,128)S(1)} %bitcast.11, f32[8,64,512]{2,1,0:T(8,128)S(1)} %bitcast.15, ...), custom_call_target="tpu_custom_call" | custom-call | bytes 1024 | tf_op jit(solution)/shard_map/pallas_call | solution.py:219
  64.9 0.0 collective-permute-done.2.refs_0_
  64.9 3.7 %shard_map.99 = (bf16[8,8,64,512]{3,2,1,0:T(8,128)(2,1)}, f32[8,8,128]{2,1,0:T(8,128)S(1)}) custom-call(bf16[8,64,512]{2,1,0:T(8,128)(2,1)} %collective-permute-done.2.refs_0_, bf16[2,64,512]{2,1,0:T(8,128)(2,1)S(1)} %get-tuple-element.17.refs_1_, f32[8,2,64,512]{3,2,1,0:T(8,128)S(1)} %get-tuple-element.18.refs_2_, ...), custom_call_target="tpu_custom_call", output_to_operand_aliasing={{0}: (6, {})} | custom-call | flops 5000000000 | bytes 1024 | tf_op jit(solution)/shard_map/pallas_call | solution.py:307
  68.6 0.0 copy-start.6
  68.6 0.0 copy-start.7
  68.6 3.7 %shard_map.100 = (bf16[8,8,64,512]{3,2,1,0:T(8,128)(2,1)}, f32[8,128]{1,0:T(8,128)S(1)}) custom-call(bf16[8,64,512]{2,1,0:T(8,128)(2,1)} %collective-permute-done.refs_0_, bf16[2,64,512]{2,1,0:T(8,128)(2,1)S(1)} %get-tuple-element.17.refs_1_, f32[8,2,64,512]{3,2,1,0:T(8,128)S(1)} %get-tuple-element.18.refs_2_, ...), custom_call_target="tpu_custom_call", output_to_operand_aliasing={{0}: (6, {})} | custom-call | flops 5000000000 | bytes 1024 | tf_op jit(solution)/shard_map/pallas_call | solution.py:307
  72.3 20.2 %collective-permute-start.8 = (f32[8,128]{1,0:T(8,128)S(1)}, f32[8,128]{1,0:T(8,128)S(1)}, u32[]{:S(2)}, u32[]{:S(2)}) collective-permute-start(f32[8,128]{1,0:T(8,128)S(1)} %get-tuple-element.25), channel_id=1, source_target_pairs={{0,192},{32,224},{64,128},{96,160},{128,64},{160,96},{192,0},{224,... | collective-permute-start | bytes 12296 | tf_op jit(solution)/shard_map/ppermute | solution.py:418
  92.5 5.8 %collective-permute-start.9 = (f32[8,128]{1,0:T(8,128)S(1)}, f32[8,128]{1,0:T(8,128)S(1)}, u32[]{:S(2)}, u32[]{:S(2)}) collective-permute-start(f32[8,128]{1,0:T(8,128)S(1)} %get-tuple-element.25), channel_id=1, source_target_pairs={{0,224},{32,192},{64,160},{96,128},{128,96},{160,64},{192,32},{224... | collective-permute-start | bytes 12296 | tf_op jit(solution)/shard_map/ppermute | solution.py:418
  98.4 0.0 collective-permute-start.6
  98.4 3.4 %collective-permute-start.7 = (f32[8,128]{1,0:T(8,128)S(1)}, f32[8,128]{1,0:T(8,128)S(1)}, u32[]{:S(2)}, u32[]{:S(2)}) collective-permute-start(f32[8,128]{1,0:T(8,128)S(1)} %get-tuple-element.25), channel_id=1, source_target_pairs={{0,160},{32,128},{64,224},{96,192},{128,32},{160,0},{192,96},{224,... | collective-permute-start | bytes 12296 | tf_op jit(solution)/shard_map/ppermute | solution.py:418
  101.8 0.6 collective-permute-start.4
  102.4 6.4 %collective-permute-start.5 = (f32[8,128]{1,0:T(8,128)S(1)}, f32[8,128]{1,0:T(8,128)S(1)}, u32[]{:S(2)}, u32[]{:S(2)}) collective-permute-start(f32[8,128]{1,0:T(8,128)S(1)} %get-tuple-element.25), channel_id=1, source_target_pairs={{0,96},{32,64},{64,32},{96,0},{128,224},{160,192},{192,160},{224,1... | collective-permute-start | bytes 12296 | tf_op jit(solution)/shard_map/ppermute | solution.py:418
  108.7 0.5 collective-permute-start.3
  109.2 0.2 select_reduce_fusion
  109.4 1.3 %collective-permute-done.5 = f32[8,128]{1,0:T(8,128)S(1)} collective-permute-done((f32[8,128]{1,0:T(8,128)S(1)}, f32[8,128]{1,0:T(8,128)S(1)}, u32[]{:S(2)}, u32[]{:S(2)}) %collective-permute-start.5) | collective-permute-done | bytes 4128 | tf_op jit(solution)/shard_map/ppermute | solution.py:418
  110.8 5.5 %collective-permute-done.3 = f32[8,128]{1,0:T(8,128)S(1)} collective-permute-done((f32[8,128]{1,0:T(8,128)S(1)}, f32[8,128]{1,0:T(8,128)S(1)}, u32[]{:S(2)}, u32[]{:S(2)}) %collective-permute-start.3) | collective-permute-done | bytes 4128 | tf_op jit(solution)/shard_map/ppermute | solution.py:418
  116.2 0.1 add_reduce_fusion
  116.4 0.5 multiply_add_fusion
  (15 shorter events, 0.0 us)
Async XLA Ops:
  0.6 46.7 %copy-start = (f32[8,512,64]{1,2,0:T(8,128)S(1)}, f32[8,512,64]{1,2,0:T(8,128)}, u32[]{:S(2)}) copy-start(f32[8,512,64]{1,2,0:T(8,128)} %param.8) | copy-start | bytes 3145732
  0.6 46.7 %copy-start.1 = (s32[8,512,64]{1,2,0:T(8,128)S(1)}, s32[8,512,64]{1,2,0:T(8,128)}, u32[]{:S(2)}) copy-start(s32[8,512,64]{1,2,0:T(8,128)} %param.12) | copy-start | bytes 3145732
  0.7 46.6 %copy-start.2 = (f32[8,512,64]{1,2,0:T(8,128)S(1)}, f32[8,512,64]{1,2,0:T(8,128)}, u32[]{:S(2)}) copy-start(f32[8,512,64]{1,2,0:T(8,128)} %param.9) | copy-start | bytes 3145732
  0.7 46.6 %copy-start.4 = (f32[64]{0:T(128)S(1)}, f32[64]{0:T(128)}, u32[]{:S(2)}) copy-start(f32[64]{0:T(128)} %param.11) | copy-start | bytes 772
  3.0 61.9 %collective-permute-start.2 = (bf16[8,64,512]{2,1,0:T(8,128)(2,1)}, bf16[8,64,512]{2,1,0:T(8,128)(2,1)}, u32[]{:S(2)}, u32[]{:S(2)}) collective-permute-start(bf16[8,64,512]{2,1,0:T(8,128)(2,1)} %get-tuple-element.15._), channel_id=1, source_target_pairs={{0,32},{32,64},{64,96},{96,128},{128,160},{160,192},{192,224},{1,3... | collective-permute-start | bytes 1572872 | tf_op jit(solution)/shard_map/ppermute | solution.py:391
  14.9 18.4 %collective-permute-start.1 = (bf16[7,16,512]{2,1,0:T(8,128)(2,1)}, bf16[7,16,512]{2,1,0:T(8,128)(2,1)S(1)}, u32[]{:S(2)}, u32[]{:S(2)}) collective-permute-start(bf16[7,16,512]{2,1,0:T(8,128)(2,1)} %shard_map.96), channel_id=1, source_target_pairs={{0,32},{2,34},{4,36},{6,38},{8,40},{10,42},{12,44},{14,46},{16,48}... | collective-permute-start | bytes 344072 | tf_op jit(solution)/shard_map/ppermute | solution.py:399
  16.6 52.0 %collective-permute-start = (bf16[8,64,512]{2,1,0:T(8,128)(2,1)}, bf16[8,64,512]{2,1,0:T(8,128)(2,1)}, u32[]{:S(2)}, u32[]{:S(2)}) collective-permute-start(bf16[8,64,512]{2,1,0:T(8,128)(2,1)} %get-tuple-element.14), channel_id=1, source_target_pairs={{32,0},{64,32},{96,64},{128,96},{160,128},{192,160},{224,192},{33,... | collective-permute-start | bytes 1572872 | tf_op jit(solution)/shard_map/ppermute | solution.py:400
  47.3 1.2 %copy-start.3 = (bf16[1920,256]{1,0:T(8,128)(2,1)S(1)}, bf16[1920,256]{1,0:T(8,128)(2,1)}, u32[]{:S(2)}) copy-start(bf16[1920,256]{1,0:T(8,128)(2,1)} %get-tuple-element.16.bands_ref) | copy-start | bytes 2949124
  48.5 16.3 %copy-start.5 = (bf16[2,192,64]{2,1,0:T(8,128)(2,1)S(1)}, bf16[2,192,64]{2,1,0:T(8,128)(2,1)}, u32[]{:S(2)}) copy-start(bf16[2,192,64]{2,1,0:T(8,128)(2,1)} %get-tuple-element.19.refs_4_) | copy-start | bytes 147460
  68.6 40.6 %copy-start.6 = (f32[4096]{0:T(1024)S(1)}, f32[4096]{0:T(1024)}, u32[]{:S(2)}) copy-start(f32[4096]{0:T(1024)} %param.15) | copy-start | bytes 49156
  68.6 40.6 %copy-start.7 = (s32[8]{0:T(128)S(1)}, s32[8]{0:T(128)}, u32[]{:S(2)}) copy-start(s32[8]{0:T(128)} %param.14) | copy-start | bytes 100
  72.3 30.1 %collective-permute-start.8 = (f32[8,128]{1,0:T(8,128)S(1)}, f32[8,128]{1,0:T(8,128)S(1)}, u32[]{:S(2)}, u32[]{:S(2)}) collective-permute-start(f32[8,128]{1,0:T(8,128)S(1)} %get-tuple-element.25), channel_id=1, source_target_pairs={{0,192},{32,224},{64,128},{96,160},{128,64},{160,96},{192,0},{224,... | collective-permute-start | bytes 12296 | tf_op jit(solution)/shard_map/ppermute | solution.py:418
  92.5 16.2 %collective-permute-start.9 = (f32[8,128]{1,0:T(8,128)S(1)}, f32[8,128]{1,0:T(8,128)S(1)}, u32[]{:S(2)}, u32[]{:S(2)}) collective-permute-start(f32[8,128]{1,0:T(8,128)S(1)} %get-tuple-element.25), channel_id=1, source_target_pairs={{0,224},{32,192},{64,160},{96,128},{128,96},{160,64},{192,32},{224... | collective-permute-start | bytes 12296 | tf_op jit(solution)/shard_map/ppermute | solution.py:418
  98.4 11.1 %collective-permute-start.6 = (f32[8,128]{1,0:T(8,128)S(1)}, f32[8,128]{1,0:T(8,128)S(1)}, u32[]{:S(2)}, u32[]{:S(2)}) collective-permute-start(f32[8,128]{1,0:T(8,128)S(1)} %get-tuple-element.25), channel_id=1, source_target_pairs={{0,128},{32,160},{64,192},{96,224},{128,0},{160,32},{192,64},{224,... | collective-permute-start | bytes 12296 | tf_op jit(solution)/shard_map/ppermute | solution.py:418
  98.4 11.1 %collective-permute-start.7 = (f32[8,128]{1,0:T(8,128)S(1)}, f32[8,128]{1,0:T(8,128)S(1)}, u32[]{:S(2)}, u32[]{:S(2)}) collective-permute-start(f32[8,128]{1,0:T(8,128)S(1)} %get-tuple-element.25), channel_id=1, source_target_pairs={{0,160},{32,128},{64,224},{96,192},{128,32},{160,0},{192,96},{224,... | collective-permute-start | bytes 12296 | tf_op jit(solution)/shard_map/ppermute | solution.py:418
  101.8 7.6 %collective-permute-start.4 = (f32[8,128]{1,0:T(8,128)S(1)}, f32[8,128]{1,0:T(8,128)S(1)}, u32[]{:S(2)}, u32[]{:S(2)}) collective-permute-start(f32[8,128]{1,0:T(8,128)S(1)} %get-tuple-element.25), channel_id=1, source_target_pairs={{0,64},{32,96},{64,0},{96,32},{128,192},{160,224},{192,128},{224,1... | collective-permute-start | bytes 12296 | tf_op jit(solution)/shard_map/ppermute | solution.py:418
  102.4 8.4 %collective-permute-start.5 = (f32[8,128]{1,0:T(8,128)S(1)}, f32[8,128]{1,0:T(8,128)S(1)}, u32[]{:S(2)}, u32[]{:S(2)}) collective-permute-start(f32[8,128]{1,0:T(8,128)S(1)} %get-tuple-element.25), channel_id=1, source_target_pairs={{0,96},{32,64},{64,32},{96,0},{128,224},{160,192},{192,160},{224,1... | collective-permute-start | bytes 12296 | tf_op jit(solution)/shard_map/ppermute | solution.py:418
  108.7 7.5 %collective-permute-start.3 = (f32[8,128]{1,0:T(8,128)S(1)}, f32[8,128]{1,0:T(8,128)S(1)}, u32[]{:S(2)}, u32[]{:S(2)}) collective-permute-start(f32[8,128]{1,0:T(8,128)S(1)} %get-tuple-element.25), channel_id=1, source_target_pairs={{0,32},{32,0},{64,96},{96,64},{128,160},{160,128},{192,224},{224,1... | collective-permute-start | bytes 12296 | tf_op jit(solution)/shard_map/ppermute | solution.py:418

commit v4 on v3

--- a/solution.py
+++ b/solution.py
@@ -1,3 +1,5 @@
+import functools
+
 import functools
 
 import jax
@@ -9,11 +11,11 @@
 
 F32, BF16 = (jnp.float32, jnp.bfloat16)
 SHARE = 8
-MAIN_FLOPS = 0
-EDGE_FLOPS = 5_000_000_000
+MAIN_FLOPS = 20_000_000_000
+EDGE_FLOPS = 2_000_000_000
 MAIN_VMEM = 44 << 20
 EDGE_VMEM = 8 << 20
-UNITS = 7
+UNITS = 5
 
 
 def spread_columns(stack, columns):
@@ -35,10 +37,40 @@
     return high, (value - high.astype(F32)).astype(BF16)
 
 
-def edges_kernel(coeff_ref, last_ref, first_ref, held_ref, sems):
+def payload_kernel(where_ref, center_ref, radius_ref, status_ref, out_ref):
+    out_ref[0:2] = center_ref[...].astype(BF16)
+    out_ref[2:4] = radius_ref[...].astype(BF16)
+    out_ref[4:5] = status_ref[...].astype(F32).astype(BF16)
+
+
+def payload_pass(where, center, radius, status):
+    rows, channels, columns = center.shape
+    part = channels * 2 // SHARE
+    box = pl.BlockSpec((2, part, columns), lambda g, w: (w[0], w[1], 0))
+    return pl.pallas_call(
+        payload_kernel,
+        out_shape=jax.ShapeDtypeStruct((UNITS, part, columns), BF16),
+        grid_spec=pltpu.PrefetchScalarGridSpec(
+            num_scalar_prefetch=1,
+            grid=(1,),
+            in_specs=[
+                box,
+                box,
+                pl.BlockSpec((1, part, columns), lambda g, w: (w[2], w[1], 0)),
+            ],
+            out_specs=pl.BlockSpec((UNITS, part, columns), lambda g, w: (0, 0, 0)),
+        ),
+        cost_estimate=pl.CostEstimate(flops=0, bytes_accessed=1 << 20, transcendentals=0),
+    )(where, center, radius, status)
+
+
+def send_kernel(sites_ref, coeff_ref, _, first_ref, second_ref, held_ref, sems):
     specs, rows = coeff_ref.shape[:2]
-    rows_of = ((rows - 1, last_ref), (0, first_ref))
-    todo = [(k, s, h, ref) for k, (h, ref) in enumerate(rows_of) for s in range(specs)]
+    todo = [
+        (k, s, sites_ref[3 + k] * (rows - 1), ref)
+        for k, ref in enumerate((first_ref, second_ref))
+        for s in range(specs)
+    ]
     reads = [
         pltpu.make_async_copy(coeff_ref.at[s, h], held_ref.at[k, s], sems.at[0, k, s])
         for k, s, h, _ in todo
@@ -56,51 +88,25 @@
         write.wait()
 
 
-def edges_pass(coeffs):
+def send_pass(sites, coeffs, after):
     specs, rows, channels, columns = coeffs.shape
     edge = jax.ShapeDtypeStruct((specs, channels, columns), BF16)
     anywhere = pl.BlockSpec(memory_space=pl.ANY)
     return pl.pallas_call(
-        edges_kernel,
+        send_kernel,
         out_shape=(edge, edge),
-        in_specs=[anywhere],
-        out_specs=(anywhere, anywhere),
-        scratch_shapes=[
-            pltpu.VMEM((2, specs, channels, columns), BF16),
-            pltpu.SemaphoreType.DMA((2, 2, specs)),
-        ],
-        cost_estimate=pl.CostEstimate(flops=0, bytes_accessed=4 << 20, transcendentals=0),
-    )(coeffs)
-
-
-def payload_kernel(where_ref, center_ref, radius_ref, status_ref, _, out_ref):
-    high, low = high_low(center_ref[...])
-    out_ref[0:2] = high
-    out_ref[2:4] = low
-    out_ref[4:6] = radius_ref[...].astype(BF16)
-    out_ref[6:7] = status_ref[...].astype(F32).astype(BF16)
-
-
-def payload_pass(where, center, radius, status, after):
-    rows, channels, columns = center.shape
-    part = channels * 2 // SHARE
-    box = pl.BlockSpec((2, part, columns), lambda g, w: (w[0], w[1], 0))
-    return pl.pallas_call(
-        payload_kernel,
-        out_shape=jax.ShapeDtypeStruct((UNITS, part, columns), BF16),
         grid_spec=pltpu.PrefetchScalarGridSpec(
             num_scalar_prefetch=1,
             grid=(1,),
-            in_specs=[
-                box,
-                box,
-                pl.BlockSpec((1, part, columns), lambda g, w: (w[2], w[1], 0)),
-                pl.BlockSpec(memory_space=pl.ANY),
+            in_specs=[anywhere, anywhere],
+            out_specs=(anywhere, anywhere),
+            scratch_shapes=[
+                pltpu.VMEM((2, specs, channels, columns), BF16),
+                pltpu.SemaphoreType.DMA((2, 2, specs)),
             ],
-            out_specs=pl.BlockSpec((UNITS, part, columns), lambda g, w: (0, 0, 0)),
-        ),
-        cost_estimate=pl.CostEstimate(flops=0, bytes_accessed=1 << 20, transcendentals=0),
-    )(where, center, radius, status, after)
+        ),
+        cost_estimate=pl.CostEstimate(flops=0, bytes_accessed=4 << 20, transcendentals=0),
+    )(sites, coeffs, after)
 
 
 def main_kernel(
@@ -137,11 +143,11 @@
                 for k in range(2):
                     at = pl.ds((base + k) * c + y * part, part)
                     ch_ref[at, :] = piece[k]
-                    cl_ref[at, :] = piece[2 + k]
-                    rh_ref[at, :] = piece[4 + k]
+                    rh_ref[at, :] = piece[2 + k]
+                    cl_ref[at, :] = jnp.zeros((part, columns), BF16)
                     rl_ref[at, :] = jnp.zeros((part, columns), BF16)
                 row = 0 if side == 0 else rows + 1
-                status_ext_ref[pl.ds(row * c + y * part, part), :] = piece[6]
+                status_ext_ref[pl.ds(row * c + y * part, part), :] = piece[4]
         for h in range(rows):
             at = pl.ds((h + 2) * c, c)
             ch_ref[at, :], cl_ref[at, :] = high_low(center_ref[h])
@@ -245,13 +251,14 @@
         ],
         compiler_params=pltpu.CompilerParams(vmem_limit_bytes=MAIN_VMEM),
         cost_estimate=pl.CostEstimate(
-            flops=MAIN_FLOPS, bytes_accessed=1024, transcendentals=0
+            flops=MAIN_FLOPS, bytes_accessed=16 << 20, transcendentals=0
         ),
     )(halo, center, radius, status, bands, bias, coeffs)
 
 
 def edge_kernel(
-    row,
+    slot,
+    sites_ref,
     halo_ref,
     slope_ref,
     edge_ref,
@@ -264,17 +271,15 @@
     done_ref,
     sems,
 ):
-    size, channels, columns = halo_ref.shape
-    specs = out_ref.shape[0]
-    step = pl.program_id(0)
+    specs, channels, columns = halo_ref.shape
+    row = sites_ref[slot] * (out_ref.shape[1] - 1)
 
     def store(s):
         return pltpu.make_async_copy(done_ref.at[s], out_ref.at[s, row], sems.at[s])
 
-    for i in range(size):
-        s = step * size + i
-        pre = (halo_ref[i].astype(F32) * slope_ref[0].astype(F32)).astype(BF16)
-        value = edge_ref[i, 0] + spread_columns(mul(weight_ref[0], pre), columns)
+    for s in range(specs):
+        pre = (halo_ref[s].astype(F32) * slope_ref[0].astype(F32)).astype(BF16)
+        value = edge_ref[s, 0] + spread_columns(mul(weight_ref[0], pre), columns)
         done_ref[s] = value.astype(BF16)
         store(s).start()
         terms = jnp.abs(value) * radius_ref[0]
@@ -282,58 +287,52 @@
         folded = terms[:, :128]
         for m in range(1, columns // 128):
             folded = folded + terms[:, m * 128 : (m + 1) * 128]
-        folded = total_ref[i] - folded
+        folded = total_ref[s] - folded
         if len(sum_ref.shape) == 3:
-            sum_ref[i] = folded
+            sum_ref[s] = folded
         else:
-            sum_ref[pl.ds(s, 1), :] = jnp.sum(folded, axis=0, keepdims=True)
-
-    @pl.when(step == pl.num_programs(0) - 1)
-    def _():
-        for s in range(specs):
-            store(s).wait()
-
-
-def edge_pass(k, halo, slope, edge, radius, weight, total, out):
+            sum_ref[s : s + 1, :] = jnp.sum(folded, axis=0, keepdims=True)
+    for s in range(specs):
+        store(s).wait()
+
+
+def edge_pass(slot, sites, halo, slope, edge, radius, weight, total, out):
     specs, rows, channels, columns = out.shape
-    size = 2
-    row = 0 if k == 0 else rows - 1
-    if k == 0:
-        sums = jax.ShapeDtypeStruct(total.shape, F32)
-        sums_spec = pl.BlockSpec((size, *total.shape[1:]), lambda g: (g, 0, 0))
-    else:
-        sums = jax.ShapeDtypeStruct((specs, 128), F32)
-        sums_spec = pl.BlockSpec((specs, 128), lambda g: (0, 0))
+    last = slot == 4
+    sums = (specs, 128) if last else total.shape
     return pl.pallas_call(
-        lambda *refs: edge_kernel(row, *refs),
-        grid=(specs // size,),
+        functools.partial(edge_kernel, slot),
         out_shape=(
             jax.ShapeDtypeStruct(out.shape, BF16),
-            sums,
-        ),
-        in_specs=[
-            pl.BlockSpec((size, channels, columns), lambda g: (g, 0, 0)),
-            pl.BlockSpec((1, channels, columns), lambda g: (k, 0, 0)),
-            pl.BlockSpec((size, 1, channels, columns), lambda g: (g, k, 0, 0)),
-            pl.BlockSpec((1, channels, columns), lambda g: (row, 0, 0)),
-            pl.BlockSpec((1, 3 * channels, channels), lambda g: (k, 0, 0)),
-            pl.BlockSpec((size, *total.shape[1:]), lambda g: (g, 0, 0)),
-            pl.BlockSpec(memory_space=pl.ANY),
-        ],
-        out_specs=(
-            pl.BlockSpec(memory_space=pl.ANY),
-            sums_spec,
-        ),
-        scratch_shapes=[
-            pltpu.VMEM((specs, channels, columns), BF16),
-            pltpu.SemaphoreType.DMA((specs,)),
-        ],
-        input_output_aliases={6: 0},
+            jax.ShapeDtypeStruct(sums, F32),
+        ),
+        grid_spec=pltpu.PrefetchScalarGridSpec(
+            num_scalar_prefetch=1,
+            grid=(1,),
+            in_specs=[
+                pl.BlockSpec(halo.shape, lambda g, e: (0, 0, 0)),
+                pl.BlockSpec((1, channels, columns), lambda g, e: (e[slot], 0, 0)),
+                pl.BlockSpec((specs, 1, channels, columns), lambda g, e: (0, e[slot], 0, 0)),
+                pl.BlockSpec((1, channels, columns), lambda g, e: (e[slot] * (rows - 1), 0, 0)),
+                pl.BlockSpec((1, 3 * channels, channels), lambda g, e: (e[slot], 0, 0)),
+                pl.BlockSpec(total.shape, lambda g, e: (0, 0, 0)),
+                pl.BlockSpec(memory_space=pl.ANY),
+            ],
+            out_specs=(
+                pl.BlockSpec(memory_space=pl.ANY),
+                pl.BlockSpec(sums, lambda g, e: (0,) * len(sums)),
+            ),
+            scratch_shapes=[
+                pltpu.VMEM((specs, channels, columns), BF16),
+                pltpu.SemaphoreType.DMA((specs,)),
+            ],
+        ),
+        input_output_aliases={7: 0},
         compiler_params=pltpu.CompilerParams(vmem_limit_bytes=EDGE_VMEM),
         cost_estimate=pl.CostEstimate(
-            flops=EDGE_FLOPS, bytes_accessed=1024, transcendentals=0
-        ),
-    )(halo, slope, edge, radius, weight, total, out)
+            flops=EDGE_FLOPS, bytes_accessed=1 << 20, transcendentals=0
+        ),
+    )(sites, halo, slope, edge, radius, weight, total, out)
 
 
 def weight_kernel(weight_ref, bands_ref, ends_ref):
@@ -384,20 +383,22 @@
     me = lax.axis_index("specs")
     core, y = (lax.rem(me, 2), me // (2 * lanes))
     up = core == 0
-    where = jnp.stack(
-        [jnp.where(up, rows // 2 - 1, 0), y, jnp.where(up, rows - 1, 0)]
+    even = 1 - lax.rem(lax.axis_index("rows"), 2)
+    sites = jnp.stack(
+        [jnp.where(up, rows // 2 - 1, 0), y, jnp.where(up, rows - 1, 0), even, 1 - even]
     ).astype(jnp.int32)
-    last, first = edges_pass(coeffs)
-    before = lax.ppermute(last, "rows", [(i, i + 1) for i in range(count - 1)])
-    box = payload_pass(where, center, radius, status, last)
+    mine = payload_pass(sites, center, radius, status)
     moves = []
     for r in range(count):
         for s in range(groups):
             other = r + (1 if s % 2 == 0 else -1)
             if 0 <= other < count:
                 moves.append((r * groups + s, other * groups + s))
-    box = lax.ppermute(box, ("rows", "specs"), moves)
-    after = lax.ppermute(first, "rows", [(i + 1, i) for i in range(count - 1)])
+    box = lax.ppermute(mine, ("rows", "specs"), moves)
+    one, two = send_pass(sites, coeffs, mine)
+    pairs = [(i, i + 1) for i in range(count - 1)]
+    one = lax.ppermute(one, "rows", [m for p in pairs[::2] for m in (p, p[::-1])])
+    two = lax.ppermute(two, "rows", [m for p in pairs[1::2] for m in (p, p[::-1])])
     halo = lax.all_gather(
         box,
         "specs",
@@ -411,17 +412,14 @@
     out, edge, slope, total = main_pass(
         halo, center, radius, status, bands, conv_bias[None, :], coeffs
     )
-    out, total = edge_pass(0, before, slope, edge, radius, ends, total, out)
-    out, partial = edge_pass(1, after, slope, edge, radius, ends, total, out)
-
-    others = [
-        lax.ppermute(partial, "rows", [(i, i ^ step) for i in range(count)])
-        for step in range(1, count)
-    ]
-    pairs = [partial, *others]
-    while len(pairs) > 1:
-        pairs = [a + b for a, b in zip(pairs[::2], pairs[1::2])]
-    summed = jnp.sum(pairs[0], axis=1)
+    out, total = edge_pass(3, sites, one, slope, edge, radius, ends, total, out)
+    out, partial = edge_pass(4, sites, two, slope, edge, radius, ends, total, out)
+
+    step = 1
+    while step < count:
+        partial = partial + lax.ppermute(partial, "rows", [(i, i ^ step) for i in range(count)])
+        step *= 2
+    summed = jnp.sum(partial, axis=1)
     pixels = rows * count * columns
     entries = spec_offsets.shape[0]
     onehot = spec_ids[:, None] == jnp.arange(entries, dtype=jnp.int32)[None, :]

time: 118 us -> 93 us (0.79)
  starting transfers between devices: 48.9 us -> 21.5 us
  waiting for transfers between devices: 19.3 us -> 23.2 us
    ppermute x7 -> x3, starting transfers between devices: 36.9 us -> 4.44 us  [per_device(): lax.ppermute(partial, 'rows', [(i, i ^ step) for i in range(count)])]
    ppermute x3, starting transfers between devices: 12 us -> 17.1 us  [the longest x1 8.19 us: per_device(): box = lax.ppermute(mine, ('rows', 'specs'), moves)]
    ppermute x7 -> x3, waiting for transfers between devices: 6.82 us -> 11.7 us  [per_device(): lax.ppermute(partial, 'rows', [(i, i ^ step) for i in range(count)])]
  transfers between devices with their start and end apart: 10 -> 6, of which waited for: 3 -> 4; matrix products, arithmetic and copies ran while one was open for 1% -> 0% of each run, Pallas kernels for 21% -> 27%
where the time goes in v4:
time: 93 us; the launch traced here: 92.1 us
  Pallas kernels  30.7 us (33%)
  waiting for transfers between devices  23.2 us (25%)
  starting transfers between devices  21.5 us (23%)
  blocking collectives  13.2 us (14%)
  local copies, waits for them, and re-layouts  1.86 us (2%)
    pallas_call x1, Pallas kernels, main_pass(): pl.pallas_call(main_kernel, grid=(specs,), out_shape=(jax.ShapeDtypeStruc...  16.4 us
    all_gather x1, blocking collectives, per_device(): lax.all_gather(box, 'specs', axis_index_groups=[[(k * lanes + z) * 2 + e...  13.2 us
    ppermute x3, waiting for transfers between devices, per_device(): lax.ppermute(partial, 'rows', [(i, i ^ step) for i in range(count)])  11.7 us
    ppermute x1, waiting for transfers between devices, per_device(): lax.ppermute(one, 'rows', [m for p in pairs[::2] for m in (p, p[::-1])])  11.6 us
    ppermute x1, starting transfers between devices, per_device(): box = lax.ppermute(mine, ('rows', 'specs'), moves)  8.19 us
    ppermute x1, starting transfers between devices, per_device(): lax.ppermute(one, 'rows', [m for p in pairs[::2] for m in (p, p[::-1])])  7.39 us
    pallas_call x2, Pallas kernels, edge_pass(): pl.pallas_call(functools.partial(edge_kernel, slot), out_shape=(jax.Shape...  6.13 us
    ppermute x3, starting transfers between devices, per_device(): lax.ppermute(partial, 'rows', [(i, i ^ step) for i in range(count)])  4.44 us
  transfers between devices with their start and end apart: 6, of which 4 were waited for; matrix products, arithmetic and copies ran while one was open for 0% of the time, Pallas kernels for 27%

profile of v4, /device:TPU:56, one launch (start us, length us, event | category | flops | bytes accessed | tf_op | source)
XLA Modules:
  0.0 92.1 jit_solution(12140334981473542664)
XLA Ops:
  0.7 0.6 stack.23.where_ref.sites_ref
  1.3 2.5 %shard_map.95._ = bf16[5,16,512]{2,1,0:T(8,128)(2,1)} custom-call(s32[5]{0:T(128)} %stack.23.where_ref.sites_ref, f32[8,64,512]{2,1,0:T(8,128)} %bitcast.16, f32[8,64,512]{2,1,0:T(8,128)} %bitcast.12, s32[8,64,512]{2,1,0:T(8,128)} %bitcast.18), custom_call_target="tpu_custom_call" | custom-call | bytes 1048576 | tf_op jit(solution)/shard_map/pallas_call | solution.py:50
  3.8 8.2 %collective-permute-start.1 = (bf16[5,16,512]{2,1,0:T(8,128)(2,1)}, bf16[5,16,512]{2,1,0:T(8,128)(2,1)S(1)}, u32[]{:S(2)}, u32[]{:S(2)}) collective-permute-start(bf16[5,16,512]{2,1,0:T(8,128)(2,1)} %shard_map.95._), channel_id=1, source_target_pairs={{0,32},{2,34},{4,36},{6,38},{8,40},{10,42},{12,44},{14,46},{16,48}... | collective-permute-start | bytes 245768 | tf_op jit(solution)/shard_map/ppermute | solution.py:397
  11.9 2.8 %shard_map.96 = (bf16[8,64,512]{2,1,0:T(8,128)(2,1)}, bf16[8,64,512]{2,1,0:T(8,128)(2,1)}) custom-call(s32[5]{0:T(128)} %stack.23.where_ref.sites_ref, bf16[8,8,64,512]{3,2,1,0:T(8,128)(2,1)} %bitcast.23, bf16[5,16,512]{2,1,0:T(8,128)(2,1)} %shard_map.95._), custom_call_target="tpu_custom_call" | custom-call | bytes 4194304 | tf_op jit(solution)/shard_map/pallas_call | solution.py:95
  14.8 1.5 %collective-permute-start = (bf16[8,64,512]{2,1,0:T(8,128)(2,1)}, bf16[8,64,512]{2,1,0:T(8,128)(2,1)}, u32[]{:S(2)}, u32[]{:S(2)}) collective-permute-start(bf16[8,64,512]{2,1,0:T(8,128)(2,1)} %get-tuple-element.14), channel_id=1, source_target_pairs={{32,64},{64,32},{96,128},{128,96},{160,192},{192,160},{33,65},{65,... | collective-permute-start | bytes 1572872 | tf_op jit(solution)/shard_map/ppermute | solution.py:401
  16.3 7.4 %collective-permute-start.2 = (bf16[8,64,512]{2,1,0:T(8,128)(2,1)}, bf16[8,64,512]{2,1,0:T(8,128)(2,1)}, u32[]{:S(2)}, u32[]{:S(2)}) collective-permute-start(bf16[8,64,512]{2,1,0:T(8,128)(2,1)} %get-tuple-element.19), channel_id=1, source_target_pairs={{0,32},{32,0},{64,96},{96,64},{128,160},{160,128},{192,224},{224,1... | collective-permute-start | bytes 1572872 | tf_op jit(solution)/shard_map/ppermute | solution.py:400
  23.7 2.9 %shard_map.97 = (bf16[1920,256]{1,0:T(8,128)(2,1)}, bf16[2,192,64]{2,1,0:T(8,128)(2,1)}) custom-call(f32[3,3,64,64]{3,2,1,0:T(8,128)} %weight_ref.1), custom_call_target="tpu_custom_call" | custom-call | tf_op jit(solution)/shard_map/pallas_call | solution.py:365
  26.5 0.0 collective-permute-done.1
  26.5 13.2 %all-gather = bf16[40,16,512]{2,1,0:T(8,128)(2,1)S(1)} all-gather(bf16[5,16,512]{2,1,0:T(8,128)(2,1)S(1)} %collective-permute-done.1), channel_id=2, replica_groups={{0,1,8,9,16,17,24,25},{2,3,10,11,18,19,26,27},{4,5,12,13,20,21,28,29},{..., dimensions={0}, use_global_device_ids=true | all-gather | bytes 737280 | tf_op jit(solution)/shard_map/all_gather | solution.py:402
  39.8 0.0 copy-done
  39.8 0.0 copy-done.1
  39.8 0.0 copy-done.2
  39.8 0.0 copy-done.6
  39.8 0.0 copy-start.5
  39.8 1.2 %copy-done.5 = bf16[1920,256]{1,0:T(8,128)(2,1)S(1)} copy-done((bf16[1920,256]{1,0:T(8,128)(2,1)S(1)}, bf16[1920,256]{1,0:T(8,128)(2,1)}, u32[]{:S(2)}) %copy-start.5) | copy-done | bytes 983064
  41.0 16.4 %shard_map.98 = (bf16[8,8,64,512]{3,2,1,0:T(8,128)(2,1)}, f32[8,2,64,512]{3,2,1,0:T(8,128)S(1)}, bf16[2,64,512]{2,1,0:T(8,128)(2,1)S(1)}, f32[8,8,128]{2,1,0:T(8,128)S(1)}) custom-call(bf16[8,5,16,512]{3,2,1,0:T(8,128)(2,1)S(1)} %bitcast.20, f32[8,64,512]{2,1,0:T(8,128)S(1)} %bitcast.17, f32[8,64,512]{2,1,0:T(8,128)S(1)} %bitcast.13, ...), custom_call_target="tpu_custom_call" | custom-call | flops 20000000000 | bytes 16777216 | tf_op jit(solution)/shard_map/pallas_call | solution.py:225
  57.4 11.6 %collective-permute-done.2.halo_ref = bf16[8,64,512]{2,1,0:T(8,128)(2,1)} collective-permute-done((bf16[8,64,512]{2,1,0:T(8,128)(2,1)}, bf16[8,64,512]{2,1,0:T(8,128)(2,1)}, u32[]{:S(2)}, u32[]{:S(2)}) %collective-permute-start.2) | collective-permute-done | bytes 524320 | tf_op jit(solution)/shard_map/ppermute | solution.py:400
  69.0 0.0 copy-done.4
  69.0 3.1 %shard_map.99 = (bf16[8,8,64,512]{3,2,1,0:T(8,128)(2,1)}, f32[8,8,128]{2,1,0:T(8,128)S(1)}) custom-call(s32[5]{0:T(128)S(1)} %copy-done.4, bf16[8,64,512]{2,1,0:T(8,128)(2,1)} %collective-permute-done.2.halo_ref, bf16[2,64,512]{2,1,0:T(8,128)(2,1)S(1)} %get-tuple-element.16.slope_ref, ...), custom_call_target="tpu_custom_call", output_to_operand_aliasing={{0}: (7, {})} | custom-call | flops 2000000000 | bytes 1048576 | tf_op jit(solution)/shard_map/pallas_call | solution.py:303
  72.1 0.0 copy-start.7
  72.1 0.0 copy-start.8
  72.1 0.0 collective-permute-done.halo_ref
  72.1 3.1 %shard_map.100 = (bf16[8,8,64,512]{3,2,1,0:T(8,128)(2,1)}, f32[8,128]{1,0:T(8,128)S(1)}) custom-call(s32[5]{0:T(128)S(1)} %copy-done.4, bf16[8,64,512]{2,1,0:T(8,128)(2,1)} %collective-permute-done.halo_ref, bf16[2,64,512]{2,1,0:T(8,128)(2,1)S(1)} %get-tuple-element.16.slope_ref, ...), custom_call_target="tpu_custom_call", output_to_operand_aliasing={{0}: (7, {})} | custom-call | flops 2000000000 | bytes 1048576 | tf_op jit(solution)/shard_map/pallas_call | solution.py:303
  75.2 0.1 collective-permute-start.3
  75.3 7.5 %collective-permute-done.3 = f32[8,128]{1,0:T(8,128)S(1)} collective-permute-done((f32[8,128]{1,0:T(8,128)S(1)}, f32[8,128]{1,0:T(8,128)S(1)}, u32[]{:S(2)}, u32[]{:S(2)}) %collective-permute-start.3) | collective-permute-done | bytes 4128 | tf_op jit(solution)/shard_map/ppermute | solution.py:420
  82.8 1.4 %collective-permute-start.4 = (f32[8,128]{1,0:T(8,128)S(1)}, f32[8,128]{1,0:T(8,128)S(1)}, u32[]{:S(2)}, u32[]{:S(2)}) collective-permute-start(f32[8,128]{1,0:T(8,128)S(1)} %add.13), channel_id=1, source_target_pairs={{0,64},{32,96},{64,0},{96,32},{128,192},{160,224},{192,128},{224,1... | collective-permute-start | bytes 12296 | tf_op jit(solution)/shard_map/ppermute | solution.py:420
  84.2 2.2 %collective-permute-done.4 = f32[8,128]{1,0:T(8,128)S(1)} collective-permute-done((f32[8,128]{1,0:T(8,128)S(1)}, f32[8,128]{1,0:T(8,128)S(1)}, u32[]{:S(2)}, u32[]{:S(2)}) %collective-permute-start.4) | collective-permute-done | bytes 4128 | tf_op jit(solution)/shard_map/ppermute | solution.py:420
  86.4 2.9 %collective-permute-start.5 = (f32[8,128]{1,0:T(8,128)S(1)}, f32[8,128]{1,0:T(8,128)S(1)}, u32[]{:S(2)}, u32[]{:S(2)}) collective-permute-start(f32[8,128]{1,0:T(8,128)S(1)} %add.14), channel_id=1, source_target_pairs={{0,128},{32,160},{64,192},{96,224},{128,0},{160,32},{192,64},{224,... | collective-permute-start | bytes 12296 | tf_op jit(solution)/shard_map/ppermute | solution.py:420
  89.3 0.2 select_reduce_fusion
  89.5 2.0 %collective-permute-done.5 = f32[8,128]{1,0:T(8,128)S(1)} collective-permute-done((f32[8,128]{1,0:T(8,128)S(1)}, f32[8,128]{1,0:T(8,128)S(1)}, u32[]{:S(2)}, u32[]{:S(2)}) %collective-permute-start.5) | collective-permute-done | bytes 4128 | tf_op jit(solution)/shard_map/ppermute | solution.py:420
  91.5 0.1 add_reduce_fusion
  91.6 0.5 multiply_add_fusion
  (11 shorter events, 0.0 us)
Async XLA Ops:
  1.3 38.5 %copy-start = (f32[8,512,64]{1,2,0:T(8,128)S(1)}, f32[8,512,64]{1,2,0:T(8,128)}, u32[]{:S(2)}) copy-start(f32[8,512,64]{1,2,0:T(8,128)} %param.9) | copy-start | bytes 3145732
  1.3 38.5 %copy-start.1 = (f32[8,512,64]{1,2,0:T(8,128)S(1)}, f32[8,512,64]{1,2,0:T(8,128)}, u32[]{:S(2)}) copy-start(f32[8,512,64]{1,2,0:T(8,128)} %param.8) | copy-start | bytes 3145732
  1.3 38.5 %copy-start.2 = (s32[8,512,64]{1,2,0:T(8,128)S(1)}, s32[8,512,64]{1,2,0:T(8,128)}, u32[]{:S(2)}) copy-start(s32[8,512,64]{1,2,0:T(8,128)} %param.12) | copy-start | bytes 3145732
  1.3 38.5 %copy-start.6 = (f32[64]{0:T(128)S(1)}, f32[64]{0:T(128)}, u32[]{:S(2)}) copy-start(f32[64]{0:T(128)} %param.11) | copy-start | bytes 772
  3.8 22.8 %collective-permute-start.1 = (bf16[5,16,512]{2,1,0:T(8,128)(2,1)}, bf16[5,16,512]{2,1,0:T(8,128)(2,1)S(1)}, u32[]{:S(2)}, u32[]{:S(2)}) collective-permute-start(bf16[5,16,512]{2,1,0:T(8,128)(2,1)} %shard_map.95._), channel_id=1, source_target_pairs={{0,32},{2,34},{4,36},{6,38},{8,40},{10,42},{12,44},{14,46},{16,48}... | collective-permute-start | bytes 245768 | tf_op jit(solution)/shard_map/ppermute | solution.py:397
  14.8 57.3 %collective-permute-start = (bf16[8,64,512]{2,1,0:T(8,128)(2,1)}, bf16[8,64,512]{2,1,0:T(8,128)(2,1)}, u32[]{:S(2)}, u32[]{:S(2)}) collective-permute-start(bf16[8,64,512]{2,1,0:T(8,128)(2,1)} %get-tuple-element.14), channel_id=1, source_target_pairs={{32,64},{64,32},{96,128},{128,96},{160,192},{192,160},{33,65},{65,... | collective-permute-start | bytes 1572872 | tf_op jit(solution)/shard_map/ppermute | solution.py:401
  16.3 52.7 %collective-permute-start.2 = (bf16[8,64,512]{2,1,0:T(8,128)(2,1)}, bf16[8,64,512]{2,1,0:T(8,128)(2,1)}, u32[]{:S(2)}, u32[]{:S(2)}) collective-permute-start(bf16[8,64,512]{2,1,0:T(8,128)(2,1)} %get-tuple-element.19), channel_id=1, source_target_pairs={{0,32},{32,0},{64,96},{96,64},{128,160},{160,128},{192,224},{224,1... | collective-permute-start | bytes 1572872 | tf_op jit(solution)/shard_map/ppermute | solution.py:400
  39.8 1.2 %copy-start.5 = (bf16[1920,256]{1,0:T(8,128)(2,1)S(1)}, bf16[1920,256]{1,0:T(8,128)(2,1)}, u32[]{:S(2)}) copy-start(bf16[1920,256]{1,0:T(8,128)(2,1)} %get-tuple-element.15.bands_ref) | copy-start | bytes 2949124
  41.0 28.0 %copy-start.3 = (bf16[2,192,64]{2,1,0:T(8,128)(2,1)S(1)}, bf16[2,192,64]{2,1,0:T(8,128)(2,1)}, u32[]{:S(2)}) copy-start(bf16[2,192,64]{2,1,0:T(8,128)(2,1)} %get-tuple-element.18.weight_ref) | copy-start | bytes 147460
  41.0 28.0 %copy-start.4 = (s32[5]{0:T(128)S(1)}, s32[5]{0:T(128)}, u32[]{:S(2)}) copy-start(s32[5]{0:T(128)} %stack.23.where_ref.sites_ref) | copy-start | bytes 64
  72.1 17.3 %copy-start.7 = (f32[4096]{0:T(1024)S(1)}, f32[4096]{0:T(1024)}, u32[]{:S(2)}) copy-start(f32[4096]{0:T(1024)} %param.15) | copy-start | bytes 49156
  72.1 17.3 %copy-start.8 = (s32[8]{0:T(128)S(1)}, s32[8]{0:T(128)}, u32[]{:S(2)}) copy-start(s32[8]{0:T(128)} %param.14) | copy-start | bytes 100
  75.2 7.6 %collective-permute-start.3 = (f32[8,128]{1,0:T(8,128)S(1)}, f32[8,128]{1,0:T(8,128)S(1)}, u32[]{:S(2)}, u32[]{:S(2)}) collective-permute-start(f32[8,128]{1,0:T(8,128)S(1)} %get-tuple-element.25), channel_id=1, source_target_pairs={{0,32},{32,0},{64,96},{96,64},{128,160},{160,128},{192,224},{224,1... | collective-permute-start | bytes 12296 | tf_op jit(solution)/shard_map/ppermute | solution.py:420
  82.8 3.6 %collective-permute-start.4 = (f32[8,128]{1,0:T(8,128)S(1)}, f32[8,128]{1,0:T(8,128)S(1)}, u32[]{:S(2)}, u32[]{:S(2)}) collective-permute-start(f32[8,128]{1,0:T(8,128)S(1)} %add.13), channel_id=1, source_target_pairs={{0,64},{32,96},{64,0},{96,32},{128,192},{160,224},{192,128},{224,1... | collective-permute-start | bytes 12296 | tf_op jit(solution)/shard_map/ppermute | solution.py:420
  86.4 5.1 %collective-permute-start.5 = (f32[8,128]{1,0:T(8,128)S(1)}, f32[8,128]{1,0:T(8,128)S(1)}, u32[]{:S(2)}, u32[]{:S(2)}) collective-permute-start(f32[8,128]{1,0:T(8,128)S(1)} %add.14), channel_id=1, source_target_pairs={{0,128},{32,160},{64,192},{96,224},{128,0},{160,32},{192,64},{224,... | collective-permute-start | bytes 12296 | tf_op jit(solution)/shard_map/ppermute | solution.py:420

commit v5 on v4

--- a/solution.py
+++ b/solution.py
@@ -14,7 +14,7 @@
 MAIN_FLOPS = 20_000_000_000
 EDGE_FLOPS = 2_000_000_000
 MAIN_VMEM = 44 << 20
-EDGE_VMEM = 8 << 20
+EDGE_VMEM = 14 << 20
 UNITS = 5
 
 
@@ -37,38 +37,54 @@
     return high, (value - high.astype(F32)).astype(BF16)
 
 
-def payload_kernel(where_ref, center_ref, radius_ref, status_ref, out_ref):
-    out_ref[0:2] = center_ref[...].astype(BF16)
-    out_ref[2:4] = radius_ref[...].astype(BF16)
-    out_ref[4:5] = status_ref[...].astype(F32).astype(BF16)
-
-
-def payload_pass(where, center, radius, status):
+def payload_kernel(
+    lanes, center_ref, radius_ref, status_ref, box_ref, center_box, radius_box, status_box, sems
+):
+    rows = center_ref.shape[0]
+    part = box_ref.shape[1]
+    me = lax.axis_index("specs")
+    up = 1 - lax.rem(me, 2)
+    here = pl.ds(pl.multiple_of(me // (2 * lanes) * part, part), part)
+    two = pl.ds(up * (rows - 2), 2)
+    one = pl.ds(up * (rows - 1), 1)
+    copies = [
+        pltpu.make_async_copy(center_ref.at[two, here], center_box, sems.at[0]),
+        pltpu.make_async_copy(radius_ref.at[two, here], radius_box, sems.at[1]),
+        pltpu.make_async_copy(status_ref.at[one, here], status_box, sems.at[2]),
+    ]
+    for copy in copies:
+        copy.start()
+    for copy in copies:
+        copy.wait()
+    box_ref[0:2] = center_box[...].astype(BF16)
+    box_ref[2:4] = radius_box[...].astype(BF16)
+    box_ref[4:5] = status_box[...].astype(F32).astype(BF16)
+
+
+def payload_pass(lanes, center, radius, status):
     rows, channels, columns = center.shape
     part = channels * 2 // SHARE
-    box = pl.BlockSpec((2, part, columns), lambda g, w: (w[0], w[1], 0))
     return pl.pallas_call(
-        payload_kernel,
+        functools.partial(payload_kernel, lanes),
         out_shape=jax.ShapeDtypeStruct((UNITS, part, columns), BF16),
-        grid_spec=pltpu.PrefetchScalarGridSpec(
-            num_scalar_prefetch=1,
-            grid=(1,),
-            in_specs=[
-                box,
-                box,
-                pl.BlockSpec((1, part, columns), lambda g, w: (w[2], w[1], 0)),
-            ],
-            out_specs=pl.BlockSpec((UNITS, part, columns), lambda g, w: (0, 0, 0)),
-        ),
+        in_specs=[pl.BlockSpec(memory_space=pl.ANY)] * 3,
+        out_specs=pl.BlockSpec(memory_space=pltpu.VMEM),
+        scratch_shapes=[
+            pltpu.VMEM((2, part, columns), F32),
+            pltpu.VMEM((2, part, columns), F32),
+            pltpu.VMEM((1, part, columns), jnp.int32),
+            pltpu.SemaphoreType.DMA((3,)),
+        ],
         cost_estimate=pl.CostEstimate(flops=0, bytes_accessed=1 << 20, transcendentals=0),
-    )(where, center, radius, status)
-
-
-def send_kernel(sites_ref, coeff_ref, _, first_ref, second_ref, held_ref, sems):
+    )(center, radius, status)
+
+
+def send_kernel(coeff_ref, _, first_ref, second_ref, held_ref, sems):
     specs, rows = coeff_ref.shape[:2]
+    odd = lax.rem(lax.axis_index("rows"), 2)
     todo = [
-        (k, s, sites_ref[3 + k] * (rows - 1), ref)
-        for k, ref in enumerate((first_ref, second_ref))
+        (k, s, h * (rows - 1), ref)
+        for k, (h, ref) in enumerate(((1 - odd, first_ref), (odd, second_ref)))
         for s in range(specs)
     ]
     reads = [
@@ -88,25 +104,21 @@
         write.wait()
 
 
-def send_pass(sites, coeffs, after):
+def send_pass(coeffs, after):
     specs, rows, channels, columns = coeffs.shape
     edge = jax.ShapeDtypeStruct((specs, channels, columns), BF16)
     anywhere = pl.BlockSpec(memory_space=pl.ANY)
     return pl.pallas_call(
         send_kernel,
         out_shape=(edge, edge),
-        grid_spec=pltpu.PrefetchScalarGridSpec(
-            num_scalar_prefetch=1,
-            grid=(1,),
-            in_specs=[anywhere, anywhere],
-            out_specs=(anywhere, anywhere),
-            scratch_shapes=[
-                pltpu.VMEM((2, specs, channels, columns), BF16),
-                pltpu.SemaphoreType.DMA((2, 2, specs)),
-            ],
-        ),
+        in_specs=[anywhere, anywhere],
+        out_specs=(anywhere, anywhere),
+        scratch_shapes=[
+            pltpu.VMEM((2, specs, channels, columns), BF16),
+            pltpu.SemaphoreType.DMA((2, 2, specs)),
+        ],
         cost_estimate=pl.CostEstimate(flops=0, bytes_accessed=4 << 20, transcendentals=0),
-    )(sites, coeffs, after)
+    )(coeffs, after)
 
 
 def main_kernel(
@@ -257,12 +269,13 @@
 
 
 def edge_kernel(
-    slot,
     sites_ref,
-    halo_ref,
+    one_ref,
+    two_ref,
     slope_ref,
     edge_ref,
-    radius_ref,
+    radius_one_ref,
+    radius_two_ref,
     weight_ref,
     total_ref,
     _,
@@ -271,68 +284,71 @@
     done_ref,
     sems,
 ):
-    specs, channels, columns = halo_ref.shape
-    row = sites_ref[slot] * (out_ref.shape[1] - 1)
-
-    def store(s):
-        return pltpu.make_async_copy(done_ref.at[s], out_ref.at[s, row], sems.at[s])
+    specs, channels, columns = one_ref.shape
+    rows = out_ref.shape[1]
+
+    def store(s, k):
+        row = sites_ref[k] * (rows - 1)
+        return pltpu.make_async_copy(done_ref.at[s, k], out_ref.at[s, row], sems.at[s, k])
 
     for s in range(specs):
-        pre = (halo_ref[s].astype(F32) * slope_ref[0].astype(F32)).astype(BF16)
-        value = edge_ref[s, 0] + spread_columns(mul(weight_ref[0], pre), columns)
-        done_ref[s] = value.astype(BF16)
-        store(s).start()
-        terms = jnp.abs(value) * radius_ref[0]
-        terms = jnp.sum(terms.reshape(channels // 8, 8, columns), axis=0)
-        folded = terms[:, :128]
-        for m in range(1, columns // 128):
-            folded = folded + terms[:, m * 128 : (m + 1) * 128]
-        folded = total_ref[s] - folded
-        if len(sum_ref.shape) == 3:
-            sum_ref[s] = folded
-        else:
-            sum_ref[s : s + 1, :] = jnp.sum(folded, axis=0, keepdims=True)
+        total = total_ref[s]
+        for k, (halo_ref, radius_ref) in enumerate(
+            ((one_ref, radius_one_ref), (two_ref, radius_two_ref))
+        ):
+            e = sites_ref[k]
+            pre = (halo_ref[s].astype(F32) * slope_ref[e].astype(F32)).astype(BF16)
+            value = edge_ref[s, e] + spread_columns(mul(weight_ref[e], pre), columns)
+            done_ref[s, k] = value.astype(BF16)
+            store(s, k).start()
+            terms = jnp.abs(value) * radius_ref[0]
+            terms = jnp.sum(terms.reshape(channels // 8, 8, columns), axis=0)
+            for m in range(columns // 128):
+                total = total - terms[:, m * 128 : (m + 1) * 128]
+        sum_ref[s : s + 1, :] = jnp.sum(total, axis=0, keepdims=True)
     for s in range(specs):
-        store(s).wait()
-
-
-def edge_pass(slot, sites, halo, slope, edge, radius, weight, total, out):
+        for k in range(2):
+            store(s, k).wait()
+
+
+def edge_pass(sites, one, two, slope, edge, radius, weight, total, out):
     specs, rows, channels, columns = out.shape
-    last = slot == 4
-    sums = (specs, 128) if last else total.shape
+    whole = lambda a: pl.BlockSpec(a.shape, lambda g, e, n=a.ndim: (0,) * n)
     return pl.pallas_call(
-        functools.partial(edge_kernel, slot),
+        edge_kernel,
         out_shape=(
             jax.ShapeDtypeStruct(out.shape, BF16),
-            jax.ShapeDtypeStruct(sums, F32),
+            jax.ShapeDtypeStruct((specs, 128), F32),
         ),
         grid_spec=pltpu.PrefetchScalarGridSpec(
             num_scalar_prefetch=1,
             grid=(1,),
             in_specs=[
-                pl.BlockSpec(halo.shape, lambda g, e: (0, 0, 0)),
-                pl.BlockSpec((1, channels, columns), lambda g, e: (e[slot], 0, 0)),
-                pl.BlockSpec((specs, 1, channels, columns), lambda g, e: (0, e[slot], 0, 0)),
-                pl.BlockSpec((1, channels, columns), lambda g, e: (e[slot] * (rows - 1), 0, 0)),
-                pl.BlockSpec((1, 3 * channels, channels), lambda g, e: (e[slot], 0, 0)),
-                pl.BlockSpec(total.shape, lambda g, e: (0, 0, 0)),
+                whole(one),
+                whole(two),
+                whole(slope),
+                whole(edge),
+                pl.BlockSpec((1, channels, columns), lambda g, e: (e[0] * (rows - 1), 0, 0)),
+                pl.BlockSpec((1, channels, columns), lambda g, e: (e[1] * (rows - 1), 0, 0)),
+                whole(weight),
+                whole(total),
                 pl.BlockSpec(memory_space=pl.ANY),
             ],
             out_specs=(
                 pl.BlockSpec(memory_space=pl.ANY),
-                pl.BlockSpec(sums, lambda g, e: (0,) * len(sums)),
+                pl.BlockSpec((specs, 128), lambda g, e: (0, 0)),
             ),
             scratch_shapes=[
-                pltpu.VMEM((specs, channels, columns), BF16),
-                pltpu.SemaphoreType.DMA((specs,)),
+                pltpu.VMEM((specs, 2, channels, columns), BF16),
+                pltpu.SemaphoreType.DMA((specs, 2)),
             ],
         ),
-        input_output_aliases={7: 0},
+        input_output_aliases={9: 0},
         compiler_params=pltpu.CompilerParams(vmem_limit_bytes=EDGE_VMEM),
         cost_estimate=pl.CostEstimate(
             flops=EDGE_FLOPS, bytes_accessed=1 << 20, transcendentals=0
         ),
-    )(sites, halo, slope, edge, radius, weight, total, out)
+    )(sites, one, two, slope, edge, radius, radius, weight, total, out)
 
 
 def weight_kernel(weight_ref, bands_ref, ends_ref):
@@ -380,14 +396,8 @@
     coeffs = jnp.swapaxes(out_coeffs, 2, 3)
 
     lanes = groups // SHARE
-    me = lax.axis_index("specs")
-    core, y = (lax.rem(me, 2), me // (2 * lanes))
-    up = core == 0
-    even = 1 - lax.rem(lax.axis_index("rows"), 2)
-    sites = jnp.stack(
-        [jnp.where(up, rows // 2 - 1, 0), y, jnp.where(up, rows - 1, 0), even, 1 - even]
-    ).astype(jnp.int32)
-    mine = payload_pass(sites, center, radius, status)
+    mine = payload_pass(lanes, center, radius, status)
+    center, radius, status, mine = lax.optimization_barrier((center, radius, status, mine))
     moves = []
     for r in range(count):
         for s in range(groups):
@@ -395,7 +405,7 @@
             if 0 <= other < count:
                 moves.append((r * groups + s, other * groups + s))
     box = lax.ppermute(mine, ("rows", "specs"), moves)
-    one, two = send_pass(sites, coeffs, mine)
+    one, two = send_pass(coeffs, mine)
     pairs = [(i, i + 1) for i in range(count - 1)]
     one = lax.ppermute(one, "rows", [m for p in pairs[::2] for m in (p, p[::-1])])
     two = lax.ppermute(two, "rows", [m for p in pairs[1::2] for m in (p, p[::-1])])
@@ -412,14 +422,18 @@
     out, edge, slope, total = main_pass(
         halo, center, radius, status, bands, conv_bias[None, :], coeffs
     )
-    out, total = edge_pass(3, sites, one, slope, edge, radius, ends, total, out)
-    out, partial = edge_pass(4, sites, two, slope, edge, radius, ends, total, out)
-
-    step = 1
-    while step < count:
-        partial = partial + lax.ppermute(partial, "rows", [(i, i ^ step) for i in range(count)])
-        step *= 2
-    summed = jnp.sum(partial, axis=1)
+    odd = lax.rem(lax.axis_index("rows"), 2)
+    sites = jnp.stack([1 - odd, odd]).astype(jnp.int32)
+    out, partial = edge_pass(sites, one, two, slope, edge, radius, ends, total, out)
+
+    partial = partial + lax.ppermute(partial, "rows", [(i, i ^ 1) for i in range(count)])
+    pairs = [partial] + [
+        lax.ppermute(partial, "rows", [(i, i ^ step) for i in range(count)])
+        for step in range(2, count, 2)
+    ]
+    while len(pairs) > 1:
+        pairs = [a + b for a, b in zip(pairs[::2], pairs[1::2])]
+    summed = jnp.sum(pairs[0], axis=1)
     pixels = rows * count * columns
     entries = spec_offsets.shape[0]
     onehot = spec_ids[:, None] == jnp.arange(entries, dtype=jnp.int32)[None, :]

time: 93 us -> 86.3 us (0.928)
  waiting for transfers between devices: 23.2 us -> 9.81 us
  starting transfers between devices: 21.5 us -> 32.6 us
  Pallas kernels: 30.7 us -> 27.3 us
    ppermute x0 -> x1, starting transfers between devices: none -> 14.5 us  [per_device(): lax.ppermute(partial, 'rows', [(i, i ^ 1) for i in range(count)])]
    ppermute x1, waiting for transfers between devices: 11.6 us -> 3.63 us  [per_device(): lax.ppermute(one, 'rows', [m for p in pairs[::2] for m in (p, p[::-1])])]
    ppermute x3, waiting for transfers between devices: 11.7 us -> 4.59 us  [per_device(): lax.ppermute(partial, 'rows', [(i, i ^ step) for i in range(count)])]
    ppermute x1, starting transfers between devices: 7.39 us -> 0.66 us  [per_device(): lax.ppermute(one, 'rows', [m for p in pairs[::2] for m in (p, p[::-1])])]
    pallas_call x4 -> x3, Pallas kernels: 11.4 us -> 7.96 us  [the longest x1 4.06 us: edge_pass(): pl.pallas_call(edge_kernel, out_shape=(jax.ShapeDtypeStruct(out.shape, BF...]
    ppermute x3, starting transfers between devices: 4.44 us -> 7.77 us  [per_device(): lax.ppermute(partial, 'rows', [(i, i ^ step) for i in range(count)])]
    ppermute x0 -> x1, waiting for transfers between devices: none -> 1.59 us  [per_device(): lax.ppermute(partial, 'rows', [(i, i ^ 1) for i in range(count)])]
  transfers between devices with their start and end apart: 6 -> 7, of which waited for: 4 -> 4; matrix products, arithmetic and copies ran while one was open for 0% -> 0% of each run, Pallas kernels for 27% -> 25%
where the time goes in v5:
time: 86.3 us; the launch traced here: 85.8 us
  starting transfers between devices  32.6 us (38%)
  Pallas kernels  27.3 us (32%)
  blocking collectives  13.2 us (15%)
  waiting for transfers between devices  9.81 us (11%)
  local copies, waits for them, and re-layouts  1.23 us (1%)
  other arithmetic  0.93 us (1%)
    pallas_call x1, Pallas kernels, main_pass(): pl.pallas_call(main_kernel, grid=(specs,), out_shape=(jax.ShapeDtypeStruc...  16.4 us
    ppermute x1, starting transfers between devices, per_device(): lax.ppermute(partial, 'rows', [(i, i ^ 1) for i in range(count)])  14.5 us
    all_gather x1, blocking collectives, per_device(): lax.all_gather(box, 'specs', axis_index_groups=[[(k * lanes + z) * 2 + e...  13.2 us
    ppermute x1, starting transfers between devices, per_device(): box = lax.ppermute(mine, ('rows', 'specs'), moves)  8.2 us
    ppermute x3, starting transfers between devices, per_device(): lax.ppermute(partial, 'rows', [(i, i ^ step) for i in range(count)])  7.77 us
    ppermute x3, waiting for transfers between devices, per_device(): lax.ppermute(partial, 'rows', [(i, i ^ step) for i in range(count)])  4.59 us
    pallas_call x1, Pallas kernels, edge_pass(): pl.pallas_call(edge_kernel, out_shape=(jax.ShapeDtypeStruct(out.shape, BF...  4.06 us
    ppermute x1, waiting for transfers between devices, per_device(): lax.ppermute(one, 'rows', [m for p in pairs[::2] for m in (p, p[::-1])])  3.63 us
  transfers between devices with their start and end apart: 7, of which 4 were waited for; matrix products, arithmetic and copies ran while one was open for 0% of the time, Pallas kernels for 25%

profile of v5, /device:TPU:56, one launch (start us, length us, event | category | flops | bytes accessed | tf_op | source)
XLA Modules:
  0.0 85.8 jit_solution(17098338808871258832)
XLA Ops:
  0.6 0.0 copy-start
  0.6 0.0 copy-start.1
  0.7 0.0 copy-start.2
  0.7 0.0 copy-start.5
  0.7 1.7 %shard_map.95._ = bf16[5,16,512]{2,1,0:T(8,128)(2,1)} custom-call(f32[8,64,512]{2,1,0:T(8,128)} %bitcast.13, f32[8,64,512]{2,1,0:T(8,128)} %bitcast.9, s32[8,64,512]{2,1,0:T(8,128)} %bitcast.15), custom_call_target="tpu_custom_call" | custom-call | bytes 1048576 | tf_op jit(solution)/shard_map/pallas_call | solution.py:67
  2.4 8.2 %collective-permute-start.2 = (bf16[5,16,512]{2,1,0:T(8,128)(2,1)}, bf16[5,16,512]{2,1,0:T(8,128)(2,1)S(1)}, u32[]{:S(2)}, u32[]{:S(2)}) collective-permute-start(bf16[5,16,512]{2,1,0:T(8,128)(2,1)} %shard_map.95._), channel_id=1, source_target_pairs={{0,32},{2,34},{4,36},{6,38},{8,40},{10,42},{12,44},{14,46},{16,48}... | collective-permute-start | bytes 245768 | tf_op jit(solution)/shard_map/ppermute | solution.py:407
  10.6 2.2 %shard_map.96 = (bf16[8,64,512]{2,1,0:T(8,128)(2,1)}, bf16[8,64,512]{2,1,0:T(8,128)(2,1)}) custom-call(bf16[8,8,64,512]{3,2,1,0:T(8,128)(2,1)} %bitcast.20, bf16[5,16,512]{2,1,0:T(8,128)(2,1)} %shard_map.95._), custom_call_target="tpu_custom_call" | custom-call | bytes 4194304 | tf_op jit(solution)/shard_map/pallas_call | solution.py:111
  12.8 0.7 collective-permute-start
  13.5 1.4 %collective-permute-start.1 = (bf16[8,64,512]{2,1,0:T(8,128)(2,1)}, bf16[8,64,512]{2,1,0:T(8,128)(2,1)}, u32[]{:S(2)}, u32[]{:S(2)}) collective-permute-start(bf16[8,64,512]{2,1,0:T(8,128)(2,1)} %get-tuple-element.18), channel_id=1, source_target_pairs={{32,64},{64,32},{96,128},{128,96},{160,192},{192,160},{33,65},{65,... | collective-permute-start | bytes 1572872 | tf_op jit(solution)/shard_map/ppermute | solution.py:411
  14.9 2.9 %shard_map.97 = (bf16[1920,256]{1,0:T(8,128)(2,1)}, bf16[2,192,64]{2,1,0:T(8,128)(2,1)}) custom-call(f32[3,3,64,64]{3,2,1,0:T(8,128)} %weight_ref.1), custom_call_target="tpu_custom_call" | custom-call | tf_op jit(solution)/shard_map/pallas_call | solution.py:381
  17.8 0.1 pad_add_fusion.sites_ref
  17.9 0.0 collective-permute-done.2
  17.9 13.2 %all-gather = bf16[40,16,512]{2,1,0:T(8,128)(2,1)S(1)} all-gather(bf16[5,16,512]{2,1,0:T(8,128)(2,1)S(1)} %collective-permute-done.2), channel_id=2, replica_groups={{0,1,8,9,16,17,24,25},{2,3,10,11,18,19,26,27},{4,5,12,13,20,21,28,29},{..., dimensions={0}, use_global_device_ids=true | all-gather | bytes 737280 | tf_op jit(solution)/shard_map/all_gather | solution.py:412
  31.1 0.0 copy-done.5
  31.1 0.0 copy-start.4
  31.1 1.2 %copy-done.4 = bf16[1920,256]{1,0:T(8,128)(2,1)S(1)} copy-done((bf16[1920,256]{1,0:T(8,128)(2,1)S(1)}, bf16[1920,256]{1,0:T(8,128)(2,1)}, u32[]{:S(2)}) %copy-start.4) | copy-done | bytes 983064
  32.3 16.4 %shard_map.98 = (bf16[8,8,64,512]{3,2,1,0:T(8,128)(2,1)}, f32[8,2,64,512]{3,2,1,0:T(8,128)S(1)}, bf16[2,64,512]{2,1,0:T(8,128)(2,1)S(1)}, f32[8,8,128]{2,1,0:T(8,128)S(1)}) custom-call(bf16[8,5,16,512]{3,2,1,0:T(8,128)(2,1)S(1)} %bitcast.17, f32[8,64,512]{2,1,0:T(8,128)S(1)} %bitcast.14, f32[8,64,512]{2,1,0:T(8,128)S(1)} %bitcast.10, ...), custom_call_target="tpu_custom_call" | custom-call | flops 20000000000 | bytes 16777216 | tf_op jit(solution)/shard_map/pallas_call | solution.py:237
  48.7 3.6 %collective-permute-done.one_ref = bf16[8,64,512]{2,1,0:T(8,128)(2,1)} collective-permute-done((bf16[8,64,512]{2,1,0:T(8,128)(2,1)}, bf16[8,64,512]{2,1,0:T(8,128)(2,1)}, u32[]{:S(2)}, u32[]{:S(2)}) %collective-permute-start) | collective-permute-done | bytes 524320 | tf_op jit(solution)/shard_map/ppermute | solution.py:410
  52.4 0.0 collective-permute-done.1.two_ref
  52.4 0.0 copy-start.7
  52.4 4.1 %shard_map.99 = (bf16[8,8,64,512]{3,2,1,0:T(8,128)(2,1)}, f32[8,128]{1,0:T(8,128)S(1)}) custom-call(s32[2]{0:T(128)S(1)} %pad_add_fusion.sites_ref, bf16[8,64,512]{2,1,0:T(8,128)(2,1)} %collective-permute-done.one_ref, bf16[8,64,512]{2,1,0:T(8,128)(2,1)} %collective-permute-done.1.two_ref, ...), custom_call_target="tpu_custom_call", output_to_operand_aliasing={{0}: (9, {})} | custom-call | flops 2000000000 | bytes 1048576 | tf_op jit(solution)/shard_map/pallas_call | solution.py:317
  56.4 14.5 %collective-permute-start.3 = (f32[8,128]{1,0:T(8,128)S(1)}, f32[8,128]{1,0:T(8,128)S(1)}, u32[]{:S(2)}, u32[]{:S(2)}) collective-permute-start(f32[8,128]{1,0:T(8,128)S(1)} %get-tuple-element.29), channel_id=1, source_target_pairs={{0,32},{32,0},{64,96},{96,64},{128,160},{160,128},{192,224},{224,1... | collective-permute-start | bytes 12296 | tf_op jit(solution)/shard_map/ppermute | solution.py:429
  71.0 1.6 %collective-permute-done.3 = f32[8,128]{1,0:T(8,128)S(1)} collective-permute-done((f32[8,128]{1,0:T(8,128)S(1)}, f32[8,128]{1,0:T(8,128)S(1)}, u32[]{:S(2)}, u32[]{:S(2)}) %collective-permute-start.3) | collective-permute-done | bytes 4128 | tf_op jit(solution)/shard_map/ppermute | solution.py:429
  72.6 1.5 %collective-permute-start.4 = (f32[8,128]{1,0:T(8,128)S(1)}, f32[8,128]{1,0:T(8,128)S(1)}, u32[]{:S(2)}, u32[]{:S(2)}) collective-permute-start(f32[8,128]{1,0:T(8,128)S(1)} %add.15), channel_id=1, source_target_pairs={{0,64},{32,96},{64,0},{96,32},{128,192},{160,224},{192,128},{224,1... | collective-permute-start | bytes 12296 | tf_op jit(solution)/shard_map/ppermute | solution.py:431
  74.1 6.2 %collective-permute-start.5 = (f32[8,128]{1,0:T(8,128)S(1)}, f32[8,128]{1,0:T(8,128)S(1)}, u32[]{:S(2)}, u32[]{:S(2)}) collective-permute-start(f32[8,128]{1,0:T(8,128)S(1)} %add.15), channel_id=1, source_target_pairs={{0,128},{32,160},{64,192},{96,224},{128,0},{160,32},{192,64},{224,... | collective-permute-start | bytes 12296 | tf_op jit(solution)/shard_map/ppermute | solution.py:431
  80.3 0.0 collective-permute-start.6
  80.4 0.2 select_reduce_fusion
  80.6 0.0 collective-permute-done.4
  80.6 1.4 %collective-permute-done.5 = f32[8,128]{1,0:T(8,128)S(1)} collective-permute-done((f32[8,128]{1,0:T(8,128)S(1)}, f32[8,128]{1,0:T(8,128)S(1)}, u32[]{:S(2)}, u32[]{:S(2)}) %collective-permute-start.5) | collective-permute-done | bytes 4128 | tf_op jit(solution)/shard_map/ppermute | solution.py:431
  82.0 3.2 %collective-permute-done.6 = f32[8,128]{1,0:T(8,128)S(1)} collective-permute-done((f32[8,128]{1,0:T(8,128)S(1)}, f32[8,128]{1,0:T(8,128)S(1)}, u32[]{:S(2)}, u32[]{:S(2)}) %collective-permute-start.6) | collective-permute-done | bytes 4128 | tf_op jit(solution)/shard_map/ppermute | solution.py:431
  85.2 0.1 add_reduce_fusion
  85.3 0.5 multiply_add_fusion
  (9 shorter events, 0.0 us)
Async XLA Ops:
  0.6 30.5 %copy-start = (f32[8,512,64]{1,2,0:T(8,128)S(1)}, f32[8,512,64]{1,2,0:T(8,128)}, u32[]{:S(2)}) copy-start(f32[8,512,64]{1,2,0:T(8,128)} %param.9) | copy-start | bytes 3145732
  0.6 30.5 %copy-start.1 = (f32[8,512,64]{1,2,0:T(8,128)S(1)}, f32[8,512,64]{1,2,0:T(8,128)}, u32[]{:S(2)}) copy-start(f32[8,512,64]{1,2,0:T(8,128)} %param.8) | copy-start | bytes 3145732
  0.7 30.5 %copy-start.2 = (s32[8,512,64]{1,2,0:T(8,128)S(1)}, s32[8,512,64]{1,2,0:T(8,128)}, u32[]{:S(2)}) copy-start(s32[8,512,64]{1,2,0:T(8,128)} %param.12) | copy-start | bytes 3145732
  0.7 30.4 %copy-start.5 = (f32[64]{0:T(128)S(1)}, f32[64]{0:T(128)}, u32[]{:S(2)}) copy-start(f32[64]{0:T(128)} %param.11) | copy-start | bytes 772
  2.4 15.5 %collective-permute-start.2 = (bf16[5,16,512]{2,1,0:T(8,128)(2,1)}, bf16[5,16,512]{2,1,0:T(8,128)(2,1)S(1)}, u32[]{:S(2)}, u32[]{:S(2)}) collective-permute-start(bf16[5,16,512]{2,1,0:T(8,128)(2,1)} %shard_map.95._), channel_id=1, source_target_pairs={{0,32},{2,34},{4,36},{6,38},{8,40},{10,42},{12,44},{14,46},{16,48}... | collective-permute-start | bytes 245768 | tf_op jit(solution)/shard_map/ppermute | solution.py:407
  12.8 39.6 %collective-permute-start = (bf16[8,64,512]{2,1,0:T(8,128)(2,1)}, bf16[8,64,512]{2,1,0:T(8,128)(2,1)}, u32[]{:S(2)}, u32[]{:S(2)}) collective-permute-start(bf16[8,64,512]{2,1,0:T(8,128)(2,1)} %get-tuple-element.17), channel_id=1, source_target_pairs={{0,32},{32,0},{64,96},{96,64},{128,160},{160,128},{192,224},{224,1... | collective-permute-start | bytes 1572872 | tf_op jit(solution)/shard_map/ppermute | solution.py:410
  13.5 38.9 %collective-permute-start.1 = (bf16[8,64,512]{2,1,0:T(8,128)(2,1)}, bf16[8,64,512]{2,1,0:T(8,128)(2,1)}, u32[]{:S(2)}, u32[]{:S(2)}) collective-permute-start(bf16[8,64,512]{2,1,0:T(8,128)(2,1)} %get-tuple-element.18), channel_id=1, source_target_pairs={{32,64},{64,32},{96,128},{128,96},{160,192},{192,160},{33,65},{65,... | collective-permute-start | bytes 1572872 | tf_op jit(solution)/shard_map/ppermute | solution.py:411
  31.1 1.2 %copy-start.4 = (bf16[1920,256]{1,0:T(8,128)(2,1)S(1)}, bf16[1920,256]{1,0:T(8,128)(2,1)}, u32[]{:S(2)}) copy-start(bf16[1920,256]{1,0:T(8,128)(2,1)} %get-tuple-element.22.bands_ref) | copy-start | bytes 2949124
  32.3 20.0 %copy-start.3 = (bf16[2,192,64]{2,1,0:T(8,128)(2,1)S(1)}, bf16[2,192,64]{2,1,0:T(8,128)(2,1)}, u32[]{:S(2)}) copy-start(bf16[2,192,64]{2,1,0:T(8,128)(2,1)} %get-tuple-element.25.weight_ref) | copy-start | bytes 147460
  52.4 28.0 %copy-start.6 = (f32[4096]{0:T(1024)S(1)}, f32[4096]{0:T(1024)}, u32[]{:S(2)}) copy-start(f32[4096]{0:T(1024)} %param.15) | copy-start | bytes 49156
  52.4 28.0 %copy-start.7 = (s32[8]{0:T(128)S(1)}, s32[8]{0:T(128)}, u32[]{:S(2)}) copy-start(s32[8]{0:T(128)} %param.14) | copy-start | bytes 100
  56.4 16.1 %collective-permute-start.3 = (f32[8,128]{1,0:T(8,128)S(1)}, f32[8,128]{1,0:T(8,128)S(1)}, u32[]{:S(2)}, u32[]{:S(2)}) collective-permute-start(f32[8,128]{1,0:T(8,128)S(1)} %get-tuple-element.29), channel_id=1, source_target_pairs={{0,32},{32,0},{64,96},{96,64},{128,160},{160,128},{192,224},{224,1... | collective-permute-start | bytes 12296 | tf_op jit(solution)/shard_map/ppermute | solution.py:429
  72.6 8.0 %collective-permute-start.4 = (f32[8,128]{1,0:T(8,128)S(1)}, f32[8,128]{1,0:T(8,128)S(1)}, u32[]{:S(2)}, u32[]{:S(2)}) collective-permute-start(f32[8,128]{1,0:T(8,128)S(1)} %add.15), channel_id=1, source_target_pairs={{0,64},{32,96},{64,0},{96,32},{128,192},{160,224},{192,128},{224,1... | collective-permute-start | bytes 12296 | tf_op jit(solution)/shard_map/ppermute | solution.py:431
  74.1 7.9 %collective-permute-start.5 = (f32[8,128]{1,0:T(8,128)S(1)}, f32[8,128]{1,0:T(8,128)S(1)}, u32[]{:S(2)}, u32[]{:S(2)}) collective-permute-start(f32[8,128]{1,0:T(8,128)S(1)} %add.15), channel_id=1, source_target_pairs={{0,128},{32,160},{64,192},{96,224},{128,0},{160,32},{192,64},{224,... | collective-permute-start | bytes 12296 | tf_op jit(solution)/shard_map/ppermute | solution.py:431
  80.3 4.8 %collective-permute-start.6 = (f32[8,128]{1,0:T(8,128)S(1)}, f32[8,128]{1,0:T(8,128)S(1)}, u32[]{:S(2)}, u32[]{:S(2)}) collective-permute-start(f32[8,128]{1,0:T(8,128)S(1)} %add.15), channel_id=1, source_target_pairs={{0,192},{32,224},{64,128},{96,160},{128,64},{160,96},{192,0},{224,... | collective-permute-start | bytes 12296 | tf_op jit(solution)/shard_map/ppermute | solution.py:431

commit v6 on v5

--- a/solution.py
+++ b/solution.py
@@ -37,66 +37,55 @@
     return high, (value - high.astype(F32)).astype(BF16)
 
 
-def payload_kernel(
-    lanes, center_ref, radius_ref, status_ref, box_ref, center_box, radius_box, status_box, sems
+def send_kernel(
+    lanes,
+    center_ref,
+    radius_ref,
+    status_ref,
+    coeff_ref,
+    box_ref,
+    first_ref,
+    second_ref,
+    held_ref,
+    center_box,
+    radius_box,
+    status_box,
+    box_sems,
+    sems,
 ):
-    rows = center_ref.shape[0]
+    specs, rows = coeff_ref.shape[:2]
     part = box_ref.shape[1]
     me = lax.axis_index("specs")
     up = 1 - lax.rem(me, 2)
     here = pl.ds(pl.multiple_of(me // (2 * lanes) * part, part), part)
     two = pl.ds(up * (rows - 2), 2)
     one = pl.ds(up * (rows - 1), 1)
-    copies = [
-        pltpu.make_async_copy(center_ref.at[two, here], center_box, sems.at[0]),
-        pltpu.make_async_copy(radius_ref.at[two, here], radius_box, sems.at[1]),
-        pltpu.make_async_copy(status_ref.at[one, here], status_box, sems.at[2]),
-    ]
-    for copy in copies:
+    odd = lax.rem(lax.axis_index("rows"), 2)
+    boxes = [
+        pltpu.make_async_copy(center_ref.at[two, here], center_box, box_sems.at[0]),
+        pltpu.make_async_copy(radius_ref.at[two, here], radius_box, box_sems.at[1]),
+        pltpu.make_async_copy(status_ref.at[one, here], status_box, box_sems.at[2]),
+    ]
+    todo = [
+        (k, s, h * (rows - 1), ref)
+        for k, (h, ref) in enumerate(((1 - odd, first_ref), (odd, second_ref)))
+        for s in range(specs)
+    ]
+    reads = [
+        pltpu.make_async_copy(coeff_ref.at[s, h], held_ref.at[k, s], sems.at[0, k, s])
+        for k, s, h, _ in todo
+    ]
+    writes = [
+        pltpu.make_async_copy(held_ref.at[k, s], ref.at[s], sems.at[1, k, s])
+        for k, s, _, ref in todo
+    ]
+    for copy in boxes + reads:
         copy.start()
-    for copy in copies:
+    for copy in boxes:
         copy.wait()
     box_ref[0:2] = center_box[...].astype(BF16)
     box_ref[2:4] = radius_box[...].astype(BF16)
     box_ref[4:5] = status_box[...].astype(F32).astype(BF16)
-
-
-def payload_pass(lanes, center, radius, status):
-    rows, channels, columns = center.shape
-    part = channels * 2 // SHARE
-    return pl.pallas_call(
-        functools.partial(payload_kernel, lanes),
-        out_shape=jax.ShapeDtypeStruct((UNITS, part, columns), BF16),
-        in_specs=[pl.BlockSpec(memory_space=pl.ANY)] * 3,
-        out_specs=pl.BlockSpec(memory_space=pltpu.VMEM),
-        scratch_shapes=[
-            pltpu.VMEM((2, part, columns), F32),
-            pltpu.VMEM((2, part, columns), F32),
-            pltpu.VMEM((1, part, columns), jnp.int32),
-            pltpu.SemaphoreType.DMA((3,)),
-        ],
-        cost_estimate=pl.CostEstimate(flops=0, bytes_accessed=1 << 20, transcendentals=0),
-    )(center, radius, status)
-
-
-def send_kernel(coeff_ref, _, first_ref, second_ref, held_ref, sems):
-    specs, rows = coeff_ref.shape[:2]
-    odd = lax.rem(lax.axis_index("rows"), 2)
-    todo = [
-        (k, s, h * (rows - 1), ref)
-        for k, (h, ref) in enumerate(((1 - odd, first_ref), (odd, second_ref)))
-        for s in range(specs)
-    ]
-    reads = [
-        pltpu.make_async_copy(coeff_ref.at[s, h], held_ref.at[k, s], sems.at[0, k, s])
-        for k, s, h, _ in todo
-    ]
-    writes = [
-        pltpu.make_async_copy(held_ref.at[k, s], ref.at[s], sems.at[1, k, s])
-        for k, s, _, ref in todo
-    ]
-    for read in reads:
-        read.start()
     for read, write in zip(reads, writes):
         read.wait()
         write.start()
@@ -104,21 +93,40 @@
         write.wait()
 
 
-def send_pass(coeffs, after):
+def send_pass(lanes, center, radius, status, coeffs):
     specs, rows, channels, columns = coeffs.shape
+    part = channels * 2 // SHARE
     edge = jax.ShapeDtypeStruct((specs, channels, columns), BF16)
     anywhere = pl.BlockSpec(memory_space=pl.ANY)
     return pl.pallas_call(
-        send_kernel,
-        out_shape=(edge, edge),
-        in_specs=[anywhere, anywhere],
-        out_specs=(anywhere, anywhere),
+        functools.partial(send_kernel, lanes),
+        out_shape=(jax.ShapeDtypeStruct((UNITS, part, columns), BF16), edge, edge),
+        in_specs=[anywhere] * 4,
+        out_specs=(pl.BlockSpec(memory_space=pltpu.VMEM), anywhere, anywhere),
         scratch_shapes=[
             pltpu.VMEM((2, specs, channels, columns), BF16),
+            pltpu.VMEM((2, part, columns), F32),
+            pltpu.VMEM((2, part, columns), F32),
+            pltpu.VMEM((1, part, columns), jnp.int32),
+            pltpu.SemaphoreType.DMA((3,)),
             pltpu.SemaphoreType.DMA((2, 2, specs)),
         ],
         cost_estimate=pl.CostEstimate(flops=0, bytes_accessed=4 << 20, transcendentals=0),
-    )(coeffs, after)
+    )(center, radius, status, coeffs)
+
+
+def later_pass(first, second, box):
+    def kernel(*refs):
+        pass
+
+    anywhere = pl.BlockSpec(memory_space=pl.ANY)
+    return pl.pallas_call(
+        kernel,
+        out_shape=tuple(jax.ShapeDtypeStruct(a.shape, a.dtype) for a in (first, second)),
+        in_specs=[anywhere] * 3,
+        out_specs=(anywhere, anywhere),
+        input_output_aliases={0: 0, 1: 1},
+    )(first, second, box)
 
 
 def main_kernel(
@@ -269,86 +277,103 @@
 
 
 def edge_kernel(
-    sites_ref,
     one_ref,
     two_ref,
     slope_ref,
     edge_ref,
-    radius_one_ref,
-    radius_two_ref,
+    radius_ref,
     weight_ref,
     total_ref,
     _,
     out_ref,
     sum_ref,
+    halo_buf,
+    edge_buf,
+    slope_buf,
+    radius_buf,
+    weight_buf,
     done_ref,
+    few_sems,
     sems,
 ):
     specs, channels, columns = one_ref.shape
     rows = out_ref.shape[1]
-
-    def store(s, k):
-        row = sites_ref[k] * (rows - 1)
-        return pltpu.make_async_copy(done_ref.at[s, k], out_ref.at[s, row], sems.at[s, k])
-
+    odd = lax.rem(lax.axis_index("rows"), 2)
+    which = (1 - odd, odd)
+    copy = pltpu.make_async_copy
+    few = [
+        copy(slope_ref, slope_buf, few_sems.at[0]),
+        copy(weight_ref, weight_buf, few_sems.at[1]),
+        copy(radius_ref.at[0], radius_buf.at[0], few_sems.at[2]),
+        copy(radius_ref.at[rows - 1], radius_buf.at[1], few_sems.at[3]),
+    ]
+    halos = [
+        [copy(ref.at[s], halo_buf.at[k, s], sems.at[k, s]) for k, ref in enumerate((one_ref, two_ref))]
+        for s in range(specs)
+    ]
+    edges = [copy(edge_ref.at[s], edge_buf.at[s], sems.at[2, s]) for s in range(specs)]
+    stores = [
+        [
+            copy(done_ref.at[s, k], out_ref.at[s, which[k] * (rows - 1)], sems.at[3 + k, s])
+            for k in range(2)
+        ]
+        for s in range(specs)
+    ]
+    for c in few:
+        c.start()
     for s in range(specs):
+        for c in (*halos[s], edges[s]):
+            c.start()
+    for c in few:
+        c.wait()
+    for s in range(specs):
+        for c in (*halos[s], edges[s]):
+            c.wait()
         total = total_ref[s]
-        for k, (halo_ref, radius_ref) in enumerate(
-            ((one_ref, radius_one_ref), (two_ref, radius_two_ref))
-        ):
-            e = sites_ref[k]
-            pre = (halo_ref[s].astype(F32) * slope_ref[e].astype(F32)).astype(BF16)
-            value = edge_ref[s, e] + spread_columns(mul(weight_ref[e], pre), columns)
+        for k in range(2):
+            e = which[k]
+            pre = (halo_buf[k, s].astype(F32) * slope_buf[e].astype(F32)).astype(BF16)
+            value = edge_buf[s, e] + spread_columns(mul(weight_buf[e], pre), columns)
             done_ref[s, k] = value.astype(BF16)
-            store(s, k).start()
-            terms = jnp.abs(value) * radius_ref[0]
+            stores[s][k].start()
+            terms = jnp.abs(value) * radius_buf[e]
             terms = jnp.sum(terms.reshape(channels // 8, 8, columns), axis=0)
             for m in range(columns // 128):
                 total = total - terms[:, m * 128 : (m + 1) * 128]
         sum_ref[s : s + 1, :] = jnp.sum(total, axis=0, keepdims=True)
     for s in range(specs):
-        for k in range(2):
-            store(s, k).wait()
-
-
-def edge_pass(sites, one, two, slope, edge, radius, weight, total, out):
+        for c in stores[s]:
+            c.wait()
+
+
+def edge_pass(one, two, slope, edge, radius, weight, total, out):
     specs, rows, channels, columns = out.shape
-    whole = lambda a: pl.BlockSpec(a.shape, lambda g, e, n=a.ndim: (0,) * n)
+    anywhere = pl.BlockSpec(memory_space=pl.ANY)
+    inside = pl.BlockSpec(memory_space=pltpu.VMEM)
     return pl.pallas_call(
         edge_kernel,
         out_shape=(
             jax.ShapeDtypeStruct(out.shape, BF16),
             jax.ShapeDtypeStruct((specs, 128), F32),
         ),
-        grid_spec=pltpu.PrefetchScalarGridSpec(
-            num_scalar_prefetch=1,
-            grid=(1,),
-            in_specs=[
-                whole(one),
-                whole(two),
-                whole(slope),
-                whole(edge),
-                pl.BlockSpec((1, channels, columns), lambda g, e: (e[0] * (rows - 1), 0, 0)),
-                pl.BlockSpec((1, channels, columns), lambda g, e: (e[1] * (rows - 1), 0, 0)),
-                whole(weight),
-                whole(total),
-                pl.BlockSpec(memory_space=pl.ANY),
-            ],
-            out_specs=(
-                pl.BlockSpec(memory_space=pl.ANY),
-                pl.BlockSpec((specs, 128), lambda g, e: (0, 0)),
-            ),
-            scratch_shapes=[
-                pltpu.VMEM((specs, 2, channels, columns), BF16),
-                pltpu.SemaphoreType.DMA((specs, 2)),
-            ],
-        ),
-        input_output_aliases={9: 0},
+        in_specs=[anywhere] * 6 + [inside, anywhere],
+        out_specs=(anywhere, inside),
+        scratch_shapes=[
+            pltpu.VMEM((2, specs, channels, columns), BF16),
+            pltpu.VMEM((specs, 2, channels, columns), F32),
+            pltpu.VMEM((2, channels, columns), BF16),
+            pltpu.VMEM((2, channels, columns), F32),
+            pltpu.VMEM((2, 3 * channels, channels), BF16),
+            pltpu.VMEM((specs, 2, channels, columns), BF16),
+            pltpu.SemaphoreType.DMA((4,)),
+            pltpu.SemaphoreType.DMA((5, specs)),
+        ],
+        input_output_aliases={7: 0},
         compiler_params=pltpu.CompilerParams(vmem_limit_bytes=EDGE_VMEM),
         cost_estimate=pl.CostEstimate(
             flops=EDGE_FLOPS, bytes_accessed=1 << 20, transcendentals=0
         ),
-    )(sites, one, two, slope, edge, radius, radius, weight, total, out)
+    )(one, two, slope, edge, radius, weight, total, out)
 
 
 def weight_kernel(weight_ref, bands_ref, ends_ref):
@@ -396,8 +421,7 @@
     coeffs = jnp.swapaxes(out_coeffs, 2, 3)
 
     lanes = groups // SHARE
-    mine = payload_pass(lanes, center, radius, status)
-    center, radius, status, mine = lax.optimization_barrier((center, radius, status, mine))
+    mine, one, two = send_pass(lanes, center, radius, status, coeffs)
     moves = []
     for r in range(count):
         for s in range(groups):
@@ -405,7 +429,7 @@
             if 0 <= other < count:
                 moves.append((r * groups + s, other * groups + s))
     box = lax.ppermute(mine, ("rows", "specs"), moves)
-    one, two = send_pass(coeffs, mine)
+    one, two = later_pass(one, two, mine)
     pairs = [(i, i + 1) for i in range(count - 1)]
     one = lax.ppermute(one, "rows", [m for p in pairs[::2] for m in (p, p[::-1])])
     two = lax.ppermute(two, "rows", [m for p in pairs[1::2] for m in (p, p[::-1])])
@@ -422,9 +446,7 @@
     out, edge, slope, total = main_pass(
         halo, center, radius, status, bands, conv_bias[None, :], coeffs
     )
-    odd = lax.rem(lax.axis_index("rows"), 2)
-    sites = jnp.stack([1 - odd, odd]).astype(jnp.int32)
-    out, partial = edge_pass(sites, one, two, slope, edge, radius, ends, total, out)
+    out, partial = edge_pass(one, two, slope, edge, radius, ends, total, out)
 
     partial = partial + lax.ppermute(partial, "rows", [(i, i ^ 1) for i in range(count)])
     pairs = [partial] + [

time: 86.3 us -> 89.3 us (1.035)
  the two profiles are of different devices: /device:TPU:56 before, /device:TPU:16 now
where the time goes in v6:
time: 89.3 us; the launch traced here: 88.8 us
  starting transfers between devices  39.5 us (44%)
  Pallas kernels  28.3 us (32%)
  blocking collectives  12 us (13%)
  waiting for transfers between devices  6.19 us (7%)
  local copies, waits for them, and re-layouts  1.23 us (1%)
    ppermute x1, starting transfers between devices, per_device(): lax.ppermute(partial, 'rows', [(i, i ^ 1) for i in range(count)])  21.8 us
    pallas_call x1, Pallas kernels, main_pass(): pl.pallas_call(main_kernel, grid=(specs,), out_shape=(jax.ShapeDtypeStruc...  16.5 us
    all_gather x1, blocking collectives, per_device(): lax.all_gather(box, 'specs', axis_index_groups=[[(k * lanes + z) * 2 + e...  12 us
    ppermute x1, starting transfers between devices, per_device(): box = lax.ppermute(mine, ('rows', 'specs'), moves)  9.1 us
    ppermute x3, starting transfers between devices, per_device(): lax.ppermute(partial, 'rows', [(i, i ^ step) for i in range(count)])  7.04 us
    pallas_call x1, Pallas kernels, edge_pass(): pl.pallas_call(edge_kernel, out_shape=(jax.ShapeDtypeStruct(out.shape, BF...  5.59 us
    ppermute x3, waiting for transfers between devices, per_device(): lax.ppermute(partial, 'rows', [(i, i ^ step) for i in range(count)])  4.59 us
    pallas_call x1, Pallas kernels, send_pass(): pl.pallas_call(functools.partial(send_kernel, lanes), out_shape=(jax.Shap...  3.34 us
  transfers between devices with their start and end apart: 7, of which 3 were waited for; matrix products, arithmetic and copies ran while one was open for 0% of the time, Pallas kernels for 22%

profile of v6, /device:TPU:16, one launch (start us, length us, event | category | flops | bytes accessed | tf_op | source)
XLA Modules:
  0.0 88.8 jit_solution(9285383791263384766)
XLA Ops:
  0.6 0.0 copy-start
  0.6 0.0 copy-start.1
  0.7 0.0 copy-start.2
  0.7 0.0 copy-start.5
  0.7 3.3 %shard_map.95 = (bf16[5,16,512]{2,1,0:T(8,128)(2,1)}, bf16[8,64,512]{2,1,0:T(8,128)(2,1)}, bf16[8,64,512]{2,1,0:T(8,128)(2,1)}) custom-call(f32[8,64,512]{2,1,0:T(8,128)} %bitcast.10, f32[8,64,512]{2,1,0:T(8,128)} %bitcast.7, s32[8,64,512]{2,1,0:T(8,128)} %bitcast.12, bf16[8,8,64,512]{3,2,1,0:T(8,128)(2,1)} %bitcast.16), custom_call_target="tpu_custom_call" | custom-call | bytes 4194304 | tf_op jit(solution)/shard_map/pallas_call | solution.py:101
  4.0 9.1 %collective-permute-start.2 = (bf16[5,16,512]{2,1,0:T(8,128)(2,1)}, bf16[5,16,512]{2,1,0:T(8,128)(2,1)S(1)}, u32[]{:S(2)}, u32[]{:S(2)}) collective-permute-start(bf16[5,16,512]{2,1,0:T(8,128)(2,1)} %get-tuple-element.17.refs_2_), channel_id=1, source_target_pairs={{0,32},{2,34},{4,36},{6,38},{8,40},{10,42},{12,44},{14,46},{16,48}... | collective-permute-start | bytes 245768 | tf_op jit(solution)/shard_map/ppermute | solution.py:431
  13.1 0.1 collective-permute-start
  13.2 1.5 %collective-permute-start.1 = (bf16[8,64,512]{2,1,0:T(8,128)(2,1)}, bf16[8,64,512]{2,1,0:T(8,128)(2,1)}, u32[]{:S(2)}, u32[]{:S(2)}) collective-permute-start(bf16[8,64,512]{2,1,0:T(8,128)(2,1)} %get-tuple-element.19), channel_id=1, source_target_pairs={{32,64},{64,32},{96,128},{128,96},{160,192},{192,160},{33,65},{65,... | collective-permute-start | bytes 1572872 | tf_op jit(solution)/shard_map/ppermute | solution.py:435
  14.7 2.9 %shard_map.97 = (bf16[1920,256]{1,0:T(8,128)(2,1)}, bf16[2,192,64]{2,1,0:T(8,128)(2,1)}) custom-call(f32[3,3,64,64]{3,2,1,0:T(8,128)} %weight_ref.1), custom_call_target="tpu_custom_call" | custom-call | tf_op jit(solution)/shard_map/pallas_call | solution.py:406
  17.6 0.0 collective-permute-done.2
  17.6 12.0 %all-gather = bf16[40,16,512]{2,1,0:T(8,128)(2,1)S(1)} all-gather(bf16[5,16,512]{2,1,0:T(8,128)(2,1)S(1)} %collective-permute-done.2), channel_id=2, replica_groups={{0,1,8,9,16,17,24,25},{2,3,10,11,18,19,26,27},{4,5,12,13,20,21,28,29},{..., dimensions={0}, use_global_device_ids=true | all-gather | bytes 737280 | tf_op jit(solution)/shard_map/all_gather | solution.py:436
  29.6 0.0 copy-done.1
  29.6 0.0 copy-start.4
  29.6 1.2 %copy-done.4 = bf16[1920,256]{1,0:T(8,128)(2,1)S(1)} copy-done((bf16[1920,256]{1,0:T(8,128)(2,1)S(1)}, bf16[1920,256]{1,0:T(8,128)(2,1)}, u32[]{:S(2)}) %copy-start.4) | copy-done | bytes 983064
  30.8 16.5 %shard_map.98 = (bf16[8,8,64,512]{3,2,1,0:T(8,128)(2,1)}, f32[8,2,64,512]{3,2,1,0:T(8,128)S(1)}, bf16[2,64,512]{2,1,0:T(8,128)(2,1)S(1)}, f32[8,8,128]{2,1,0:T(8,128)S(1)}) custom-call(bf16[8,5,16,512]{3,2,1,0:T(8,128)(2,1)S(1)} %bitcast.14, f32[8,64,512]{2,1,0:T(8,128)S(1)} %bitcast.11, f32[8,64,512]{2,1,0:T(8,128)S(1)} %bitcast.8, ...), custom_call_target="tpu_custom_call" | custom-call | flops 20000000000 | bytes 16777216 | tf_op jit(solution)/shard_map/pallas_call | solution.py:245
  47.4 0.0 collective-permute-done.one_ref
  47.4 0.0 collective-permute-done.1.two_ref
  47.4 0.0 copy-start.6
  47.4 0.0 copy-start.7
  47.4 5.6 %shard_map.99 = (bf16[8,8,64,512]{3,2,1,0:T(8,128)(2,1)}, f32[8,128]{1,0:T(8,128)S(1)}) custom-call(bf16[8,64,512]{2,1,0:T(8,128)(2,1)} %collective-permute-done.one_ref, bf16[8,64,512]{2,1,0:T(8,128)(2,1)} %collective-permute-done.1.two_ref, bf16[2,64,512]{2,1,0:T(8,128)(2,1)S(1)} %get-tuple-element.21.slope_ref, ...), custom_call_target="tpu_custom_call", output_to_operand_aliasing={{0}: (7, {})} | custom-call | flops 2000000000 | bytes 1048576 | tf_op jit(solution)/shard_map/pallas_call | solution.py:353
  53.0 21.8 %collective-permute-start.3 = (f32[8,128]{1,0:T(8,128)S(1)}, f32[8,128]{1,0:T(8,128)S(1)}, u32[]{:S(2)}, u32[]{:S(2)}) collective-permute-start(f32[8,128]{1,0:T(8,128)S(1)} %get-tuple-element.27), channel_id=1, source_target_pairs={{0,32},{32,0},{64,96},{96,64},{128,160},{160,128},{192,224},{224,1... | collective-permute-start | bytes 12296 | tf_op jit(solution)/shard_map/ppermute | solution.py:451
  74.8 1.6 %collective-permute-done.3 = f32[8,128]{1,0:T(8,128)S(1)} collective-permute-done((f32[8,128]{1,0:T(8,128)S(1)}, f32[8,128]{1,0:T(8,128)S(1)}, u32[]{:S(2)}, u32[]{:S(2)}) %collective-permute-start.3) | collective-permute-done | bytes 4128 | tf_op jit(solution)/shard_map/ppermute | solution.py:451
  76.3 1.5 %collective-permute-start.4 = (f32[8,128]{1,0:T(8,128)S(1)}, f32[8,128]{1,0:T(8,128)S(1)}, u32[]{:S(2)}, u32[]{:S(2)}) collective-permute-start(f32[8,128]{1,0:T(8,128)S(1)} %add.15), channel_id=1, source_target_pairs={{0,64},{32,96},{64,0},{96,32},{128,192},{160,224},{192,128},{224,1... | collective-permute-start | bytes 12296 | tf_op jit(solution)/shard_map/ppermute | solution.py:453
  77.8 5.6 %collective-permute-start.5 = (f32[8,128]{1,0:T(8,128)S(1)}, f32[8,128]{1,0:T(8,128)S(1)}, u32[]{:S(2)}, u32[]{:S(2)}) collective-permute-start(f32[8,128]{1,0:T(8,128)S(1)} %add.15), channel_id=1, source_target_pairs={{0,128},{32,160},{64,192},{96,224},{128,0},{160,32},{192,64},{224,... | collective-permute-start | bytes 12296 | tf_op jit(solution)/shard_map/ppermute | solution.py:453
  83.4 0.0 collective-permute-start.6
  83.4 0.0 copy-done.6
  83.4 0.2 select_reduce_fusion
  83.6 0.0 collective-permute-done.4
  83.6 1.4 %collective-permute-done.5 = f32[8,128]{1,0:T(8,128)S(1)} collective-permute-done((f32[8,128]{1,0:T(8,128)S(1)}, f32[8,128]{1,0:T(8,128)S(1)}, u32[]{:S(2)}, u32[]{:S(2)}) %collective-permute-start.5) | collective-permute-done | bytes 4128 | tf_op jit(solution)/shard_map/ppermute | solution.py:453
  85.0 3.2 %collective-permute-done.6 = f32[8,128]{1,0:T(8,128)S(1)} collective-permute-done((f32[8,128]{1,0:T(8,128)S(1)}, f32[8,128]{1,0:T(8,128)S(1)}, u32[]{:S(2)}, u32[]{:S(2)}) %collective-permute-start.6) | collective-permute-done | bytes 4128 | tf_op jit(solution)/shard_map/ppermute | solution.py:453
  88.2 0.1 add_reduce_fusion
  88.3 0.5 multiply_add_fusion
  (8 shorter events, 0.0 us)
Async XLA Ops:
  0.6 29.0 %copy-start = (f32[8,512,64]{1,2,0:T(8,128)S(1)}, f32[8,512,64]{1,2,0:T(8,128)}, u32[]{:S(2)}) copy-start(f32[8,512,64]{1,2,0:T(8,128)} %param.9) | copy-start | bytes 3145732
  0.6 29.0 %copy-start.1 = (f32[8,512,64]{1,2,0:T(8,128)S(1)}, f32[8,512,64]{1,2,0:T(8,128)}, u32[]{:S(2)}) copy-start(f32[8,512,64]{1,2,0:T(8,128)} %param.8) | copy-start | bytes 3145732
  0.7 29.0 %copy-start.2 = (s32[8,512,64]{1,2,0:T(8,128)S(1)}, s32[8,512,64]{1,2,0:T(8,128)}, u32[]{:S(2)}) copy-start(s32[8,512,64]{1,2,0:T(8,128)} %param.12) | copy-start | bytes 3145732
  0.7 29.0 %copy-start.5 = (f32[64]{0:T(128)S(1)}, f32[64]{0:T(128)}, u32[]{:S(2)}) copy-start(f32[64]{0:T(128)} %param.11) | copy-start | bytes 772
  4.0 13.6 %collective-permute-start.2 = (bf16[5,16,512]{2,1,0:T(8,128)(2,1)}, bf16[5,16,512]{2,1,0:T(8,128)(2,1)S(1)}, u32[]{:S(2)}, u32[]{:S(2)}) collective-permute-start(bf16[5,16,512]{2,1,0:T(8,128)(2,1)} %get-tuple-element.17.refs_2_), channel_id=1, source_target_pairs={{0,32},{2,34},{4,36},{6,38},{8,40},{10,42},{12,44},{14,46},{16,48}... | collective-permute-start | bytes 245768 | tf_op jit(solution)/shard_map/ppermute | solution.py:431
  13.1 34.2 %collective-permute-start = (bf16[8,64,512]{2,1,0:T(8,128)(2,1)}, bf16[8,64,512]{2,1,0:T(8,128)(2,1)}, u32[]{:S(2)}, u32[]{:S(2)}) collective-permute-start(bf16[8,64,512]{2,1,0:T(8,128)(2,1)} %get-tuple-element.18), channel_id=1, source_target_pairs={{0,32},{32,0},{64,96},{96,64},{128,160},{160,128},{192,224},{224,1... | collective-permute-start | bytes 1572872 | tf_op jit(solution)/shard_map/ppermute | solution.py:434
  13.2 34.1 %collective-permute-start.1 = (bf16[8,64,512]{2,1,0:T(8,128)(2,1)}, bf16[8,64,512]{2,1,0:T(8,128)(2,1)}, u32[]{:S(2)}, u32[]{:S(2)}) collective-permute-start(bf16[8,64,512]{2,1,0:T(8,128)(2,1)} %get-tuple-element.19), channel_id=1, source_target_pairs={{32,64},{64,32},{96,128},{128,96},{160,192},{192,160},{33,65},{65,... | collective-permute-start | bytes 1572872 | tf_op jit(solution)/shard_map/ppermute | solution.py:435
  29.6 1.2 %copy-start.4 = (bf16[1920,256]{1,0:T(8,128)(2,1)S(1)}, bf16[1920,256]{1,0:T(8,128)(2,1)}, u32[]{:S(2)}) copy-start(bf16[1920,256]{1,0:T(8,128)(2,1)} %get-tuple-element.20.bands_ref) | copy-start | bytes 2949124
  30.8 16.5 %copy-start.3 = (bf16[2,192,64]{2,1,0:T(8,128)(2,1)S(1)}, bf16[2,192,64]{2,1,0:T(8,128)(2,1)}, u32[]{:S(2)}) copy-start(bf16[2,192,64]{2,1,0:T(8,128)(2,1)} %get-tuple-element.23.weight_ref) | copy-start | bytes 147460
  47.4 36.0 %copy-start.6 = (f32[4096]{0:T(1024)S(1)}, f32[4096]{0:T(1024)}, u32[]{:S(2)}) copy-start(f32[4096]{0:T(1024)} %param.15) | copy-start | bytes 49156
  47.4 36.0 %copy-start.7 = (s32[8]{0:T(128)S(1)}, s32[8]{0:T(128)}, u32[]{:S(2)}) copy-start(s32[8]{0:T(128)} %param.14) | copy-start | bytes 100
  53.0 23.3 %collective-permute-start.3 = (f32[8,128]{1,0:T(8,128)S(1)}, f32[8,128]{1,0:T(8,128)S(1)}, u32[]{:S(2)}, u32[]{:S(2)}) collective-permute-start(f32[8,128]{1,0:T(8,128)S(1)} %get-tuple-element.27), channel_id=1, source_target_pairs={{0,32},{32,0},{64,96},{96,64},{128,160},{160,128},{192,224},{224,1... | collective-permute-start | bytes 12296 | tf_op jit(solution)/shard_map/ppermute | solution.py:451
  76.3 7.3 %collective-permute-start.4 = (f32[8,128]{1,0:T(8,128)S(1)}, f32[8,128]{1,0:T(8,128)S(1)}, u32[]{:S(2)}, u32[]{:S(2)}) collective-permute-start(f32[8,128]{1,0:T(8,128)S(1)} %add.15), channel_id=1, source_target_pairs={{0,64},{32,96},{64,0},{96,32},{128,192},{160,224},{192,128},{224,1... | collective-permute-start | bytes 12296 | tf_op jit(solution)/shard_map/ppermute | solution.py:453
  77.8 7.2 %collective-permute-start.5 = (f32[8,128]{1,0:T(8,128)S(1)}, f32[8,128]{1,0:T(8,128)S(1)}, u32[]{:S(2)}, u32[]{:S(2)}) collective-permute-start(f32[8,128]{1,0:T(8,128)S(1)} %add.15), channel_id=1, source_target_pairs={{0,128},{32,160},{64,192},{96,224},{128,0},{160,32},{192,64},{224,... | collective-permute-start | bytes 12296 | tf_op jit(solution)/shard_map/ppermute | solution.py:453
  83.4 4.8 %collective-permute-start.6 = (f32[8,128]{1,0:T(8,128)S(1)}, f32[8,128]{1,0:T(8,128)S(1)}, u32[]{:S(2)}, u32[]{:S(2)}) collective-permute-start(f32[8,128]{1,0:T(8,128)S(1)} %add.15), channel_id=1, source_target_pairs={{0,192},{32,224},{64,128},{96,160},{128,64},{160,96},{192,0},{224,... | collective-permute-start | bytes 12296 | tf_op jit(solution)/shard_map/ppermute | solution.py:453

commit v7 on v5

--- a/solution.py
+++ b/solution.py
@@ -37,51 +37,35 @@
     return high, (value - high.astype(F32)).astype(BF16)
 
 
-def payload_kernel(
-    lanes, center_ref, radius_ref, status_ref, box_ref, center_box, radius_box, status_box, sems
+def send_kernel(
+    lanes,
+    center_ref,
+    radius_ref,
+    status_ref,
+    coeff_ref,
+    box_ref,
+    first_ref,
+    second_ref,
+    held_ref,
+    center_box,
+    radius_box,
+    status_box,
+    box_sems,
+    sems,
 ):
-    rows = center_ref.shape[0]
+    specs, rows = coeff_ref.shape[:2]
     part = box_ref.shape[1]
     me = lax.axis_index("specs")
     up = 1 - lax.rem(me, 2)
     here = pl.ds(pl.multiple_of(me // (2 * lanes) * part, part), part)
     two = pl.ds(up * (rows - 2), 2)
     one = pl.ds(up * (rows - 1), 1)
-    copies = [
-        pltpu.make_async_copy(center_ref.at[two, here], center_box, sems.at[0]),
-        pltpu.make_async_copy(radius_ref.at[two, here], radius_box, sems.at[1]),
-        pltpu.make_async_copy(status_ref.at[one, here], status_box, sems.at[2]),
+    odd = lax.rem(lax.axis_index("rows"), 2)
+    boxes = [
+        pltpu.make_async_copy(center_ref.at[two, here], center_box, box_sems.at[0]),
+        pltpu.make_async_copy(radius_ref.at[two, here], radius_box, box_sems.at[1]),
+        pltpu.make_async_copy(status_ref.at[one, here], status_box, box_sems.at[2]),
     ]
-    for copy in copies:
-        copy.start()
-    for copy in copies:
-        copy.wait()
-    box_ref[0:2] = center_box[...].astype(BF16)
-    box_ref[2:4] = radius_box[...].astype(BF16)
-    box_ref[4:5] = status_box[...].astype(F32).astype(BF16)
-
-
-def payload_pass(lanes, center, radius, status):
-    rows, channels, columns = center.shape
-    part = channels * 2 // SHARE
-    return pl.pallas_call(
-        functools.partial(payload_kernel, lanes),
-        out_shape=jax.ShapeDtypeStruct((UNITS, part, columns), BF16),
-        in_specs=[pl.BlockSpec(memory_space=pl.ANY)] * 3,
-        out_specs=pl.BlockSpec(memory_space=pltpu.VMEM),
-        scratch_shapes=[
-            pltpu.VMEM((2, part, columns), F32),
-            pltpu.VMEM((2, part, columns), F32),
-            pltpu.VMEM((1, part, columns), jnp.int32),
-            pltpu.SemaphoreType.DMA((3,)),
-        ],
-        cost_estimate=pl.CostEstimate(flops=0, bytes_accessed=1 << 20, transcendentals=0),
-    )(center, radius, status)
-
-
-def send_kernel(coeff_ref, _, first_ref, second_ref, held_ref, sems):
-    specs, rows = coeff_ref.shape[:2]
-    odd = lax.rem(lax.axis_index("rows"), 2)
     todo = [
         (k, s, h * (rows - 1), ref)
         for k, (h, ref) in enumerate(((1 - odd, first_ref), (odd, second_ref)))
@@ -95,8 +79,13 @@
         pltpu.make_async_copy(held_ref.at[k, s], ref.at[s], sems.at[1, k, s])
         for k, s, _, ref in todo
     ]
-    for read in reads:
-        read.start()
+    for copy in boxes + reads:
+        copy.start()
+    for copy in boxes:
+        copy.wait()
+    box_ref[0:2] = center_box[...].astype(BF16)
+    box_ref[2:4] = radius_box[...].astype(BF16)
+    box_ref[4:5] = status_box[...].astype(F32).astype(BF16)
     for read, write in zip(reads, writes):
         read.wait()
         write.start()
@@ -104,21 +93,40 @@
         write.wait()
 
 
-def send_pass(coeffs, after):
+def send_pass(lanes, center, radius, status, coeffs):
     specs, rows, channels, columns = coeffs.shape
+    part = channels * 2 // SHARE
     edge = jax.ShapeDtypeStruct((specs, channels, columns), BF16)
     anywhere = pl.BlockSpec(memory_space=pl.ANY)
     return pl.pallas_call(
-        send_kernel,
-        out_shape=(edge, edge),
-        in_specs=[anywhere, anywhere],
-        out_specs=(anywhere, anywhere),
+        functools.partial(send_kernel, lanes),
+        out_shape=(jax.ShapeDtypeStruct((UNITS, part, columns), BF16), edge, edge),
+        in_specs=[anywhere] * 4,
+        out_specs=(pl.BlockSpec(memory_space=pltpu.VMEM), anywhere, anywhere),
         scratch_shapes=[
             pltpu.VMEM((2, specs, channels, columns), BF16),
+            pltpu.VMEM((2, part, columns), F32),
+            pltpu.VMEM((2, part, columns), F32),
+            pltpu.VMEM((1, part, columns), jnp.int32),
+            pltpu.SemaphoreType.DMA((3,)),
             pltpu.SemaphoreType.DMA((2, 2, specs)),
         ],
         cost_estimate=pl.CostEstimate(flops=0, bytes_accessed=4 << 20, transcendentals=0),
-    )(coeffs, after)
+    )(center, radius, status, coeffs)
+
+
+def later_pass(first, second, box):
+    def kernel(*refs):
+        pass
+
+    anywhere = pl.BlockSpec(memory_space=pl.ANY)
+    return pl.pallas_call(
+        kernel,
+        out_shape=tuple(jax.ShapeDtypeStruct(a.shape, a.dtype) for a in (first, second)),
+        in_specs=[anywhere] * 3,
+        out_specs=(anywhere, anywhere),
+        input_output_aliases={0: 0, 1: 1},
+    )(first, second, box)
 
 
 def main_kernel(
@@ -300,12 +308,14 @@
             pre = (halo_ref[s].astype(F32) * slope_ref[e].astype(F32)).astype(BF16)
             value = edge_ref[s, e] + spread_columns(mul(weight_ref[e], pre), columns)
             done_ref[s, k] = value.astype(BF16)
-            store(s, k).start()
             terms = jnp.abs(value) * radius_ref[0]
             terms = jnp.sum(terms.reshape(channels // 8, 8, columns), axis=0)
             for m in range(columns // 128):
                 total = total - terms[:, m * 128 : (m + 1) * 128]
         sum_ref[s : s + 1, :] = jnp.sum(total, axis=0, keepdims=True)
+    for s in range(specs):
+        for k in range(2):
+            store(s, k).start()
     for s in range(specs):
         for k in range(2):
             store(s, k).wait()
@@ -396,8 +406,7 @@
     coeffs = jnp.swapaxes(out_coeffs, 2, 3)
 
     lanes = groups // SHARE
-    mine = payload_pass(lanes, center, radius, status)
-    center, radius, status, mine = lax.optimization_barrier((center, radius, status, mine))
+    mine, one, two = send_pass(lanes, center, radius, status, coeffs)
     moves = []
     for r in range(count):
         for s in range(groups):
@@ -405,7 +414,7 @@
             if 0 <= other < count:
                 moves.append((r * groups + s, other * groups + s))
     box = lax.ppermute(mine, ("rows", "specs"), moves)
-    one, two = send_pass(coeffs, mine)
+    one, two = later_pass(one, two, mine)
     pairs = [(i, i + 1) for i in range(count - 1)]
     one = lax.ppermute(one, "rows", [m for p in pairs[::2] for m in (p, p[::-1])])
     two = lax.ppermute(two, "rows", [m for p in pairs[1::2] for m in (p, p[::-1])])

time: 86.3 us -> 88.1 us (1.021)
  the two profiles are of different devices: /device:TPU:56 before, /device:TPU:16 now
where the time goes in v7:
time: 88.1 us; the launch traced here: 87.6 us
  starting transfers between devices  39.5 us (45%)
  Pallas kernels  27 us (31%)
  blocking collectives  12 us (14%)
  waiting for transfers between devices  6.19 us (7%)
  local copies, waits for them, and re-layouts  1.23 us (1%)
  other arithmetic  0.93 us (1%)
    ppermute x1, starting transfers between devices, per_device(): lax.ppermute(partial, 'rows', [(i, i ^ 1) for i in range(count)])  21.8 us
    pallas_call x1, Pallas kernels, main_pass(): pl.pallas_call(main_kernel, grid=(specs,), out_shape=(jax.ShapeDtypeStruc...  16.4 us
    all_gather x1, blocking collectives, per_device(): lax.all_gather(box, 'specs', axis_index_groups=[[(k * lanes + z) * 2 + e...  12 us
    ppermute x1, starting transfers between devices, per_device(): box = lax.ppermute(mine, ('rows', 'specs'), moves)  9.1 us
    ppermute x3, starting transfers between devices, per_device(): lax.ppermute(partial, 'rows', [(i, i ^ step) for i in range(count)])  7.04 us
    ppermute x3, waiting for transfers between devices, per_device(): lax.ppermute(partial, 'rows', [(i, i ^ step) for i in range(count)])  4.59 us
    pallas_call x1, Pallas kernels, edge_pass(): pl.pallas_call(edge_kernel, out_shape=(jax.ShapeDtypeStruct(out.shape, BF...  4.37 us
    pallas_call x1, Pallas kernels, send_pass(): pl.pallas_call(functools.partial(send_kernel, lanes), out_shape=(jax.Shap...  3.34 us
  transfers between devices with their start and end apart: 7, of which 3 were waited for; matrix products, arithmetic and copies ran while one was open for 0% of the time, Pallas kernels for 22%

profile of v7, /device:TPU:16, one launch (start us, length us, event | category | flops | bytes accessed | tf_op | source)
XLA Modules:
  0.0 87.6 jit_solution(2333279421006116575)
XLA Ops:
  0.6 0.0 copy-start
  0.6 0.0 copy-start.1
  0.7 0.0 copy-start.2
  0.7 0.0 copy-start.5
  0.7 3.3 %shard_map.95 = (bf16[5,16,512]{2,1,0:T(8,128)(2,1)}, bf16[8,64,512]{2,1,0:T(8,128)(2,1)}, bf16[8,64,512]{2,1,0:T(8,128)(2,1)}) custom-call(f32[8,64,512]{2,1,0:T(8,128)} %bitcast.13, f32[8,64,512]{2,1,0:T(8,128)} %bitcast.9, s32[8,64,512]{2,1,0:T(8,128)} %bitcast.15, bf16[8,8,64,512]{3,2,1,0:T(8,128)(2,1)} %bitcast.19), custom_call_target="tpu_custom_call" | custom-call | bytes 4194304 | tf_op jit(solution)/shard_map/pallas_call | solution.py:101
  4.0 9.1 %collective-permute-start.2 = (bf16[5,16,512]{2,1,0:T(8,128)(2,1)}, bf16[5,16,512]{2,1,0:T(8,128)(2,1)S(1)}, u32[]{:S(2)}, u32[]{:S(2)}) collective-permute-start(bf16[5,16,512]{2,1,0:T(8,128)(2,1)} %get-tuple-element.17.refs_2_), channel_id=1, source_target_pairs={{0,32},{2,34},{4,36},{6,38},{8,40},{10,42},{12,44},{14,46},{16,48}... | collective-permute-start | bytes 245768 | tf_op jit(solution)/shard_map/ppermute | solution.py:416
  13.1 0.1 collective-permute-start
  13.2 1.5 %collective-permute-start.1 = (bf16[8,64,512]{2,1,0:T(8,128)(2,1)}, bf16[8,64,512]{2,1,0:T(8,128)(2,1)}, u32[]{:S(2)}, u32[]{:S(2)}) collective-permute-start(bf16[8,64,512]{2,1,0:T(8,128)(2,1)} %get-tuple-element.19), channel_id=1, source_target_pairs={{32,64},{64,32},{96,128},{128,96},{160,192},{192,160},{33,65},{65,... | collective-permute-start | bytes 1572872 | tf_op jit(solution)/shard_map/ppermute | solution.py:420
  14.7 2.9 %shard_map.97 = (bf16[1920,256]{1,0:T(8,128)(2,1)}, bf16[2,192,64]{2,1,0:T(8,128)(2,1)}) custom-call(f32[3,3,64,64]{3,2,1,0:T(8,128)} %weight_ref.1), custom_call_target="tpu_custom_call" | custom-call | tf_op jit(solution)/shard_map/pallas_call | solution.py:391
  17.6 0.1 pad_add_fusion.sites_ref
  17.7 0.0 collective-permute-done.2
  17.7 12.0 %all-gather = bf16[40,16,512]{2,1,0:T(8,128)(2,1)S(1)} all-gather(bf16[5,16,512]{2,1,0:T(8,128)(2,1)S(1)} %collective-permute-done.2), channel_id=2, replica_groups={{0,1,8,9,16,17,24,25},{2,3,10,11,18,19,26,27},{4,5,12,13,20,21,28,29},{..., dimensions={0}, use_global_device_ids=true | all-gather | bytes 737280 | tf_op jit(solution)/shard_map/all_gather | solution.py:421
  29.7 0.0 copy-done
  29.7 0.0 copy-start.4
  29.7 1.2 %copy-done.4 = bf16[1920,256]{1,0:T(8,128)(2,1)S(1)} copy-done((bf16[1920,256]{1,0:T(8,128)(2,1)S(1)}, bf16[1920,256]{1,0:T(8,128)(2,1)}, u32[]{:S(2)}) %copy-start.4) | copy-done | bytes 983064
  30.9 16.4 %shard_map.98 = (bf16[8,8,64,512]{3,2,1,0:T(8,128)(2,1)}, f32[8,2,64,512]{3,2,1,0:T(8,128)S(1)}, bf16[2,64,512]{2,1,0:T(8,128)(2,1)S(1)}, f32[8,8,128]{2,1,0:T(8,128)S(1)}) custom-call(bf16[8,5,16,512]{3,2,1,0:T(8,128)(2,1)S(1)} %bitcast.17, f32[8,64,512]{2,1,0:T(8,128)S(1)} %bitcast.14, f32[8,64,512]{2,1,0:T(8,128)S(1)} %bitcast.10, ...), custom_call_target="tpu_custom_call" | custom-call | flops 20000000000 | bytes 16777216 | tf_op jit(solution)/shard_map/pallas_call | solution.py:245
  47.3 0.0 collective-permute-done.one_ref
  47.3 0.0 collective-permute-done.1.two_ref
  47.3 0.0 copy-start.6
  47.4 0.0 copy-start.7
  47.4 4.4 %shard_map.99 = (bf16[8,8,64,512]{3,2,1,0:T(8,128)(2,1)}, f32[8,128]{1,0:T(8,128)S(1)}) custom-call(s32[2]{0:T(128)S(1)} %pad_add_fusion.sites_ref, bf16[8,64,512]{2,1,0:T(8,128)(2,1)} %collective-permute-done.one_ref, bf16[8,64,512]{2,1,0:T(8,128)(2,1)} %collective-permute-done.1.two_ref, ...), custom_call_target="tpu_custom_call", output_to_operand_aliasing={{0}: (9, {})} | custom-call | flops 2000000000 | bytes 1048576 | tf_op jit(solution)/shard_map/pallas_call | solution.py:327
  51.7 21.8 %collective-permute-start.3 = (f32[8,128]{1,0:T(8,128)S(1)}, f32[8,128]{1,0:T(8,128)S(1)}, u32[]{:S(2)}, u32[]{:S(2)}) collective-permute-start(f32[8,128]{1,0:T(8,128)S(1)} %get-tuple-element.27), channel_id=1, source_target_pairs={{0,32},{32,0},{64,96},{96,64},{128,160},{160,128},{192,224},{224,1... | collective-permute-start | bytes 12296 | tf_op jit(solution)/shard_map/ppermute | solution.py:438
  73.5 1.6 %collective-permute-done.3 = f32[8,128]{1,0:T(8,128)S(1)} collective-permute-done((f32[8,128]{1,0:T(8,128)S(1)}, f32[8,128]{1,0:T(8,128)S(1)}, u32[]{:S(2)}, u32[]{:S(2)}) %collective-permute-start.3) | collective-permute-done | bytes 4128 | tf_op jit(solution)/shard_map/ppermute | solution.py:438
  75.1 1.5 %collective-permute-start.4 = (f32[8,128]{1,0:T(8,128)S(1)}, f32[8,128]{1,0:T(8,128)S(1)}, u32[]{:S(2)}, u32[]{:S(2)}) collective-permute-start(f32[8,128]{1,0:T(8,128)S(1)} %add.15), channel_id=1, source_target_pairs={{0,64},{32,96},{64,0},{96,32},{128,192},{160,224},{192,128},{224,1... | collective-permute-start | bytes 12296 | tf_op jit(solution)/shard_map/ppermute | solution.py:440
  76.6 5.5 %collective-permute-start.5 = (f32[8,128]{1,0:T(8,128)S(1)}, f32[8,128]{1,0:T(8,128)S(1)}, u32[]{:S(2)}, u32[]{:S(2)}) collective-permute-start(f32[8,128]{1,0:T(8,128)S(1)} %add.15), channel_id=1, source_target_pairs={{0,128},{32,160},{64,192},{96,224},{128,0},{160,32},{192,64},{224,... | collective-permute-start | bytes 12296 | tf_op jit(solution)/shard_map/ppermute | solution.py:440
  82.2 0.0 collective-permute-start.6
  82.2 0.2 select_reduce_fusion
  82.4 0.0 collective-permute-done.4
  82.4 1.4 %collective-permute-done.5 = f32[8,128]{1,0:T(8,128)S(1)} collective-permute-done((f32[8,128]{1,0:T(8,128)S(1)}, f32[8,128]{1,0:T(8,128)S(1)}, u32[]{:S(2)}, u32[]{:S(2)}) %collective-permute-start.5) | collective-permute-done | bytes 4128 | tf_op jit(solution)/shard_map/ppermute | solution.py:440
  83.8 3.2 %collective-permute-done.6 = f32[8,128]{1,0:T(8,128)S(1)} collective-permute-done((f32[8,128]{1,0:T(8,128)S(1)}, f32[8,128]{1,0:T(8,128)S(1)}, u32[]{:S(2)}, u32[]{:S(2)}) %collective-permute-start.6) | collective-permute-done | bytes 4128 | tf_op jit(solution)/shard_map/ppermute | solution.py:440
  87.0 0.1 add_reduce_fusion
  87.1 0.5 multiply_add_fusion
  (9 shorter events, 0.0 us)
Async XLA Ops:
  0.6 29.1 %copy-start = (f32[8,512,64]{1,2,0:T(8,128)S(1)}, f32[8,512,64]{1,2,0:T(8,128)}, u32[]{:S(2)}) copy-start(f32[8,512,64]{1,2,0:T(8,128)} %param.9) | copy-start | bytes 3145732
  0.6 29.1 %copy-start.1 = (f32[8,512,64]{1,2,0:T(8,128)S(1)}, f32[8,512,64]{1,2,0:T(8,128)}, u32[]{:S(2)}) copy-start(f32[8,512,64]{1,2,0:T(8,128)} %param.8) | copy-start | bytes 3145732
  0.7 29.1 %copy-start.2 = (s32[8,512,64]{1,2,0:T(8,128)S(1)}, s32[8,512,64]{1,2,0:T(8,128)}, u32[]{:S(2)}) copy-start(s32[8,512,64]{1,2,0:T(8,128)} %param.12) | copy-start | bytes 3145732
  0.7 29.0 %copy-start.5 = (f32[64]{0:T(128)S(1)}, f32[64]{0:T(128)}, u32[]{:S(2)}) copy-start(f32[64]{0:T(128)} %param.11) | copy-start | bytes 772
  4.0 13.7 %collective-permute-start.2 = (bf16[5,16,512]{2,1,0:T(8,128)(2,1)}, bf16[5,16,512]{2,1,0:T(8,128)(2,1)S(1)}, u32[]{:S(2)}, u32[]{:S(2)}) collective-permute-start(bf16[5,16,512]{2,1,0:T(8,128)(2,1)} %get-tuple-element.17.refs_2_), channel_id=1, source_target_pairs={{0,32},{2,34},{4,36},{6,38},{8,40},{10,42},{12,44},{14,46},{16,48}... | collective-permute-start | bytes 245768 | tf_op jit(solution)/shard_map/ppermute | solution.py:416
  13.1 34.2 %collective-permute-start = (bf16[8,64,512]{2,1,0:T(8,128)(2,1)}, bf16[8,64,512]{2,1,0:T(8,128)(2,1)}, u32[]{:S(2)}, u32[]{:S(2)}) collective-permute-start(bf16[8,64,512]{2,1,0:T(8,128)(2,1)} %get-tuple-element.18), channel_id=1, source_target_pairs={{0,32},{32,0},{64,96},{96,64},{128,160},{160,128},{192,224},{224,1... | collective-permute-start | bytes 1572872 | tf_op jit(solution)/shard_map/ppermute | solution.py:419
  13.2 34.1 %collective-permute-start.1 = (bf16[8,64,512]{2,1,0:T(8,128)(2,1)}, bf16[8,64,512]{2,1,0:T(8,128)(2,1)}, u32[]{:S(2)}, u32[]{:S(2)}) collective-permute-start(bf16[8,64,512]{2,1,0:T(8,128)(2,1)} %get-tuple-element.19), channel_id=1, source_target_pairs={{32,64},{64,32},{96,128},{128,96},{160,192},{192,160},{33,65},{65,... | collective-permute-start | bytes 1572872 | tf_op jit(solution)/shard_map/ppermute | solution.py:420
  29.7 1.2 %copy-start.4 = (bf16[1920,256]{1,0:T(8,128)(2,1)S(1)}, bf16[1920,256]{1,0:T(8,128)(2,1)}, u32[]{:S(2)}) copy-start(bf16[1920,256]{1,0:T(8,128)(2,1)} %get-tuple-element.20.bands_ref) | copy-start | bytes 2949124
  30.9 16.4 %copy-start.3 = (bf16[2,192,64]{2,1,0:T(8,128)(2,1)S(1)}, bf16[2,192,64]{2,1,0:T(8,128)(2,1)}, u32[]{:S(2)}) copy-start(bf16[2,192,64]{2,1,0:T(8,128)(2,1)} %get-tuple-element.23.weight_ref) | copy-start | bytes 147460
  47.3 34.8 %copy-start.6 = (f32[4096]{0:T(1024)S(1)}, f32[4096]{0:T(1024)}, u32[]{:S(2)}) copy-start(f32[4096]{0:T(1024)} %param.15) | copy-start | bytes 49156
  47.4 34.8 %copy-start.7 = (s32[8]{0:T(128)S(1)}, s32[8]{0:T(128)}, u32[]{:S(2)}) copy-start(s32[8]{0:T(128)} %param.14) | copy-start | bytes 100
  51.7 23.4 %collective-permute-start.3 = (f32[8,128]{1,0:T(8,128)S(1)}, f32[8,128]{1,0:T(8,128)S(1)}, u32[]{:S(2)}, u32[]{:S(2)}) collective-permute-start(f32[8,128]{1,0:T(8,128)S(1)} %get-tuple-element.27), channel_id=1, source_target_pairs={{0,32},{32,0},{64,96},{96,64},{128,160},{160,128},{192,224},{224,1... | collective-permute-start | bytes 12296 | tf_op jit(solution)/shard_map/ppermute | solution.py:438
  75.1 7.3 %collective-permute-start.4 = (f32[8,128]{1,0:T(8,128)S(1)}, f32[8,128]{1,0:T(8,128)S(1)}, u32[]{:S(2)}, u32[]{:S(2)}) collective-permute-start(f32[8,128]{1,0:T(8,128)S(1)} %add.15), channel_id=1, source_target_pairs={{0,64},{32,96},{64,0},{96,32},{128,192},{160,224},{192,128},{224,1... | collective-permute-start | bytes 12296 | tf_op jit(solution)/shard_map/ppermute | solution.py:440
  76.6 7.2 %collective-permute-start.5 = (f32[8,128]{1,0:T(8,128)S(1)}, f32[8,128]{1,0:T(8,128)S(1)}, u32[]{:S(2)}, u32[]{:S(2)}) collective-permute-start(f32[8,128]{1,0:T(8,128)S(1)} %add.15), channel_id=1, source_target_pairs={{0,128},{32,160},{64,192},{96,224},{128,0},{160,32},{192,64},{224,... | collective-permute-start | bytes 12296 | tf_op jit(solution)/shard_map/ppermute | solution.py:440
  82.2 4.8 %collective-permute-start.6 = (f32[8,128]{1,0:T(8,128)S(1)}, f32[8,128]{1,0:T(8,128)S(1)}, u32[]{:S(2)}, u32[]{:S(2)}) collective-permute-start(f32[8,128]{1,0:T(8,128)S(1)} %add.15), channel_id=1, source_target_pairs={{0,192},{32,224},{64,128},{96,160},{128,64},{160,96},{192,0},{224,... | collective-permute-start | bytes 12296 | tf_op jit(solution)/shard_map/ppermute | solution.py:440

commit v8 on v5

--- a/solution.py
+++ b/solution.py
@@ -278,19 +278,10 @@
     radius_two_ref,
     weight_ref,
     total_ref,
-    _,
-    out_ref,
+    done_ref,
     sum_ref,
-    done_ref,
-    sems,
 ):
     specs, channels, columns = one_ref.shape
-    rows = out_ref.shape[1]
-
-    def store(s, k):
-        row = sites_ref[k] * (rows - 1)
-        return pltpu.make_async_copy(done_ref.at[s, k], out_ref.at[s, row], sems.at[s, k])
-
     for s in range(specs):
         total = total_ref[s]
         for k, (halo_ref, radius_ref) in enumerate(
@@ -300,26 +291,24 @@
             pre = (halo_ref[s].astype(F32) * slope_ref[e].astype(F32)).astype(BF16)
             value = edge_ref[s, e] + spread_columns(mul(weight_ref[e], pre), columns)
             done_ref[s, k] = value.astype(BF16)
-            store(s, k).start()
             terms = jnp.abs(value) * radius_ref[0]
             terms = jnp.sum(terms.reshape(channels // 8, 8, columns), axis=0)
             for m in range(columns // 128):
                 total = total - terms[:, m * 128 : (m + 1) * 128]
         sum_ref[s : s + 1, :] = jnp.sum(total, axis=0, keepdims=True)
-    for s in range(specs):
-        for k in range(2):
-            store(s, k).wait()
-
-
-def edge_pass(sites, one, two, slope, edge, radius, weight, total, out):
-    specs, rows, channels, columns = out.shape
-    whole = lambda a: pl.BlockSpec(a.shape, lambda g, e, n=a.ndim: (0,) * n)
+
+
+def edge_pass(sites, one, two, slope, edge, radius, weight, total):
+    specs, channels, columns = one.shape
+    rows = radius.shape[0]
+    whole = lambda a: pl.BlockSpec(a.shape, lambda g, e, n=len(a.shape): (0,) * n)
+    out = (
+        jax.ShapeDtypeStruct((specs, 2, channels, columns), BF16),
+        jax.ShapeDtypeStruct((specs, 128), F32),
+    )
     return pl.pallas_call(
         edge_kernel,
-        out_shape=(
-            jax.ShapeDtypeStruct(out.shape, BF16),
-            jax.ShapeDtypeStruct((specs, 128), F32),
-        ),
+        out_shape=out,
         grid_spec=pltpu.PrefetchScalarGridSpec(
             num_scalar_prefetch=1,
             grid=(1,),
@@ -332,23 +321,48 @@
                 pl.BlockSpec((1, channels, columns), lambda g, e: (e[1] * (rows - 1), 0, 0)),
                 whole(weight),
                 whole(total),
-                pl.BlockSpec(memory_space=pl.ANY),
             ],
-            out_specs=(
-                pl.BlockSpec(memory_space=pl.ANY),
-                pl.BlockSpec((specs, 128), lambda g, e: (0, 0)),
-            ),
-            scratch_shapes=[
-                pltpu.VMEM((specs, 2, channels, columns), BF16),
-                pltpu.SemaphoreType.DMA((specs, 2)),
-            ],
-        ),
-        input_output_aliases={9: 0},
+            out_specs=tuple(whole(a) for a in out),
+        ),
         compiler_params=pltpu.CompilerParams(vmem_limit_bytes=EDGE_VMEM),
         cost_estimate=pl.CostEstimate(
             flops=EDGE_FLOPS, bytes_accessed=1 << 20, transcendentals=0
         ),
-    )(sites, one, two, slope, edge, radius, radius, weight, total, out)
+    )(sites, one, two, slope, edge, radius, radius, weight, total)
+
+
+def place_kernel(sites_ref, done_ref, _, out_ref, sems):
+    specs = done_ref.shape[0]
+    rows = out_ref.shape[1]
+    copies = [
+        pltpu.make_async_copy(
+            done_ref.at[s, k], out_ref.at[s, sites_ref[k] * (rows - 1)], sems.at[s, k]
+        )
+        for s in range(specs)
+        for k in range(2)
+    ]
+    for copy in copies:
+        copy.start()
+    for copy in copies:
+        copy.wait()
+
+
+def place_pass(sites, done, out):
+    anywhere = pl.BlockSpec(memory_space=pl.ANY)
+    return pl.pallas_call(
+        place_kernel,
+        out_shape=jax.ShapeDtypeStruct(out.shape, BF16),
+        grid_spec=pltpu.PrefetchScalarGridSpec(
+            num_scalar_prefetch=1,
+            grid=(1,),
+            in_specs=[pl.BlockSpec(done.shape, lambda g, e: (0, 0, 0, 0)), anywhere],
+            out_specs=anywhere,
+            scratch_shapes=[pltpu.SemaphoreType.DMA(done.shape[:2])],
+        ),
+        input_output_aliases={2: 0},
+        compiler_params=pltpu.CompilerParams(vmem_limit_bytes=16 << 20),
+        cost_estimate=pl.CostEstimate(flops=0, bytes_accessed=4 << 20, transcendentals=0),
+    )(sites, done, out)
 
 
 def weight_kernel(weight_ref, bands_ref, ends_ref):
@@ -424,7 +438,8 @@
     )
     odd = lax.rem(lax.axis_index("rows"), 2)
     sites = jnp.stack([1 - odd, odd]).astype(jnp.int32)
-    out, partial = edge_pass(sites, one, two, slope, edge, radius, ends, total, out)
+    done, partial = edge_pass(sites, one, two, slope, edge, radius, ends, total)
+    out = place_pass(sites, done, out)
 
     partial = partial + lax.ppermute(partial, "rows", [(i, i ^ 1) for i in range(count)])
     pairs = [partial] + [

time: 86.3 us -> 85.6 us (level)
  waiting for transfers between devices: 9.81 us -> 8.15 us
    ppermute x3, waiting for transfers between devices: 4.59 us -> 2.94 us  [per_device(): lax.ppermute(partial, 'rows', [(i, i ^ step) for i in range(count)])]
    pallas_call x1 -> x2, Pallas kernels: 4.06 us -> 4.93 us  [the longest x1 3.3 us: edge_pass(): pl.pallas_call(edge_kernel, out_shape=out, grid_spec=pltpu.PrefetchScalar...]
  transfers between devices with their start and end apart: 7 -> 7, of which waited for: 4 -> 3; matrix products, arithmetic and copies ran while one was open for 0% -> 0% of each run, Pallas kernels for 25% -> 27%
where the time goes in v8:
time: 85.6 us; the launch traced here: 85.1 us
  starting transfers between devices  32.7 us (38%)
  Pallas kernels  28.1 us (33%)
  blocking collectives  13.2 us (15%)
  waiting for transfers between devices  8.15 us (10%)
  local copies, waits for them, and re-layouts  1.22 us (1%)
  other arithmetic  0.93 us (1%)
    pallas_call x1, Pallas kernels, main_pass(): pl.pallas_call(main_kernel, grid=(specs,), out_shape=(jax.ShapeDtypeStruc...  16.4 us
    ppermute x1, starting transfers between devices, per_device(): lax.ppermute(partial, 'rows', [(i, i ^ 1) for i in range(count)])  14.6 us
    all_gather x1, blocking collectives, per_device(): lax.all_gather(box, 'specs', axis_index_groups=[[(k * lanes + z) * 2 + e...  13.2 us
    ppermute x1, starting transfers between devices, per_device(): box = lax.ppermute(mine, ('rows', 'specs'), moves)  8.2 us
    ppermute x3, starting transfers between devices, per_device(): lax.ppermute(partial, 'rows', [(i, i ^ step) for i in range(count)])  7.79 us
    ppermute x1, waiting for transfers between devices, per_device(): lax.ppermute(one, 'rows', [m for p in pairs[::2] for m in (p, p[::-1])])  3.62 us
    pallas_call x1, Pallas kernels, edge_pass(): pl.pallas_call(edge_kernel, out_shape=out, grid_spec=pltpu.PrefetchScalar...  3.3 us
    ppermute x3, waiting for transfers between devices, per_device(): lax.ppermute(partial, 'rows', [(i, i ^ step) for i in range(count)])  2.94 us
  transfers between devices with their start and end apart: 7, of which 3 were waited for; matrix products, arithmetic and copies ran while one was open for 0% of the time, Pallas kernels for 27%

profile of v8, /device:TPU:56, one launch (start us, length us, event | category | flops | bytes accessed | tf_op | source)
XLA Modules:
  0.0 85.1 jit_solution(13071017179662647454)
XLA Ops:
  0.6 0.0 copy-start
  0.6 0.0 copy-start.1
  0.7 0.0 copy-start.2
  0.7 1.7 %shard_map.95._ = bf16[5,16,512]{2,1,0:T(8,128)(2,1)} custom-call(f32[8,64,512]{2,1,0:T(8,128)} %bitcast.9, f32[8,64,512]{2,1,0:T(8,128)} %bitcast.13, s32[8,64,512]{2,1,0:T(8,128)} %bitcast.11), custom_call_target="tpu_custom_call" | custom-call | bytes 1048576 | tf_op jit(solution)/shard_map/pallas_call | solution.py:67
  2.4 8.2 %collective-permute-start.2 = (bf16[5,16,512]{2,1,0:T(8,128)(2,1)}, bf16[5,16,512]{2,1,0:T(8,128)(2,1)S(1)}, u32[]{:S(2)}, u32[]{:S(2)}) collective-permute-start(bf16[5,16,512]{2,1,0:T(8,128)(2,1)} %shard_map.95._), channel_id=1, source_target_pairs={{0,32},{2,34},{4,36},{6,38},{8,40},{10,42},{12,44},{14,46},{16,48}... | collective-permute-start | bytes 245768 | tf_op jit(solution)/shard_map/ppermute | solution.py:421
  10.6 2.2 %shard_map.96 = (bf16[8,64,512]{2,1,0:T(8,128)(2,1)}, bf16[8,64,512]{2,1,0:T(8,128)(2,1)}) custom-call(bf16[8,8,64,512]{3,2,1,0:T(8,128)(2,1)} %bitcast.20, bf16[5,16,512]{2,1,0:T(8,128)(2,1)} %shard_map.95._), custom_call_target="tpu_custom_call" | custom-call | bytes 4194304 | tf_op jit(solution)/shard_map/pallas_call | solution.py:111
  12.8 0.7 collective-permute-start
  13.5 1.4 %collective-permute-start.1 = (bf16[8,64,512]{2,1,0:T(8,128)(2,1)}, bf16[8,64,512]{2,1,0:T(8,128)(2,1)}, u32[]{:S(2)}, u32[]{:S(2)}) collective-permute-start(bf16[8,64,512]{2,1,0:T(8,128)(2,1)} %get-tuple-element.18), channel_id=1, source_target_pairs={{32,64},{64,32},{96,128},{128,96},{160,192},{192,160},{33,65},{65,... | collective-permute-start | bytes 1572872 | tf_op jit(solution)/shard_map/ppermute | solution.py:425
  14.9 2.9 %shard_map.97 = (bf16[1920,256]{1,0:T(8,128)(2,1)}, bf16[2,192,64]{2,1,0:T(8,128)(2,1)}) custom-call(f32[3,3,64,64]{3,2,1,0:T(8,128)} %weight_ref.1), custom_call_target="tpu_custom_call" | custom-call | tf_op jit(solution)/shard_map/pallas_call | solution.py:395
  17.8 0.1 pad_add_fusion.sites_ref
  17.9 0.0 collective-permute-done.2
  17.9 13.2 %all-gather = bf16[40,16,512]{2,1,0:T(8,128)(2,1)S(1)} all-gather(bf16[5,16,512]{2,1,0:T(8,128)(2,1)S(1)} %collective-permute-done.2), channel_id=2, replica_groups={{0,1,8,9,16,17,24,25},{2,3,10,11,18,19,26,27},{4,5,12,13,20,21,28,29},{..., dimensions={0}, use_global_device_ids=true | all-gather | bytes 737280 | tf_op jit(solution)/shard_map/all_gather | solution.py:426
  31.1 0.0 copy-done.1
  31.1 0.0 copy-start.3
  31.1 1.2 %copy-done.3 = bf16[1920,256]{1,0:T(8,128)(2,1)S(1)} copy-done((bf16[1920,256]{1,0:T(8,128)(2,1)S(1)}, bf16[1920,256]{1,0:T(8,128)(2,1)}, u32[]{:S(2)}) %copy-start.3) | copy-done | bytes 983064
  32.3 16.4 %shard_map.98 = (bf16[8,8,64,512]{3,2,1,0:T(8,128)(2,1)}, f32[8,2,64,512]{3,2,1,0:T(8,128)S(1)}, bf16[2,64,512]{2,1,0:T(8,128)(2,1)S(1)}, f32[8,8,128]{2,1,0:T(8,128)S(1)}) custom-call(bf16[8,5,16,512]{3,2,1,0:T(8,128)(2,1)S(1)} %bitcast.17, f32[8,64,512]{2,1,0:T(8,128)S(1)} %bitcast.10, f32[8,64,512]{2,1,0:T(8,128)S(1)} %bitcast.14, ...), custom_call_target="tpu_custom_call" | custom-call | flops 20000000000 | bytes 16777216 | tf_op jit(solution)/shard_map/pallas_call | solution.py:237
  48.7 3.6 %collective-permute-done.one_ref = bf16[8,64,512]{2,1,0:T(8,128)(2,1)} collective-permute-done((bf16[8,64,512]{2,1,0:T(8,128)(2,1)}, bf16[8,64,512]{2,1,0:T(8,128)(2,1)}, u32[]{:S(2)}, u32[]{:S(2)}) %collective-permute-start) | collective-permute-done | bytes 524320 | tf_op jit(solution)/shard_map/ppermute | solution.py:424
  52.4 0.0 collective-permute-done.1.two_ref
  52.4 3.3 %shard_map.99 = (bf16[8,2,64,512]{3,2,1,0:T(8,128)(2,1)S(1)}, f32[8,128]{1,0:T(8,128)S(1)}) custom-call(s32[2]{0:T(128)S(1)} %pad_add_fusion.sites_ref, bf16[8,64,512]{2,1,0:T(8,128)(2,1)} %collective-permute-done.one_ref, bf16[8,64,512]{2,1,0:T(8,128)(2,1)} %collective-permute-done.1.two_ref, bf16[2,64,512]{2,1,0:T(8,128)(2,1)S(1)} %get-tuple-element.23.slope_ref, ...), custom_call_target="tpu_custom_call" | custom-call | flops 2000000000 | bytes 1048576 | tf_op jit(solution)/shard_map/pallas_call | solution.py:309
  55.7 14.6 %collective-permute-start.3 = (f32[8,128]{1,0:T(8,128)S(1)}, f32[8,128]{1,0:T(8,128)S(1)}, u32[]{:S(2)}, u32[]{:S(2)}) collective-permute-start(f32[8,128]{1,0:T(8,128)S(1)} %get-tuple-element.29), channel_id=1, source_target_pairs={{0,32},{32,0},{64,96},{96,64},{128,160},{160,128},{192,224},{224,1... | collective-permute-start | bytes 12296 | tf_op jit(solution)/shard_map/ppermute | solution.py:444
  70.2 1.6 %collective-permute-done.3 = f32[8,128]{1,0:T(8,128)S(1)} collective-permute-done((f32[8,128]{1,0:T(8,128)S(1)}, f32[8,128]{1,0:T(8,128)S(1)}, u32[]{:S(2)}, u32[]{:S(2)}) %collective-permute-start.3) | collective-permute-done | bytes 4128 | tf_op jit(solution)/shard_map/ppermute | solution.py:444
  71.8 1.5 %collective-permute-start.4 = (f32[8,128]{1,0:T(8,128)S(1)}, f32[8,128]{1,0:T(8,128)S(1)}, u32[]{:S(2)}, u32[]{:S(2)}) collective-permute-start(f32[8,128]{1,0:T(8,128)S(1)} %add.15), channel_id=1, source_target_pairs={{0,64},{32,96},{64,0},{96,32},{128,192},{160,224},{192,128},{224,1... | collective-permute-start | bytes 12296 | tf_op jit(solution)/shard_map/ppermute | solution.py:446
  73.3 6.3 %collective-permute-start.5 = (f32[8,128]{1,0:T(8,128)S(1)}, f32[8,128]{1,0:T(8,128)S(1)}, u32[]{:S(2)}, u32[]{:S(2)}) collective-permute-start(f32[8,128]{1,0:T(8,128)S(1)} %add.15), channel_id=1, source_target_pairs={{0,128},{32,160},{64,192},{96,224},{128,0},{160,32},{192,64},{224,... | collective-permute-start | bytes 12296 | tf_op jit(solution)/shard_map/ppermute | solution.py:446
  79.6 0.0 collective-permute-start.6
  79.6 0.0 copy-done.7
  79.6 0.2 select_reduce_fusion
  79.8 1.6 %shard_map.100 = bf16[8,8,64,512]{3,2,1,0:T(8,128)(2,1)} custom-call(s32[2]{0:T(128)S(1)} %pad_add_fusion.sites_ref, bf16[8,2,64,512]{3,2,1,0:T(8,128)(2,1)S(1)} %get-tuple-element.27.done_ref, bf16[8,8,64,512]{3,2,1,0:T(8,128)(2,1)} %get-tuple-element.28._), custom_call_target="tpu_custom_call", output_to_operand_aliasing={{}: (2, {})} | custom-call | bytes 4194304 | tf_op jit(solution)/shard_map/pallas_call | solution.py:352
  81.5 0.0 collective-permute-done.4
  81.5 0.0 collective-permute-done.5
  81.5 2.9 %collective-permute-done.6 = f32[8,128]{1,0:T(8,128)S(1)} collective-permute-done((f32[8,128]{1,0:T(8,128)S(1)}, f32[8,128]{1,0:T(8,128)S(1)}, u32[]{:S(2)}, u32[]{:S(2)}) %collective-permute-start.6) | collective-permute-done | bytes 4128 | tf_op jit(solution)/shard_map/ppermute | solution.py:446
  84.4 0.1 add_reduce_fusion
  84.5 0.5 multiply_add_fusion
  (10 shorter events, 0.0 us)
Async XLA Ops:
  0.6 30.5 %copy-start = (f32[8,512,64]{1,2,0:T(8,128)S(1)}, f32[8,512,64]{1,2,0:T(8,128)}, u32[]{:S(2)}) copy-start(f32[8,512,64]{1,2,0:T(8,128)} %param.8) | copy-start | bytes 3145732
  0.6 30.5 %copy-start.1 = (s32[8,512,64]{1,2,0:T(8,128)S(1)}, s32[8,512,64]{1,2,0:T(8,128)}, u32[]{:S(2)}) copy-start(s32[8,512,64]{1,2,0:T(8,128)} %param.12) | copy-start | bytes 3145732
  0.7 30.5 %copy-start.2 = (f32[8,512,64]{1,2,0:T(8,128)S(1)}, f32[8,512,64]{1,2,0:T(8,128)}, u32[]{:S(2)}) copy-start(f32[8,512,64]{1,2,0:T(8,128)} %param.9) | copy-start | bytes 3145732
  0.7 30.4 %copy-start.5 = (f32[64]{0:T(128)S(1)}, f32[64]{0:T(128)}, u32[]{:S(2)}) copy-start(f32[64]{0:T(128)} %param.11) | copy-start | bytes 772
  2.4 15.5 %collective-permute-start.2 = (bf16[5,16,512]{2,1,0:T(8,128)(2,1)}, bf16[5,16,512]{2,1,0:T(8,128)(2,1)S(1)}, u32[]{:S(2)}, u32[]{:S(2)}) collective-permute-start(bf16[5,16,512]{2,1,0:T(8,128)(2,1)} %shard_map.95._), channel_id=1, source_target_pairs={{0,32},{2,34},{4,36},{6,38},{8,40},{10,42},{12,44},{14,46},{16,48}... | collective-permute-start | bytes 245768 | tf_op jit(solution)/shard_map/ppermute | solution.py:421
  12.8 39.6 %collective-permute-start = (bf16[8,64,512]{2,1,0:T(8,128)(2,1)}, bf16[8,64,512]{2,1,0:T(8,128)(2,1)}, u32[]{:S(2)}, u32[]{:S(2)}) collective-permute-start(bf16[8,64,512]{2,1,0:T(8,128)(2,1)} %get-tuple-element.17), channel_id=1, source_target_pairs={{0,32},{32,0},{64,96},{96,64},{128,160},{160,128},{192,224},{224,1... | collective-permute-start | bytes 1572872 | tf_op jit(solution)/shard_map/ppermute | solution.py:424
  13.5 38.9 %collective-permute-start.1 = (bf16[8,64,512]{2,1,0:T(8,128)(2,1)}, bf16[8,64,512]{2,1,0:T(8,128)(2,1)}, u32[]{:S(2)}, u32[]{:S(2)}) collective-permute-start(bf16[8,64,512]{2,1,0:T(8,128)(2,1)} %get-tuple-element.18), channel_id=1, source_target_pairs={{32,64},{64,32},{96,128},{128,96},{160,192},{192,160},{33,65},{65,... | collective-permute-start | bytes 1572872 | tf_op jit(solution)/shard_map/ppermute | solution.py:425
  31.1 1.2 %copy-start.3 = (bf16[1920,256]{1,0:T(8,128)(2,1)S(1)}, bf16[1920,256]{1,0:T(8,128)(2,1)}, u32[]{:S(2)}) copy-start(bf16[1920,256]{1,0:T(8,128)(2,1)} %get-tuple-element.22.bands_ref) | copy-start | bytes 2949124
  32.3 20.0 %copy-start.4 = (bf16[2,192,64]{2,1,0:T(8,128)(2,1)S(1)}, bf16[2,192,64]{2,1,0:T(8,128)(2,1)}, u32[]{:S(2)}) copy-start(bf16[2,192,64]{2,1,0:T(8,128)(2,1)} %get-tuple-element.25.weight_ref) | copy-start | bytes 147460
  48.7 30.9 %copy-start.6 = (f32[4096]{0:T(1024)S(1)}, f32[4096]{0:T(1024)}, u32[]{:S(2)}) copy-start(f32[4096]{0:T(1024)} %param.15) | copy-start | bytes 49156
  48.7 30.9 %copy-start.7 = (s32[8]{0:T(128)S(1)}, s32[8]{0:T(128)}, u32[]{:S(2)}) copy-start(s32[8]{0:T(128)} %param.14) | copy-start | bytes 100
  55.7 16.1 %collective-permute-start.3 = (f32[8,128]{1,0:T(8,128)S(1)}, f32[8,128]{1,0:T(8,128)S(1)}, u32[]{:S(2)}, u32[]{:S(2)}) collective-permute-start(f32[8,128]{1,0:T(8,128)S(1)} %get-tuple-element.29), channel_id=1, source_target_pairs={{0,32},{32,0},{64,96},{96,64},{128,160},{160,128},{192,224},{224,1... | collective-permute-start | bytes 12296 | tf_op jit(solution)/shard_map/ppermute | solution.py:444
  71.8 9.7 %collective-permute-start.4 = (f32[8,128]{1,0:T(8,128)S(1)}, f32[8,128]{1,0:T(8,128)S(1)}, u32[]{:S(2)}, u32[]{:S(2)}) collective-permute-start(f32[8,128]{1,0:T(8,128)S(1)} %add.15), channel_id=1, source_target_pairs={{0,64},{32,96},{64,0},{96,32},{128,192},{160,224},{192,128},{224,1... | collective-permute-start | bytes 12296 | tf_op jit(solution)/shard_map/ppermute | solution.py:446
  73.3 8.2 %collective-permute-start.5 = (f32[8,128]{1,0:T(8,128)S(1)}, f32[8,128]{1,0:T(8,128)S(1)}, u32[]{:S(2)}, u32[]{:S(2)}) collective-permute-start(f32[8,128]{1,0:T(8,128)S(1)} %add.15), channel_id=1, source_target_pairs={{0,128},{32,160},{64,192},{96,224},{128,0},{160,32},{192,64},{224,... | collective-permute-start | bytes 12296 | tf_op jit(solution)/shard_map/ppermute | solution.py:446
  79.6 4.8 %collective-permute-start.6 = (f32[8,128]{1,0:T(8,128)S(1)}, f32[8,128]{1,0:T(8,128)S(1)}, u32[]{:S(2)}, u32[]{:S(2)}) collective-permute-start(f32[8,128]{1,0:T(8,128)S(1)} %add.15), channel_id=1, source_target_pairs={{0,192},{32,224},{64,128},{96,160},{128,64},{160,96},{192,0},{224,... | collective-permute-start | bytes 12296 | tf_op jit(solution)/shard_map/ppermute | solution.py:446

commit v9 on v8

--- a/solution.py
+++ b/solution.py
@@ -11,8 +11,8 @@
 
 F32, BF16 = (jnp.float32, jnp.bfloat16)
 SHARE = 8
-MAIN_FLOPS = 20_000_000_000
-EDGE_FLOPS = 2_000_000_000
+MAIN_FLOPS = 2_000_000_000
+EDGE_FLOPS = 10_000_000_000
 MAIN_VMEM = 44 << 20
 EDGE_VMEM = 14 << 20
 UNITS = 5
@@ -269,57 +269,45 @@
 
 
 def edge_kernel(
-    sites_ref,
-    one_ref,
-    two_ref,
-    slope_ref,
-    edge_ref,
-    radius_one_ref,
-    radius_two_ref,
-    weight_ref,
-    total_ref,
-    done_ref,
-    sum_ref,
+    last, sites_ref, halo_ref, slope_ref, edge_ref, radius_ref, weight_ref, total_ref, done_ref, sum_ref
 ):
-    specs, channels, columns = one_ref.shape
+    specs, channels, columns = halo_ref.shape
     for s in range(specs):
+        pre = (halo_ref[s].astype(F32) * slope_ref[0].astype(F32)).astype(BF16)
+        value = edge_ref[s, 0] + spread_columns(mul(weight_ref[0], pre), columns)
+        done_ref[s] = value.astype(BF16)
+        terms = jnp.abs(value) * radius_ref[0]
+        terms = jnp.sum(terms.reshape(channels // 8, 8, columns), axis=0)
         total = total_ref[s]
-        for k, (halo_ref, radius_ref) in enumerate(
-            ((one_ref, radius_one_ref), (two_ref, radius_two_ref))
-        ):
-            e = sites_ref[k]
-            pre = (halo_ref[s].astype(F32) * slope_ref[e].astype(F32)).astype(BF16)
-            value = edge_ref[s, e] + spread_columns(mul(weight_ref[e], pre), columns)
-            done_ref[s, k] = value.astype(BF16)
-            terms = jnp.abs(value) * radius_ref[0]
-            terms = jnp.sum(terms.reshape(channels // 8, 8, columns), axis=0)
-            for m in range(columns // 128):
-                total = total - terms[:, m * 128 : (m + 1) * 128]
-        sum_ref[s : s + 1, :] = jnp.sum(total, axis=0, keepdims=True)
-
-
-def edge_pass(sites, one, two, slope, edge, radius, weight, total):
-    specs, channels, columns = one.shape
+        for m in range(columns // 128):
+            total = total - terms[:, m * 128 : (m + 1) * 128]
+        if last:
+            sum_ref[s : s + 1, :] = jnp.sum(total, axis=0, keepdims=True)
+        else:
+            sum_ref[s] = total
+
+
+def edge_pass(k, sites, halo, slope, edge, radius, weight, total):
+    specs, channels, columns = halo.shape
     rows = radius.shape[0]
     whole = lambda a: pl.BlockSpec(a.shape, lambda g, e, n=len(a.shape): (0,) * n)
+    last = k == 1
     out = (
-        jax.ShapeDtypeStruct((specs, 2, channels, columns), BF16),
-        jax.ShapeDtypeStruct((specs, 128), F32),
-    )
-    return pl.pallas_call(
-        edge_kernel,
+        jax.ShapeDtypeStruct((specs, channels, columns), BF16),
+        jax.ShapeDtypeStruct((specs, 128) if last else total.shape, F32),
+    )
+    return pl.pallas_call(
+        functools.partial(edge_kernel, last),
         out_shape=out,
         grid_spec=pltpu.PrefetchScalarGridSpec(
             num_scalar_prefetch=1,
             grid=(1,),
             in_specs=[
-                whole(one),
-                whole(two),
-                whole(slope),
-                whole(edge),
-                pl.BlockSpec((1, channels, columns), lambda g, e: (e[0] * (rows - 1), 0, 0)),
-                pl.BlockSpec((1, channels, columns), lambda g, e: (e[1] * (rows - 1), 0, 0)),
-                whole(weight),
+                whole(halo),
+                pl.BlockSpec((1, channels, columns), lambda g, e: (e[k], 0, 0)),
+                pl.BlockSpec((specs, 1, channels, columns), lambda g, e: (0, e[k], 0, 0)),
+                pl.BlockSpec((1, channels, columns), lambda g, e: (e[k] * (rows - 1), 0, 0)),
+                pl.BlockSpec((1, 3 * channels, channels), lambda g, e: (e[k], 0, 0)),
                 whole(total),
             ],
             out_specs=tuple(whole(a) for a in out),
@@ -328,18 +316,18 @@
         cost_estimate=pl.CostEstimate(
             flops=EDGE_FLOPS, bytes_accessed=1 << 20, transcendentals=0
         ),
-    )(sites, one, two, slope, edge, radius, radius, weight, total)
-
-
-def place_kernel(sites_ref, done_ref, _, out_ref, sems):
-    specs = done_ref.shape[0]
+    )(sites, halo, slope, edge, radius, weight, total)
+
+
+def place_kernel(sites_ref, one_ref, two_ref, _, out_ref, sems):
+    specs = one_ref.shape[0]
     rows = out_ref.shape[1]
     copies = [
         pltpu.make_async_copy(
-            done_ref.at[s, k], out_ref.at[s, sites_ref[k] * (rows - 1)], sems.at[s, k]
+            ref.at[s], out_ref.at[s, sites_ref[k] * (rows - 1)], sems.at[s, k]
         )
         for s in range(specs)
-        for k in range(2)
+        for k, ref in enumerate((one_ref, two_ref))
     ]
     for copy in copies:
         copy.start()
@@ -347,7 +335,7 @@
         copy.wait()
 
 
-def place_pass(sites, done, out):
+def place_pass(sites, one, two, out):
     anywhere = pl.BlockSpec(memory_space=pl.ANY)
     return pl.pallas_call(
         place_kernel,
@@ -355,14 +343,14 @@
         grid_spec=pltpu.PrefetchScalarGridSpec(
             num_scalar_prefetch=1,
             grid=(1,),
-            in_specs=[pl.BlockSpec(done.shape, lambda g, e: (0, 0, 0, 0)), anywhere],
+            in_specs=[pl.BlockSpec(one.shape, lambda g, e: (0, 0, 0))] * 2 + [anywhere],
             out_specs=anywhere,
-            scratch_shapes=[pltpu.SemaphoreType.DMA(done.shape[:2])],
-        ),
-        input_output_aliases={2: 0},
+            scratch_shapes=[pltpu.SemaphoreType.DMA((one.shape[0], 2))],
+        ),
+        input_output_aliases={3: 0},
         compiler_params=pltpu.CompilerParams(vmem_limit_bytes=16 << 20),
         cost_estimate=pl.CostEstimate(flops=0, bytes_accessed=4 << 20, transcendentals=0),
-    )(sites, done, out)
+    )(sites, one, two, out)
 
 
 def weight_kernel(weight_ref, bands_ref, ends_ref):
@@ -438,8 +426,9 @@
     )
     odd = lax.rem(lax.axis_index("rows"), 2)
     sites = jnp.stack([1 - odd, odd]).astype(jnp.int32)
-    done, partial = edge_pass(sites, one, two, slope, edge, radius, ends, total)
-    out = place_pass(sites, done, out)
+    one, total = edge_pass(0, sites, one, slope, edge, radius, ends, total)
+    two, partial = edge_pass(1, sites, two, slope, edge, radius, ends, total)
+    out = place_pass(sites, one, two, out)
 
     partial = partial + lax.ppermute(partial, "rows", [(i, i ^ 1) for i in range(count)])
     pairs = [partial] + [

time: 85.6 us -> 84.7 us (0.989)
  starting transfers between devices: 32.7 us -> 30.3 us
  Pallas kernels: 28.1 us -> 29.5 us
    ppermute x1, starting transfers between devices: 14.6 us -> 12.1 us  [per_device(): lax.ppermute(partial, 'rows', [(i, i ^ 1) for i in range(count)])]
    pallas_call x1 -> x2, Pallas kernels: 3.3 us -> 4.75 us  [edge_pass(): pl.pallas_call(functools.partial(edge_kernel, last), out_shape=out, grid_...]
  transfers between devices with their start and end apart: 7 -> 7, of which waited for: 3 -> 3; matrix products, arithmetic and copies ran while one was open for 0% -> 0% of each run, Pallas kernels for 27% -> 30%
where the time goes in v9:
time: 84.7 us; the launch traced here: 84.2 us
  starting transfers between devices  30.3 us (36%)
  Pallas kernels  29.5 us (35%)
  blocking collectives  13.2 us (16%)
  waiting for transfers between devices  8.21 us (10%)
  local copies, waits for them, and re-layouts  1.23 us (1%)
  other arithmetic  0.93 us (1%)
    pallas_call x1, Pallas kernels, main_pass(): pl.pallas_call(main_kernel, grid=(specs,), out_shape=(jax.ShapeDtypeStruc...  16.4 us
    all_gather x1, blocking collectives, per_device(): lax.all_gather(box, 'specs', axis_index_groups=[[(k * lanes + z) * 2 + e...  13.2 us
    ppermute x1, starting transfers between devices, per_device(): lax.ppermute(partial, 'rows', [(i, i ^ 1) for i in range(count)])  12.1 us
    ppermute x1, starting transfers between devices, per_device(): box = lax.ppermute(mine, ('rows', 'specs'), moves)  8.2 us
    ppermute x3, starting transfers between devices, per_device(): lax.ppermute(partial, 'rows', [(i, i ^ step) for i in range(count)])  7.84 us
    pallas_call x2, Pallas kernels, edge_pass(): pl.pallas_call(functools.partial(edge_kernel, last), out_shape=out, grid_...  4.75 us
    ppermute x1, waiting for transfers between devices, per_device(): lax.ppermute(one, 'rows', [m for p in pairs[::2] for m in (p, p[::-1])])  3.68 us
    ppermute x3, waiting for transfers between devices, per_device(): lax.ppermute(partial, 'rows', [(i, i ^ step) for i in range(count)])  2.94 us
  transfers between devices with their start and end apart: 7, of which 3 were waited for; matrix products, arithmetic and copies ran while one was open for 0% of the time, Pallas kernels for 30%

profile of v9, /device:TPU:56, one launch (start us, length us, event | category | flops | bytes accessed | tf_op | source)
XLA Modules:
  0.0 84.2 jit_solution(17130031825972105960)
XLA Ops:
  0.7 1.7 %shard_map.95._ = bf16[5,16,512]{2,1,0:T(8,128)(2,1)} custom-call(f32[8,64,512]{2,1,0:T(8,128)} %bitcast.9, f32[8,64,512]{2,1,0:T(8,128)} %bitcast.13, s32[8,64,512]{2,1,0:T(8,128)} %bitcast.11), custom_call_target="tpu_custom_call" | custom-call | bytes 1048576 | tf_op jit(solution)/shard_map/pallas_call | solution.py:67
  2.4 8.2 %collective-permute-start.1 = (bf16[5,16,512]{2,1,0:T(8,128)(2,1)}, bf16[5,16,512]{2,1,0:T(8,128)(2,1)S(1)}, u32[]{:S(2)}, u32[]{:S(2)}) collective-permute-start(bf16[5,16,512]{2,1,0:T(8,128)(2,1)} %shard_map.95._), channel_id=1, source_target_pairs={{0,32},{2,34},{4,36},{6,38},{8,40},{10,42},{12,44},{14,46},{16,48}... | collective-permute-start | bytes 245768 | tf_op jit(solution)/shard_map/ppermute | solution.py:409
  10.6 2.2 %shard_map.96 = (bf16[8,64,512]{2,1,0:T(8,128)(2,1)}, bf16[8,64,512]{2,1,0:T(8,128)(2,1)}) custom-call(bf16[8,8,64,512]{3,2,1,0:T(8,128)(2,1)} %bitcast.19, bf16[5,16,512]{2,1,0:T(8,128)(2,1)} %shard_map.95._), custom_call_target="tpu_custom_call" | custom-call | bytes 4194304 | tf_op jit(solution)/shard_map/pallas_call | solution.py:111
  12.8 0.7 collective-permute-start
  13.4 1.5 %collective-permute-start.2 = (bf16[8,64,512]{2,1,0:T(8,128)(2,1)}, bf16[8,64,512]{2,1,0:T(8,128)(2,1)}, u32[]{:S(2)}, u32[]{:S(2)}) collective-permute-start(bf16[8,64,512]{2,1,0:T(8,128)(2,1)} %get-tuple-element.29), channel_id=1, source_target_pairs={{32,64},{64,32},{96,128},{128,96},{160,192},{192,160},{33,65},{65,... | collective-permute-start | bytes 1572872 | tf_op jit(solution)/shard_map/ppermute | solution.py:413
  14.9 0.1 pad_add_fusion.sites_ref
  15.0 2.9 %shard_map.97 = (bf16[1920,256]{1,0:T(8,128)(2,1)}, bf16[2,192,64]{2,1,0:T(8,128)(2,1)}) custom-call(f32[3,3,64,64]{3,2,1,0:T(8,128)} %weight_ref.1), custom_call_target="tpu_custom_call" | custom-call | tf_op jit(solution)/shard_map/pallas_call | solution.py:383
  17.9 0.0 collective-permute-done.1
  17.9 13.2 %all-gather = bf16[40,16,512]{2,1,0:T(8,128)(2,1)S(1)} all-gather(bf16[5,16,512]{2,1,0:T(8,128)(2,1)S(1)} %collective-permute-done.1), channel_id=2, replica_groups={{0,1,8,9,16,17,24,25},{2,3,10,11,18,19,26,27},{4,5,12,13,20,21,28,29},{..., dimensions={0}, use_global_device_ids=true | all-gather | bytes 737280 | tf_op jit(solution)/shard_map/all_gather | solution.py:414
  31.1 0.0 copy-done
  31.1 0.0 copy-start.3
  31.1 1.2 %copy-done.3 = bf16[1920,256]{1,0:T(8,128)(2,1)S(1)} copy-done((bf16[1920,256]{1,0:T(8,128)(2,1)S(1)}, bf16[1920,256]{1,0:T(8,128)(2,1)}, u32[]{:S(2)}) %copy-start.3) | copy-done | bytes 983064
  32.3 16.4 %shard_map.98 = (bf16[8,8,64,512]{3,2,1,0:T(8,128)(2,1)}, f32[8,2,64,512]{3,2,1,0:T(8,128)S(1)}, bf16[2,64,512]{2,1,0:T(8,128)(2,1)S(1)}, f32[8,8,128]{2,1,0:T(8,128)S(1)}) custom-call(bf16[8,5,16,512]{3,2,1,0:T(8,128)(2,1)S(1)} %bitcast.17, f32[8,64,512]{2,1,0:T(8,128)S(1)} %bitcast.10, f32[8,64,512]{2,1,0:T(8,128)S(1)} %bitcast.14, ...), custom_call_target="tpu_custom_call" | custom-call | flops 2000000000 | bytes 16777216 | tf_op jit(solution)/shard_map/pallas_call | solution.py:237
  48.7 3.7 %collective-permute-done.halo_ref = bf16[8,64,512]{2,1,0:T(8,128)(2,1)} collective-permute-done((bf16[8,64,512]{2,1,0:T(8,128)(2,1)}, bf16[8,64,512]{2,1,0:T(8,128)(2,1)}, u32[]{:S(2)}, u32[]{:S(2)}) %collective-permute-start) | collective-permute-done | bytes 524320 | tf_op jit(solution)/shard_map/ppermute | solution.py:412
  52.4 2.4 %shard_map.99 = (bf16[8,64,512]{2,1,0:T(8,128)(2,1)S(1)}, f32[8,8,128]{2,1,0:T(8,128)S(1)}) custom-call(s32[2]{0:T(128)S(1)} %pad_add_fusion.sites_ref, bf16[8,64,512]{2,1,0:T(8,128)(2,1)} %collective-permute-done.halo_ref, bf16[2,64,512]{2,1,0:T(8,128)(2,1)S(1)} %get-tuple-element.24.slope_ref, f32[8,2,64,512]{3,2,1,0:T(8,128)S(1)} %get-tuple-element.25.edge_ref, ...), custom_call_target="tpu_custom_call" | custom-call | flops 10000000000 | bytes 1048576 | tf_op jit(solution)/shard_map/pallas_call | solution.py:299
  54.7 0.0 collective-permute-done.2.halo_ref
  54.7 0.0 copy-start.6
  54.7 0.0 copy-start.7
  54.8 2.4 %shard_map.100 = (bf16[8,64,512]{2,1,0:T(8,128)(2,1)S(1)}, f32[8,128]{1,0:T(8,128)S(1)}) custom-call(s32[2]{0:T(128)S(1)} %pad_add_fusion.sites_ref, bf16[8,64,512]{2,1,0:T(8,128)(2,1)} %collective-permute-done.2.halo_ref, bf16[2,64,512]{2,1,0:T(8,128)(2,1)S(1)} %get-tuple-element.24.slope_ref, f32[8,2,64,512]{3,2,1,0:T(8,128)S(1)} %get-tuple-element.25.edge_ref, ...), custom_call_target="tpu_custom_call" | custom-call | flops 10000000000 | bytes 1048576 | tf_op jit(solution)/shard_map/pallas_call | solution.py:299
  57.1 12.1 %collective-permute-start.3 = (f32[8,128]{1,0:T(8,128)S(1)}, f32[8,128]{1,0:T(8,128)S(1)}, u32[]{:S(2)}, u32[]{:S(2)}) collective-permute-start(f32[8,128]{1,0:T(8,128)S(1)} %get-tuple-element.33), channel_id=1, source_target_pairs={{0,32},{32,0},{64,96},{96,64},{128,160},{160,128},{192,224},{224,1... | collective-permute-start | bytes 12296 | tf_op jit(solution)/shard_map/ppermute | solution.py:433
  69.3 1.6 %collective-permute-done.3 = f32[8,128]{1,0:T(8,128)S(1)} collective-permute-done((f32[8,128]{1,0:T(8,128)S(1)}, f32[8,128]{1,0:T(8,128)S(1)}, u32[]{:S(2)}, u32[]{:S(2)}) %collective-permute-start.3) | collective-permute-done | bytes 4128 | tf_op jit(solution)/shard_map/ppermute | solution.py:433
  70.9 1.5 %collective-permute-start.4 = (f32[8,128]{1,0:T(8,128)S(1)}, f32[8,128]{1,0:T(8,128)S(1)}, u32[]{:S(2)}, u32[]{:S(2)}) collective-permute-start(f32[8,128]{1,0:T(8,128)S(1)} %add.15), channel_id=1, source_target_pairs={{0,64},{32,96},{64,0},{96,32},{128,192},{160,224},{192,128},{224,1... | collective-permute-start | bytes 12296 | tf_op jit(solution)/shard_map/ppermute | solution.py:435
  72.4 6.3 %collective-permute-start.5 = (f32[8,128]{1,0:T(8,128)S(1)}, f32[8,128]{1,0:T(8,128)S(1)}, u32[]{:S(2)}, u32[]{:S(2)}) collective-permute-start(f32[8,128]{1,0:T(8,128)S(1)} %add.15), channel_id=1, source_target_pairs={{0,128},{32,160},{64,192},{96,224},{128,0},{160,32},{192,64},{224,... | collective-permute-start | bytes 12296 | tf_op jit(solution)/shard_map/ppermute | solution.py:435
  78.7 0.0 collective-permute-start.6
  78.7 0.0 copy-done.6
  78.7 0.2 select_reduce_fusion
  78.9 1.6 %shard_map.101 = bf16[8,8,64,512]{3,2,1,0:T(8,128)(2,1)} custom-call(s32[2]{0:T(128)S(1)} %pad_add_fusion.sites_ref, bf16[8,64,512]{2,1,0:T(8,128)(2,1)S(1)} %get-tuple-element.28.one_ref, bf16[8,64,512]{2,1,0:T(8,128)(2,1)S(1)} %get-tuple-element.31.two_ref, bf16[8,8,64,512]{3,2,1,0:T(8,128)(2,1)} %get-tuple-element.32._), custom_call_target="tpu_custom_call", output_to_operand_aliasing={{}: (3, {})} | custom-call | bytes 4194304 | tf_op jit(solution)/shard_map/pallas_call | solution.py:340
  80.6 0.0 collective-permute-done.4
  80.6 0.0 collective-permute-done.5
  80.6 2.9 %collective-permute-done.6 = f32[8,128]{1,0:T(8,128)S(1)} collective-permute-done((f32[8,128]{1,0:T(8,128)S(1)}, f32[8,128]{1,0:T(8,128)S(1)}, u32[]{:S(2)}, u32[]{:S(2)}) %collective-permute-start.6) | collective-permute-done | bytes 4128 | tf_op jit(solution)/shard_map/ppermute | solution.py:435
  83.5 0.1 add_reduce_fusion
  83.7 0.5 multiply_add_fusion
  (11 shorter events, 0.0 us)
Async XLA Ops:
  0.6 30.5 %copy-start = (f32[8,512,64]{1,2,0:T(8,128)S(1)}, f32[8,512,64]{1,2,0:T(8,128)}, u32[]{:S(2)}) copy-start(f32[8,512,64]{1,2,0:T(8,128)} %param.8) | copy-start | bytes 3145732
  0.6 30.5 %copy-start.1 = (s32[8,512,64]{1,2,0:T(8,128)S(1)}, s32[8,512,64]{1,2,0:T(8,128)}, u32[]{:S(2)}) copy-start(s32[8,512,64]{1,2,0:T(8,128)} %param.12) | copy-start | bytes 3145732
  0.7 30.5 %copy-start.2 = (f32[8,512,64]{1,2,0:T(8,128)S(1)}, f32[8,512,64]{1,2,0:T(8,128)}, u32[]{:S(2)}) copy-start(f32[8,512,64]{1,2,0:T(8,128)} %param.9) | copy-start | bytes 3145732
  0.7 30.4 %copy-start.4 = (f32[64]{0:T(128)S(1)}, f32[64]{0:T(128)}, u32[]{:S(2)}) copy-start(f32[64]{0:T(128)} %param.11) | copy-start | bytes 772
  2.4 15.5 %collective-permute-start.1 = (bf16[5,16,512]{2,1,0:T(8,128)(2,1)}, bf16[5,16,512]{2,1,0:T(8,128)(2,1)S(1)}, u32[]{:S(2)}, u32[]{:S(2)}) collective-permute-start(bf16[5,16,512]{2,1,0:T(8,128)(2,1)} %shard_map.95._), channel_id=1, source_target_pairs={{0,32},{2,34},{4,36},{6,38},{8,40},{10,42},{12,44},{14,46},{16,48}... | collective-permute-start | bytes 245768 | tf_op jit(solution)/shard_map/ppermute | solution.py:409
  12.8 39.6 %collective-permute-start = (bf16[8,64,512]{2,1,0:T(8,128)(2,1)}, bf16[8,64,512]{2,1,0:T(8,128)(2,1)}, u32[]{:S(2)}, u32[]{:S(2)}) collective-permute-start(bf16[8,64,512]{2,1,0:T(8,128)(2,1)} %get-tuple-element.19), channel_id=1, source_target_pairs={{0,32},{32,0},{64,96},{96,64},{128,160},{160,128},{192,224},{224,1... | collective-permute-start | bytes 1572872 | tf_op jit(solution)/shard_map/ppermute | solution.py:412
  13.4 41.3 %collective-permute-start.2 = (bf16[8,64,512]{2,1,0:T(8,128)(2,1)}, bf16[8,64,512]{2,1,0:T(8,128)(2,1)}, u32[]{:S(2)}, u32[]{:S(2)}) collective-permute-start(bf16[8,64,512]{2,1,0:T(8,128)(2,1)} %get-tuple-element.29), channel_id=1, source_target_pairs={{32,64},{64,32},{96,128},{128,96},{160,192},{192,160},{33,65},{65,... | collective-permute-start | bytes 1572872 | tf_op jit(solution)/shard_map/ppermute | solution.py:413
  31.1 1.2 %copy-start.3 = (bf16[1920,256]{1,0:T(8,128)(2,1)S(1)}, bf16[1920,256]{1,0:T(8,128)(2,1)}, u32[]{:S(2)}) copy-start(bf16[1920,256]{1,0:T(8,128)(2,1)} %get-tuple-element.23.bands_ref) | copy-start | bytes 2949124
  32.3 20.0 %copy-start.5 = (bf16[2,192,64]{2,1,0:T(8,128)(2,1)S(1)}, bf16[2,192,64]{2,1,0:T(8,128)(2,1)}, u32[]{:S(2)}) copy-start(bf16[2,192,64]{2,1,0:T(8,128)(2,1)} %get-tuple-element.26.weight_ref) | copy-start | bytes 147460
  54.7 24.0 %copy-start.6 = (f32[4096]{0:T(1024)S(1)}, f32[4096]{0:T(1024)}, u32[]{:S(2)}) copy-start(f32[4096]{0:T(1024)} %param.15) | copy-start | bytes 49156
  54.7 24.0 %copy-start.7 = (s32[8]{0:T(128)S(1)}, s32[8]{0:T(128)}, u32[]{:S(2)}) copy-start(s32[8]{0:T(128)} %param.14) | copy-start | bytes 100
  57.1 13.7 %collective-permute-start.3 = (f32[8,128]{1,0:T(8,128)S(1)}, f32[8,128]{1,0:T(8,128)S(1)}, u32[]{:S(2)}, u32[]{:S(2)}) collective-permute-start(f32[8,128]{1,0:T(8,128)S(1)} %get-tuple-element.33), channel_id=1, source_target_pairs={{0,32},{32,0},{64,96},{96,64},{128,160},{160,128},{192,224},{224,1... | collective-permute-start | bytes 12296 | tf_op jit(solution)/shard_map/ppermute | solution.py:433
  70.9 9.7 %collective-permute-start.4 = (f32[8,128]{1,0:T(8,128)S(1)}, f32[8,128]{1,0:T(8,128)S(1)}, u32[]{:S(2)}, u32[]{:S(2)}) collective-permute-start(f32[8,128]{1,0:T(8,128)S(1)} %add.15), channel_id=1, source_target_pairs={{0,64},{32,96},{64,0},{96,32},{128,192},{160,224},{192,128},{224,1... | collective-permute-start | bytes 12296 | tf_op jit(solution)/shard_map/ppermute | solution.py:435
  72.4 8.2 %collective-permute-start.5 = (f32[8,128]{1,0:T(8,128)S(1)}, f32[8,128]{1,0:T(8,128)S(1)}, u32[]{:S(2)}, u32[]{:S(2)}) collective-permute-start(f32[8,128]{1,0:T(8,128)S(1)} %add.15), channel_id=1, source_target_pairs={{0,128},{32,160},{64,192},{96,224},{128,0},{160,32},{192,64},{224,... | collective-permute-start | bytes 12296 | tf_op jit(solution)/shard_map/ppermute | solution.py:435
  78.7 4.8 %collective-permute-start.6 = (f32[8,128]{1,0:T(8,128)S(1)}, f32[8,128]{1,0:T(8,128)S(1)}, u32[]{:S(2)}, u32[]{:S(2)}) collective-permute-start(f32[8,128]{1,0:T(8,128)S(1)} %add.15), channel_id=1, source_target_pairs={{0,192},{32,224},{64,128},{96,160},{128,64},{160,96},{192,0},{224,... | collective-permute-start | bytes 12296 | tf_op jit(solution)/shard_map/ppermute | solution.py:435
